TPU v7x, 32 devices: a whole 2x2x4 slice. The times are simulated.
32 devices in a mesh: group: 4 (over z), replica: 8 (over y, x, core).
Axes of the slice: x: 2, y: 2, z: 4, core: 2. Of those that a mesh axis runs over, the one named last changes fastest.
Arguments:
- layer_input: bfloat16 [8, 1024, 2560], P('replica', 'group')
- positions: int32 [8, 1024], P('replica', 'group'), may hold values from 0 to 543, as said below
- piece_starts: int32 [8, 2], P('replica'), may hold values from 0 to 768, as said below
- gain_attn: bfloat16 [2560], P('group'), may hold values from 0.5 to 1.5
- w_query: bfloat16 [2560, 2560], P('group'), may hold values from -0.125 to 0.125
- w_key: bfloat16 [2560, 640], P('group'), may hold values from -0.125 to 0.125
- w_value: bfloat16 [2560, 640], P('group'), may hold values from -0.125 to 0.125
- w_out: bfloat16 [2560, 2560], P('group'), may hold values from -2 to 2
- gain_mlp: bfloat16 [2560], P('group'), may hold values from 0.5 to 1.5
- w_gate: bfloat16 [2560, 7168], P('group'), may hold values from -0.125 to 0.125
- w_up: bfloat16 [2560, 7168], P('group'), may hold values from -0.125 to 0.125
- w_down: bfloat16 [2560, 7168], P('group'), may hold values from -0.0625 to 0.0625
- out_grad: bfloat16 [8, 1024, 2560], P('replica', 'group'), may hold values from -6 to 6
Outputs:
- layer_out: bfloat16 [8, 1024, 2560], P('replica', 'group')
- input_grad: float32 [8, 1024, 2560], P('replica', 'group')
- grad_norm_attn: float32 [2560], P(('group', 'replica'))
- grad_query: float32 [2560, 2560], P(('group', 'replica'))
- grad_key: float32 [2560, 640], P(('group', 'replica'))
- grad_value: float32 [2560, 640], P(('group', 'replica'))
- grad_out: float32 [2560, 2560], P(('group', 'replica'))
- grad_norm_mlp: float32 [2560], P(('group', 'replica'))
- grad_gate: float32 [2560, 7168], P(('group', 'replica'))
- grad_up: float32 [2560, 7168], P(('group', 'replica'))
- grad_down: float32 [2560, 7168], P(('group', 'replica'))
- stream_rms: float32 [8, 3], P('replica')
Inputs may be any that keep to these rules, and one draw needn't show every extreme that they name: `piece_starts`: each sequence holds two picture pieces of 256 tokens that start at multiples of 128, the second starting 256 or more tokens after the first, both ending inside the sequence. `positions`: outside picture pieces a token's position is one more than the previous token's; the j-th token of a piece whose first token has position p gets p + j // 16, and the token after the piece gets p + 16; a sequence's first token has position 0.
All inputs are finite; a program needn't handle non-finite values.
Results may differ from a plain program's by a relative error of at most 0.018.
Values may be sent and summed in bfloat16 or wider, within the bound.
No kernel may reach another device: no remote copies, remote signals or barrier semaphores. Data moves between devices by JAX's collectives and lax.ppermute only.
A program may use at most 384 MiB of HBM per device.

v0:
```python
import jax
import jax.numpy as jnp
from jax import lax
from jax.sharding import PartitionSpec as P

HEADS = 32
KV_HEADS = 8
HEAD_DIM = 80
PIECE = 256


epsilon = 1e-05
rope_base = 1000000.0


def rope_tables(places):
    halves = HEAD_DIM // 2
    frequency = rope_base ** (-(jnp.arange(halves, dtype=jnp.float32) * 2.0 / HEAD_DIM))
    angles = places.astype(jnp.float32)[..., None] * frequency
    angles = jnp.concatenate([angles, angles], axis=-1)
    return (jnp.cos(angles), jnp.sin(angles))


def rotate(values, cosine, sine):
    halves = HEAD_DIM // 2
    turned = jnp.concatenate([-values[..., halves:], values[..., :halves]], axis=-1)
    return values * cosine[:, :, None, :] + turned * sine[:, :, None, :]


def unrotate(grads, cosine, sine):
    halves = HEAD_DIM // 2
    shifted = grads * sine[:, :, None, :]
    turned = jnp.concatenate([shifted[..., halves:], -shifted[..., :halves]], axis=-1)
    return grads * cosine[:, :, None, :] + turned


def times_t(left, right):
    return lax.dot_general(
        left, right, (((1,), (1,)), ((), ())), preferred_element_type=jnp.float32
    )


def inner_t(left, right):
    return lax.dot_general(
        left, right, (((0,), (0,)), ((), ())), preferred_element_type=jnp.float32
    )


def inverse_rms(values):
    return lax.rsqrt(jnp.mean(values * values, axis=-1, keepdims=True) + epsilon)


def norm_back(grad_normed, source, inverse, gain_full):
    weighted = grad_normed * gain_full
    average = jnp.mean(weighted * source, axis=-1, keepdims=True)
    return inverse * weighted - source * (inverse * inverse * inverse) * average


def piece_index(starts, places):
    labels = jnp.zeros(places.shape, jnp.int32)
    for which in range(2):
        inside = (places >= starts[which]) & (places < starts[which] + PIECE)
        labels = jnp.where(inside, which + 1, labels)
    return labels


def shards(
    layer_input,
    positions,
    piece_starts,
    gain_attn,
    w_query,
    w_key,
    w_value,
    w_out,
    gain_mlp,
    w_gate,
    w_up,
    w_down,
    out_grad,
):
    sequences, block_size, model_width = layer_input.shape
    token_rows = sequences * block_size
    kv_width = KV_HEADS * HEAD_DIM
    repeats = HEADS // KV_HEADS
    scaling = HEAD_DIM ** (-0.5)
    full_len = block_size * lax.axis_size("group")
    source = layer_input.astype(jnp.float32).reshape(token_rows, model_width)
    inverse_one = inverse_rms(source)
    unit_one = source * inverse_one
    gain_piece = lax.all_gather(gain_attn, "group", axis=0, tiled=True)
    query_piece = lax.all_gather(w_query, "group", axis=0, tiled=True)
    key_piece = lax.all_gather(w_key, "group", axis=0, tiled=True)
    value_piece = lax.all_gather(w_value, "group", axis=0, tiled=True)
    out_piece = lax.all_gather(w_out, "group", axis=0, tiled=True)
    scaled = unit_one * gain_piece.astype(jnp.float32)
    scaled = scaled.astype(jnp.bfloat16)
    query = jnp.dot(scaled, query_piece, preferred_element_type=jnp.float32)
    keyed = jnp.dot(scaled, key_piece, preferred_element_type=jnp.float32)
    valued = jnp.dot(scaled, value_piece, preferred_element_type=jnp.float32)
    normed = scaled
    gains = gain_piece
    out_full = out_piece
    query_lin, key_lin, value_lin, normed_one, gain_one_low, out_full = (
        query,
        keyed,
        valued,
        normed,
        gains,
        out_full,
    )
    gain_one = gain_one_low.astype(jnp.float32)
    cosine, sine = rope_tables(positions)
    query_rot = rotate(
        query_lin.reshape(sequences, block_size, HEADS, HEAD_DIM), cosine, sine
    ).astype(jnp.bfloat16)
    key_rot = rotate(
        key_lin.reshape(sequences, block_size, KV_HEADS, HEAD_DIM), cosine, sine
    ).astype(jnp.bfloat16)
    key_rot = key_rot.reshape(sequences, block_size, kv_width)
    value_low = value_lin.astype(jnp.bfloat16).reshape(sequences, block_size, kv_width)
    key_all, value_all = (
        lax.all_gather(key_rot, "group", axis=1, tiled=True),
        lax.all_gather(value_low, "group", axis=1, tiled=True),
    )
    query_places = lax.axis_index("group") * block_size + jnp.arange(block_size, dtype=jnp.int32)
    key_places = jnp.arange(full_len, dtype=jnp.int32)

    def allowed_for(starts):
        query_labels = piece_index(starts, query_places)
        key_labels = piece_index(starts, key_places)
        causal = key_places[None, :] <= query_places[:, None]
        same_piece = (query_labels[:, None] == key_labels[None, :]) & (query_labels[:, None] > 0)
        return causal | same_piece

    def scores_of(query_seq, key_seq, starts):
        grouped = query_seq.reshape(block_size, KV_HEADS, repeats, HEAD_DIM)
        keys_grouped = key_seq.reshape(full_len, KV_HEADS, HEAD_DIM)
        raw = (
            jnp.einsum("qkrd,skd->krqs", grouped, keys_grouped, preferred_element_type=jnp.float32)
            * scaling
        )
        return jnp.where(allowed_for(starts)[None, None], raw, -1e30)

    def attend_one(packed):
        query_seq, key_seq, value_seq, starts = packed
        masked = scores_of(query_seq, key_seq, starts)
        highest_score = jnp.max(masked, axis=-1, keepdims=True)
        raised = jnp.exp(masked - highest_score)
        summed = jnp.sum(raised, axis=-1, keepdims=True)
        chances_low = (raised / summed).astype(jnp.bfloat16)
        values_grouped = value_seq.reshape(full_len, KV_HEADS, HEAD_DIM)
        mixed = jnp.einsum(
            "krqs,skd->qkrd", chances_low, values_grouped, preferred_element_type=jnp.float32
        )
        return (mixed.reshape(block_size, model_width), highest_score + jnp.log(summed))

    mixed_all, log_totals = lax.map(attend_one, (query_rot, key_all, value_all, piece_starts))
    mixed_low = mixed_all.reshape(token_rows, model_width).astype(jnp.bfloat16)
    middle = source + times_t(mixed_low, out_full)
    inverse_two = inverse_rms(middle)
    unit_two = middle * inverse_two
    gain_piece = lax.all_gather(gain_mlp, "group", axis=0, tiled=True)
    gate_piece = lax.all_gather(w_gate, "group", axis=0, tiled=True)
    up_piece = lax.all_gather(w_up, "group", axis=0, tiled=True)
    down_piece = lax.all_gather(w_down, "group", axis=0, tiled=True)
    scaled = unit_two * gain_piece.astype(jnp.float32)
    scaled = scaled.astype(jnp.bfloat16)
    gated = jnp.dot(scaled, gate_piece, preferred_element_type=jnp.float32)
    lifted = jnp.dot(scaled, up_piece, preferred_element_type=jnp.float32)
    normed = scaled
    gains = gain_piece
    down_full = down_piece
    gated, lifted, normed_two, gain_two_low, down_full = (gated, lifted, normed, gains, down_full)
    gain_two = gain_two_low.astype(jnp.float32)
    activated = jax.nn.silu(gated)
    hidden = (activated * lifted).astype(jnp.bfloat16)
    output_full = middle + times_t(hidden, down_full)
    grad_low = out_grad.reshape(token_rows, model_width)
    grad_top = grad_low.astype(jnp.float32)
    grad_hidden = jnp.dot(grad_low, down_full, preferred_element_type=jnp.float32)
    sigmoid_gate = jax.nn.sigmoid(gated)
    grad_gate_low = (
        grad_hidden * lifted * (sigmoid_gate + gated * sigmoid_gate * (1.0 - sigmoid_gate))
    ).astype(jnp.bfloat16)
    grad_lift_low = (grad_hidden * activated).astype(jnp.bfloat16)
    gate_piece = lax.all_gather(w_gate, "group", axis=0, tiled=True)
    up_piece = lax.all_gather(w_up, "group", axis=0, tiled=True)
    added = times_t(grad_gate_low, gate_piece) + times_t(grad_lift_low, up_piece)
    grad_normed_two = added
    grad_gain_two = jnp.sum(grad_normed_two * unit_two, axis=0)
    grad_middle = grad_top + norm_back(grad_normed_two, middle, inverse_two, gain_two)
    grad_middle_low = grad_middle.astype(jnp.bfloat16)
    grad_mixed_low = jnp.dot(grad_middle_low, out_full, preferred_element_type=jnp.float32).astype(
        jnp.bfloat16
    )

    def attend_back(packed):
        query_seq, key_seq, value_seq, starts, log_total, grad_seq = packed
        masked = scores_of(query_seq, key_seq, starts)
        chances = jnp.exp(masked - log_total)
        grad_grouped = grad_seq.reshape(block_size, KV_HEADS, repeats, HEAD_DIM)
        values_grouped = value_seq.reshape(full_len, KV_HEADS, HEAD_DIM)
        keys_grouped = key_seq.reshape(full_len, KV_HEADS, HEAD_DIM)
        query_grouped = query_seq.reshape(block_size, KV_HEADS, repeats, HEAD_DIM)
        grad_value_seq = jnp.einsum(
            "krqs,qkrd->skd",
            chances.astype(jnp.bfloat16),
            grad_grouped,
            preferred_element_type=jnp.float32,
        )
        grad_chance = jnp.einsum(
            "qkrd,skd->krqs", grad_grouped, values_grouped, preferred_element_type=jnp.float32
        )
        grad_score = chances * (
            grad_chance - jnp.sum(chances * grad_chance, axis=-1, keepdims=True)
        )
        grad_score = grad_score.astype(jnp.bfloat16)
        grad_query_seq = (
            jnp.einsum(
                "krqs,skd->qkrd", grad_score, keys_grouped, preferred_element_type=jnp.float32
            )
            * scaling
        )
        grad_key_seq = (
            jnp.einsum(
                "krqs,qkrd->skd", grad_score, query_grouped, preferred_element_type=jnp.float32
            )
            * scaling
        )
        return (
            grad_query_seq.reshape(block_size, HEADS, HEAD_DIM),
            grad_key_seq.reshape(full_len, kv_width),
            grad_value_seq.reshape(full_len, kv_width),
        )

    grad_query_rot, grad_key_full, grad_value_full = lax.map(
        attend_back,
        (
            query_rot,
            key_all,
            value_all,
            piece_starts,
            log_totals,
            grad_mixed_low.reshape(sequences, block_size, model_width),
        ),
    )
    grad_key_rot, grad_value_sum = (
        lax.psum_scatter(grad_key_full, "group", scatter_dimension=1, tiled=True),
        lax.psum_scatter(grad_value_full, "group", scatter_dimension=1, tiled=True),
    )
    grad_query_low = (
        unrotate(grad_query_rot, cosine, sine).astype(jnp.bfloat16).reshape(token_rows, model_width)
    )
    grad_key_low = (
        unrotate(grad_key_rot.reshape(sequences, block_size, KV_HEADS, HEAD_DIM), cosine, sine)
        .astype(jnp.bfloat16)
        .reshape(token_rows, kv_width)
    )
    grad_value_low = grad_value_sum.astype(jnp.bfloat16).reshape(token_rows, kv_width)
    query_piece = lax.all_gather(w_query, "group", axis=0, tiled=True)
    key_piece = lax.all_gather(w_key, "group", axis=0, tiled=True)
    value_piece = lax.all_gather(w_value, "group", axis=0, tiled=True)
    added = (
        times_t(grad_query_low, query_piece)
        + times_t(grad_key_low, key_piece)
        + times_t(grad_value_low, value_piece)
    )
    grad_gain_one = jnp.sum(added * unit_one, axis=0)
    input_grad = grad_middle + norm_back(added, source, inverse_one, gain_one)
    normed_own, middle_own, normed_mlp_own, top_own = (
        lax.all_to_all(normed_one, "group", split_axis=1, concat_axis=0, tiled=True),
        lax.all_to_all(grad_middle_low, "group", split_axis=1, concat_axis=0, tiled=True),
        lax.all_to_all(normed_two, "group", split_axis=1, concat_axis=0, tiled=True),
        lax.all_to_all(grad_low, "group", split_axis=1, concat_axis=0, tiled=True),
    )
    query_rows, key_rows, value_rows, mixed_rows = (
        lax.all_gather(grad_query_low, "group", axis=0, tiled=True),
        lax.all_gather(grad_key_low, "group", axis=0, tiled=True),
        lax.all_gather(grad_value_low, "group", axis=0, tiled=True),
        lax.all_gather(mixed_low, "group", axis=0, tiled=True),
    )
    gate_rows, lift_rows, hidden_rows = (
        lax.all_gather(grad_gate_low, "group", axis=0, tiled=True),
        lax.all_gather(grad_lift_low, "group", axis=0, tiled=True),
        lax.all_gather(hidden, "group", axis=0, tiled=True),
    )
    partial_sums = (
        inner_t(normed_own, query_rows),
        inner_t(normed_own, key_rows),
        inner_t(normed_own, value_rows),
        inner_t(middle_own, mixed_rows),
        inner_t(normed_mlp_own, gate_rows),
        inner_t(normed_mlp_own, lift_rows),
        inner_t(top_own, hidden_rows),
    )
    grad_query, grad_key, grad_value, grad_out, grad_gate, grad_up, grad_down = (
        lax.psum_scatter(
            partial_sums[0].astype(jnp.bfloat16), "replica", scatter_dimension=0, tiled=True
        ).astype(jnp.float32),
        lax.psum_scatter(
            partial_sums[1].astype(jnp.bfloat16), "replica", scatter_dimension=0, tiled=True
        ).astype(jnp.float32),
        lax.psum_scatter(
            partial_sums[2].astype(jnp.bfloat16), "replica", scatter_dimension=0, tiled=True
        ).astype(jnp.float32),
        lax.psum_scatter(
            partial_sums[3].astype(jnp.bfloat16), "replica", scatter_dimension=0, tiled=True
        ).astype(jnp.float32),
        lax.psum_scatter(
            partial_sums[4].astype(jnp.bfloat16), "replica", scatter_dimension=0, tiled=True
        ).astype(jnp.float32),
        lax.psum_scatter(
            partial_sums[5].astype(jnp.bfloat16), "replica", scatter_dimension=0, tiled=True
        ).astype(jnp.float32),
        lax.psum_scatter(
            partial_sums[6].astype(jnp.bfloat16), "replica", scatter_dimension=0, tiled=True
        ).astype(jnp.float32),
    )
    gain_owned = lax.psum_scatter(
        jnp.stack([grad_gain_one, grad_gain_two]),
        ("group", "replica"),
        scatter_dimension=1,
        tiled=True,
    )
    squares = jnp.stack(
        [
            jnp.sum((source * source).reshape(sequences, -1), axis=1),
            jnp.sum((middle * middle).reshape(sequences, -1), axis=1),
            jnp.sum((output_full * output_full).reshape(sequences, -1), axis=1),
        ],
        axis=1,
    )
    square_totals = lax.psum(squares, "group")
    stream_rms = jnp.sqrt(square_totals / (full_len * model_width))
    layer_out = output_full.astype(jnp.bfloat16).reshape(sequences, block_size, model_width)
    input_grad = input_grad.reshape(sequences, block_size, model_width)
    return (
        layer_out,
        input_grad,
        gain_owned[0],
        grad_query,
        grad_key,
        grad_value,
        grad_out,
        gain_owned[1],
        grad_gate,
        grad_up,
        grad_down,
        stream_rms,
    )


def solution(mesh):
    placed = (
        P("replica", "group", None),
        P("replica", "group"),
        P("replica", None),
        P("group"),
        P("group", None),
        P("group", None),
        P("group", None),
        P("group", None),
        P("group"),
        P("group", None),
        P("group", None),
        P("group", None),
        P("replica", "group", None),
    )
    return jax.shard_map(
        shards,
        mesh=mesh,
        in_specs=placed,
        out_specs=(
            P("replica", "group", None),
            P("replica", "group", None),
            P(("group", "replica")),
            P(("group", "replica"), None),
            P(("group", "replica"), None),
            P(("group", "replica"), None),
            P(("group", "replica"), None),
            P(("group", "replica")),
            P(("group", "replica"), None),
            P(("group", "replica"), None),
            P(("group", "replica"), None),
            P("replica", None),
        ),
        check_vma=False,
    )
```

profile of v0, /device:TPU:0, one launch (start us, length us, event | category | flops | bytes accessed | tf_op | source)
XLA Modules:
  0.0 4407.6 jit_solution(10174914001787924033)
XLA Ops:
  9.4 14.6 all-gather.3
  27.3 50.7 %all-gather.24.cloned.1.call-done = bf16[2560,640]{1,0:T(8,128)(2,1)} async-done(((bf16[640,640]{1,0:T(8,128)(2,1)}), bf16[2560,640]{1,0:T(8,128)(2,1)}) %all-gather.24.cloned.1.call-update) | async-done | bytes 3276816 | tf_op jit(solution)/shard_map/all_gather | solution.py:93
  86.8 57.1 %all-gather.22.cloned.1.call-done = bf16[2560,640]{1,0:T(8,128)(2,1)} async-done(((bf16[640,640]{1,0:T(8,128)(2,1)}), bf16[2560,640]{1,0:T(8,128)(2,1)}) %all-gather.22.cloned.1.call-update) | async-done | bytes 3276816 | tf_op jit(solution)/shard_map/all_gather | solution.py:94
  153.2 13.4 all-gather.4
  179.2 32.1 all-gather.48.cloned.1.call-done
  213.7 224.8 %all-gather.26.cloned.1.call-done = bf16[2560,2560]{1,0:T(8,128)(2,1)} async-done(((bf16[640,2560]{1,0:T(8,128)(2,1)}), bf16[2560,2560]{1,0:T(8,128)(2,1)}) %all-gather.26.cloned.1.call-update) | async-done | bytes 13107216 | tf_op jit(solution)/shard_map/all_gather | solution.py:92
  438.5 8.5 fusion.39
  447.7 14.4 fusion.49
  462.2 13.2 fusion.3
  475.4 13.8 fusion.28
  489.3 175.7 %all-gather.28.cloned.1.call-done = bf16[2560,2560]{1,0:T(8,128)(2,1)} async-done(((bf16[640,2560]{1,0:T(8,128)(2,1)}), bf16[2560,2560]{1,0:T(8,128)(2,1)}) %all-gather.28.cloned.1.call-update) | async-done | bytes 13107216 | tf_op jit(solution)/shard_map/all_gather | solution.py:95
  674.4 604.7 %all-gather.30.cloned.1.call-done = bf16[2560,7168]{1,0:T(8,128)(2,1)} async-done(((bf16[640,7168]{1,0:T(8,128)(2,1)}), bf16[2560,7168]{1,0:T(8,128)(2,1)}) %all-gather.30.cloned.1.call-update) | async-done | bytes 36700176 | tf_op jit(solution)/shard_map/all_gather | solution.py:164
  1279.1 24.5 fusion.50
  1303.6 590.1 %all-gather.32.cloned.1.call-done = bf16[2560,7168]{1,0:T(8,128)(2,1)} async-done(((bf16[640,7168]{1,0:T(8,128)(2,1)}), bf16[2560,7168]{1,0:T(8,128)(2,1)}) %all-gather.32.cloned.1.call-update) | async-done | bytes 36700176 | tf_op jit(solution)/shard_map/all_gather | solution.py:165
  1893.7 24.5 fusion.51
  1918.3 590.1 %all-gather.34.cloned.1.call-done = bf16[2560,7168]{1,0:T(8,128)(2,1)} async-done(((bf16[640,7168]{1,0:T(8,128)(2,1)}), bf16[2560,7168]{1,0:T(8,128)(2,1)}) %all-gather.34.cloned.1.call-update) | async-done | bytes 36700176 | tf_op jit(solution)/shard_map/all_gather | solution.py:166
  2508.4 27.7 multiply_convert_fusion
  2536.1 18.5 fusion.52
  2554.6 20.8 multiply_reduce_fusion.1
  2589.8 14.7 fusion.5
  2605.8 22.3 fusion
  2628.1 28.1 fusion.2
  2656.3 12.5 bitcast_multiply_fusion.3
  2671.4 48.2 %reduce-scatter.15.cloned.1.call-done = f32[1,256,640]{1,2,0:T(8,128)} async-done(((f32[1,1024,640]{1,2,0:T(8,128)}), f32[1,256,640]{1,2,0:T(8,128)}) %reduce-scatter.15.cloned.1.call-update) | async-done | bytes 655376 | tf_op jit(solution)/shard_map/reduce_scatter | solution.py:249
  2722.2 9.1 convolution_multiply_fusion
  2755.8 91.9 %all-gather.40.cloned.1.call-done = bf16[1024,2560]{0,1:T(8,128)(2,1)} async-done(((bf16[256,2560]{0,1:T(8,128)(2,1)}), bf16[1024,2560]{0,1:T(8,128)(2,1)}) %all-gather.40.cloned.1.call-update) | async-done | bytes 5242896 | tf_op jit(solution)/shard_map/all_gather | solution.py:281
  2860.7 51.1 %all_to_all.73 = bf16[256,4,640]{2,0,1:T(8,128)(2,1)S(1)} all-to-all(bf16[256,4,640]{2,0,1:T(8,128)(2,1)S(1)} %fusion.27), channel_id=1, replica_groups=mesh['group'=4,'replica'=8] {'group'}, dimensions={1} | all-to-all | bytes 2621440 | tf_op jit(solution)/shard_map/all_to_all | solution.py:272
  2915.3 24.7 all-gather.38.cloned.1.call-done
  2943.5 94.7 %all-gather.36.cloned.1.call-done = bf16[1024,2560]{0,1:T(8,128)(2,1)} async-done(((bf16[256,2560]{0,1:T(8,128)(2,1)}), bf16[1024,2560]{0,1:T(8,128)(2,1)}) %all-gather.36.cloned.1.call-update) | async-done | bytes 5242896 | tf_op jit(solution)/shard_map/all_gather | solution.py:278
  3049.1 76.3 %all_to_all.74 = bf16[256,4,640]{0,2,1:T(8,128)(2,1)S(1)} all-to-all(bf16[256,4,640]{0,2,1:T(8,128)(2,1)} %bitcast.221), channel_id=1, replica_groups=mesh['group'=4,'replica'=8] {'group'}, dimensions={1} | all-to-all | bytes 2621440 | tf_op jit(solution)/shard_map/all_to_all | solution.py:275
  3126.8 191.6 %all-gather.46.cloned.1.call-done = bf16[1024,7168]{1,0:T(8,128)(2,1)} async-done(((bf16[256,7168]{1,0:T(8,128)(2,1)}), bf16[1024,7168]{1,0:T(8,128)(2,1)}) %all-gather.46.cloned.1.call-update) | async-done | bytes 14680080 | tf_op jit(solution)/shard_map/all_gather | solution.py:286
  3318.4 17.5 fusion.9
  3335.9 12.9 copy.109
  3350.2 75.0 %all_to_all.75 = bf16[256,4,640]{2,0,1:T(8,128)(2,1)S(1)} all-to-all(bf16[256,4,640]{2,0,1:T(8,128)(2,1)S(1)} %bitcast.220), channel_id=1, replica_groups=mesh['group'=4,'replica'=8] {'group'}, dimensions={1} | all-to-all | bytes 2621440 | tf_op jit(solution)/shard_map/all_to_all | solution.py:274
  3425.2 173.3 %all-gather.42.cloned.1.call-done = bf16[1024,7168]{1,0:T(8,128)(2,1)} async-done(((bf16[256,7168]{1,0:T(8,128)(2,1)}), bf16[1024,7168]{1,0:T(8,128)(2,1)}) %all-gather.42.cloned.1.call-update) | async-done | bytes 14680080 | tf_op jit(solution)/shard_map/all_gather | solution.py:284
  3598.5 17.4 convolution_convert_fusion.1
  3616.2 234.4 %all-gather.44.cloned.1.call-done = bf16[1024,7168]{1,0:T(8,128)(2,1)} async-done(((bf16[256,7168]{1,0:T(8,128)(2,1)}), bf16[1024,7168]{1,0:T(8,128)(2,1)}) %all-gather.44.cloned.1.call-update) | async-done | bytes 14680080 | tf_op jit(solution)/shard_map/all_gather | solution.py:285
  3850.6 17.4 convolution_convert_fusion
  3869.3 20.0 multiply_reduce_fusion
  3891.3 8.6 psum.7
  3905.2 81.6 %reduce-scatter.31.cloned.1.call-done = f32[80,2]{1,0:T(8,128)} async-done(((f32[2560,2]{1,0:T(8,128)}), f32[80,2]{1,0:T(8,128)}) %reduce-scatter.31.cloned.1.call-update) | async-done | bytes 656
  3988.9 44.5 %reduce-scatter.25.cloned.1.call-done = bf16[80,2560]{1,0:T(8,128)(2,1)} async-done(((bf16[640,2560]{1,0:T(8,128)(2,1)}), bf16[80,2560]{1,0:T(8,128)(2,1)}) %reduce-scatter.25.cloned.1.call-update) | async-done | bytes 409616 | tf_op jit(solution)/shard_map/reduce_scatter | solution.py:307
  4035.3 36.8 reduce-scatter.23.cloned.1.call-done
  4073.7 36.9 reduce-scatter.21.cloned.1.call-done
  4112.1 49.1 %reduce-scatter.19.cloned.1.call-done = bf16[80,2560]{1,0:T(8,128)(2,1)} async-done(((bf16[640,2560]{1,0:T(8,128)(2,1)}), bf16[80,2560]{1,0:T(8,128)(2,1)}) %reduce-scatter.19.cloned.1.call-update) | async-done | bytes 409616 | tf_op jit(solution)/shard_map/reduce_scatter | solution.py:298
  4163.2 77.1 %reduce-scatter.33.cloned.1.call-done = bf16[80,7168]{1,0:T(8,128)(2,1)} async-done(((bf16[640,7168]{1,0:T(8,128)(2,1)}), bf16[80,7168]{1,0:T(8,128)(2,1)}) %reduce-scatter.33.cloned.1.call-update) | async-done | bytes 1146896
  4244.0 74.9 %reduce-scatter.27.cloned.1.call-done = bf16[80,7168]{1,0:T(8,128)(2,1)} async-done(((bf16[640,7168]{1,0:T(8,128)(2,1)}), bf16[80,7168]{1,0:T(8,128)(2,1)}) %reduce-scatter.27.cloned.1.call-update) | async-done | bytes 1146896 | tf_op jit(solution)/shard_map/reduce_scatter | solution.py:310
  4321.8 76.2 %reduce-scatter.29.cloned.1.call-done = bf16[80,7168]{1,0:T(8,128)(2,1)} async-done(((bf16[640,7168]{1,0:T(8,128)(2,1)}), bf16[80,7168]{1,0:T(8,128)(2,1)}) %reduce-scatter.29.cloned.1.call-update) | async-done | bytes 1146896 | tf_op jit(solution)/shard_map/reduce_scatter | solution.py:313
  (212 shorter events, 153.4 us)
Async XLA Ops:
  7.2 70.8 %all-gather.24.cloned.1.call-start = ((), (), s32[]{:S(2)}) async-start(), calls=%async_computation.15 | async-start | bytes 4096000 | tf_op jit(solution)/shard_map/all_gather | solution.py:93
  7.9 18.5 copy-start
  7.9 136.0 %all-gather.22.cloned.1.call-start = ((), (), s32[]{:S(2)}) async-start(), calls=%async_computation.14 | async-start | bytes 4096000 | tf_op jit(solution)/shard_map/all_gather | solution.py:94
  8.7 168.9 %all-gather.50.cloned.1.call-start = ((), (), s32[]{:S(2)}) async-start(), calls=%async_computation.36 | async-start | bytes 1638400 | tf_op jit(solution)/shard_map/all_gather | solution.py:123
  24.7 413.8 %copy-start.27 = (f32[2560]{0:T(1024)}, f32[2560]{0:T(1024)S(1)}, u32[]{:S(2)}) copy-start(f32[2560]{0:T(1024)S(1)} %reshape.535) | copy-start | bytes 30724
  25.8 421.4 %copy-start.22 = (f32[256,80]{0,1:T(8,128)}, f32[256,80]{0,1:T(8,128)S(1)}, u32[]{:S(2)}) copy-start(f32[256,80]{0,1:T(8,128)S(1)} %get-tuple-element.147) | copy-start | bytes 245764
  25.8 421.4 %copy-start.24 = (f32[256,80]{0,1:T(8,128)}, f32[256,80]{0,1:T(8,128)S(1)}, u32[]{:S(2)}) copy-start(f32[256,80]{0,1:T(8,128)S(1)} %get-tuple-element.148) | copy-start | bytes 245764
  27.3 411.2 %copy-start.31 = (f32[256]{0:T(256)}, f32[256]{0:T(256)S(1)}, u32[]{:S(2)}) copy-start(f32[256]{0:T(256)S(1)} %get-tuple-element.150) | copy-start | bytes 3076
  86.8 124.5 %all-gather.48.cloned.1.call-start = ((), (), s32[]{:S(2)}) async-start(), calls=%async_computation.35 | async-start | bytes 1638400 | tf_op jit(solution)/shard_map/all_gather | solution.py:124
  147.8 290.7 %all-gather.26.cloned.1.call-start = ((), (), s32[]{:S(2)}) async-start(), calls=%async_computation.16 | async-start | bytes 16384000 | tf_op jit(solution)/shard_map/all_gather | solution.py:92
  148.4 516.5 %all-gather.28.cloned.1.call-start = ((), (), s32[]{:S(2)}) async-start(), calls=%async_computation.17 | async-start | bytes 16384000 | tf_op jit(solution)/shard_map/all_gather | solution.py:95
  149.0 1130.1 %all-gather.30.cloned.1.call-start = ((), (), s32[]{:S(2)}) async-start(), calls=%async_computation.18 | async-start | bytes 45875200 | tf_op jit(solution)/shard_map/all_gather | solution.py:164
  149.7 1744.0 %all-gather.32.cloned.1.call-start = ((), (), s32[]{:S(2)}) async-start(), calls=%async_computation.19 | async-start | bytes 45875200 | tf_op jit(solution)/shard_map/all_gather | solution.py:165
  150.5 2.7 copy-start.34
  150.5 2357.9 %all-gather.34.cloned.1.call-start = ((), (), s32[]{:S(2)}) async-start(), calls=%async_computation.20 | async-start | bytes 45875200 | tf_op jit(solution)/shard_map/all_gather | solution.py:166
  151.2 2518.3 %reduce-scatter.17.cloned.1.call-start = ((), (), s32[]{:S(2)}) async-start(), calls=%async_computation.22 | async-start | bytes 3276800 | tf_op jit(solution)/shard_map/reduce_scatter | solution.py:250
  179.1 268.6 %copy-start.4 = (bf16[1024,640]{0,1:T(8,128)(2,1)}, bf16[1024,640]{0,1:T(8,128)(2,1)S(1)}, u32[]{:S(2)}) copy-start(bf16[1024,640]{0,1:T(8,128)(2,1)S(1)} %copy.84) | copy-start | bytes 3932164
  447.7 14.4 copy-start.2
  462.1 13.3 copy-start.8
  489.2 183.1 %copy-start.26 = (bf16[8,80,4,256]{3,1,2,0:T(8,128)(2,1)}, bf16[8,80,4,256]{3,1,2,0:T(8,128)(2,1)S(1)}, u32[]{:S(2)}) copy-start(bf16[8,80,4,256]{3,1,2,0:T(8,128)(2,1)S(1)} %fusion.28) | copy-start | bytes 3932164
  674.3 1219.4 %copy-start.12 = (bf16[256,2560]{1,0:T(8,128)(2,1)}, bf16[256,2560]{1,0:T(8,128)(2,1)S(1)}, u32[]{:S(2)}) copy-start(bf16[256,2560]{1,0:T(8,128)(2,1)S(1)} %multiply_convert_fusion.3) | copy-start | bytes 3932164
  1303.6 1204.8 %copy-start.10 = (bf16[1,256,2560]{2,1,0:T(8,128)(2,1)S(1)}, bf16[1,256,2560]{2,1,0:T(8,128)(2,1)}, u32[]{:S(2)}) copy-start(bf16[1,256,2560]{2,1,0:T(8,128)(2,1)} %param.25) | copy-start | bytes 3932164
  2536.1 18.5 copy-start.7
  2604.5 115.0 %reduce-scatter.15.cloned.1.call-start = ((), (), s32[]{:S(2)}) async-start(), calls=%async_computation.21 | async-start | bytes 3276800 | tf_op jit(solution)/shard_map/reduce_scatter | solution.py:249
  2628.1 28.1 copy-start.3
  2668.8 50.8 %copy-start.25 = (f32[256,80]{0,1:T(8,128)S(1)}, f32[256,80]{0,1:T(8,128)}, u32[]{:S(2)}) copy-start(f32[256,80]{0,1:T(8,128)} %copy-done.24) | copy-start | bytes 245764
  2668.8 178.9 %all-gather.40.cloned.1.call-start = ((), (), s32[]{:S(2)}) async-start(), calls=%async_computation.28 | async-start | bytes 6553600 | tf_op jit(solution)/shard_map/all_gather | solution.py:281
  2669.4 51.5 %copy-start.23 = (f32[256,80]{0,1:T(8,128)S(1)}, f32[256,80]{0,1:T(8,128)}, u32[]{:S(2)}) copy-start(f32[256,80]{0,1:T(8,128)} %copy-done.22) | copy-start | bytes 245764
  2669.4 242.4 %all-gather.52.cloned.1.call-start = ((), (), s32[]{:S(2)}) async-start(), calls=%async_computation.37 | async-start | bytes 1638400 | tf_op jit(solution)/shard_map/all_gather | solution.py:280
  2671.3 268.7 %all-gather.38.cloned.1.call-start = ((), (), s32[]{:S(2)}) async-start(), calls=%async_computation.25 | async-start | bytes 1638400 | tf_op jit(solution)/shard_map/all_gather | solution.py:279
  2721.8 316.5 %all-gather.36.cloned.1.call-start = ((), (), s32[]{:S(2)}) async-start(), calls=%async_computation.23 | async-start | bytes 6553600 | tf_op jit(solution)/shard_map/all_gather | solution.py:278
  2733.6 584.8 %all-gather.46.cloned.1.call-start = ((), (), s32[]{:S(2)}) async-start(), calls=%async_computation.34 | async-start | bytes 18350080 | tf_op jit(solution)/shard_map/all_gather | solution.py:286
  2734.2 864.3 %all-gather.42.cloned.1.call-start = ((), (), s32[]{:S(2)}) async-start(), calls=%async_computation.30 | async-start | bytes 18350080 | tf_op jit(solution)/shard_map/all_gather | solution.py:284
  2734.8 1115.8 %all-gather.44.cloned.1.call-start = ((), (), s32[]{:S(2)}) async-start(), calls=%async_computation.32 | async-start | bytes 18350080 | tf_op jit(solution)/shard_map/all_gather | solution.py:285
  2736.1 5.6 copy-start.16
  2737.3 110.4 %all-to-all-start.1 = ((bf16[256,4,640]{2,0,1:T(8,128)(2,1)}), bf16[256,4,640]{2,0,1:T(8,128)(2,1)}, u32[]{:S(2)}, u32[]{:S(2)}) async-start(bf16[256,4,640]{2,0,1:T(8,128)(2,1)} %bitcast.218), calls=%async_computation.6 | async-start | bytes 2621440 | tf_op jit(solution)/shard_map/all_to_all | solution.py:273
  2741.6 7.0 copy-start.20
  2741.6 1245.1 %reduce-scatter.31.cloned.1.call-start = ((), (), s32[]{:S(2)}) async-start(), calls=%async_computation.38 | async-start | bytes 1351680
  2741.7 6.9 copy-start.17
  2748.6 2.3 copy-start.19
  2755.6 1277.7 %reduce-scatter.25.cloned.1.call-start = ((), (), s32[]{:S(2)}) async-start(), calls=%async_computation.29 | async-start | bytes 3686400 | tf_op jit(solution)/shard_map/reduce_scatter | solution.py:307
  2855.9 1216.2 %reduce-scatter.23.cloned.1.call-start = ((), (), s32[]{:S(2)}) async-start(), calls=%async_computation.27 | async-start | bytes 921600 | tf_op jit(solution)/shard_map/reduce_scatter | solution.py:304
  2915.3 1195.3 %reduce-scatter.21.cloned.1.call-start = ((), (), s32[]{:S(2)}) async-start(), calls=%async_computation.26 | async-start | bytes 921600 | tf_op jit(solution)/shard_map/reduce_scatter | solution.py:301
  2943.5 1217.8 %reduce-scatter.19.cloned.1.call-start = ((), (), s32[]{:S(2)}) async-start(), calls=%async_computation.24 | async-start | bytes 3686400 | tf_op jit(solution)/shard_map/reduce_scatter | solution.py:298
  3046.1 1194.1 %reduce-scatter.33.cloned.1.call-start = ((), (), s32[]{:S(2)}) async-start(), calls=%async_computation.39 | async-start | bytes 10321920
  3348.8 970.1 %reduce-scatter.27.cloned.1.call-start = ((), (), s32[]{:S(2)}) async-start(), calls=%async_computation.31 | async-start | bytes 10321920 | tf_op jit(solution)/shard_map/reduce_scatter | solution.py:310
  3615.9 782.0 %reduce-scatter.29.cloned.1.call-start = ((), (), s32[]{:S(2)}) async-start(), calls=%async_computation.33 | async-start | bytes 10321920 | tf_op jit(solution)/shard_map/reduce_scatter | solution.py:313
  3869.3 31.1 copy-start.33
  (15 other events, 21.5 us)
Sparse Core Ops, SparseCore 0:
  9.6 68.3 all-gather.23
  79.5 64.2 all-gather.21
  146.0 31.4 all-gather.49
  179.5 31.6 all-gather.47
  212.7 225.7 all-gather.25
  439.9 224.9 all-gather.27
  666.5 612.5 all-gather.29
  1280.6 613.0 all-gather.31
  1895.3 613.0 all-gather.33
  2604.6 50.8 reduce-scatter.16
  2668.9 50.5 reduce-scatter.14
  2721.0 126.6 all-gather.39
  2849.8 56.4 all-gather.51
  2908.4 31.6 all-gather.37
  2942.0 96.2 all-gather.35
  3039.7 278.6 all-gather.45
  3319.8 278.6 all-gather.41
  3599.9 250.6 all-gather.43
  3853.4 133.3 reduce-scatter.30
  3990.4 42.8 reduce-scatter.24
  4037.6 34.4 reduce-scatter.22
  4076.0 34.4 reduce-scatter.20
  4114.4 46.8 reduce-scatter.18
  4165.2 75.0 reduce-scatter.32
  4243.9 75.0 reduce-scatter.26
  4322.9 75.0 reduce-scatter.28
where the time goes:
time: 4410 us
  waiting for transfers between devices  3680 us (83%)
  matrix products  341 us (8%)
  blocking collectives  239 us (5%)
  other arithmetic  83.8 us (2%)
  local copies, waits for them, and re-layouts  45.2 us (1%)
    all_gather x1, waiting for transfers between devices, shards(): gate_piece = lax.all_gather(w_gate, 'group', axis=0, tiled=True)  605 us
    all_gather x1, waiting for transfers between devices, shards(): down_piece = lax.all_gather(w_down, 'group', axis=0, tiled=True)  590 us
    all_gather x1, waiting for transfers between devices, shards(): up_piece = lax.all_gather(w_up, 'group', axis=0, tiled=True)  590 us
    all_gather x1, waiting for transfers between devices, shards(): lax.all_gather(grad_lift_low, 'group', axis=0, tiled=True)  234 us
    all_gather x1, waiting for transfers between devices, shards(): query_piece = lax.all_gather(w_query, 'group', axis=0, tiled=True)  225 us
    all_gather x1, waiting for transfers between devices, shards(): lax.all_gather(hidden, 'group', axis=0, tiled=True)  192 us
    all_gather x1, waiting for transfers between devices, shards(): out_piece = lax.all_gather(w_out, 'group', axis=0, tiled=True)  176 us
    all_gather x1, waiting for transfers between devices, shards(): lax.all_gather(grad_gate_low, 'group', axis=0, tiled=True)  173 us
  transfers between devices with their start and end apart: 27, of which 24 were waited for; matrix products, arithmetic and copies ran while one was open for 8% of the time, Pallas kernels for 0%

commit v1 on v0

v1 whole, which is shorter than its diff:
```python
import numpy as np

import jax
import jax.numpy as jnp
from jax import lax
from jax.sharding import Mesh, PartitionSpec as P

HEADS = 32
KV_HEADS = 8
HEAD_DIM = 80
PIECE = 256

epsilon = 1e-05
rope_base = 1000000.0

CHIPS = 4
SUM_AXES = ("group", "core", "dp")
REPLICA = ("dp", "chip", "core")


def rope_tables(places):
    halves = HEAD_DIM // 2
    frequency = rope_base ** (-(jnp.arange(halves, dtype=jnp.float32) * 2.0 / HEAD_DIM))
    angles = places.astype(jnp.float32)[..., None] * frequency
    angles = jnp.concatenate([angles, angles], axis=-1)
    return (jnp.cos(angles), jnp.sin(angles))


def rotate(values, cosine, sine):
    halves = HEAD_DIM // 2
    turned = jnp.concatenate([-values[..., halves:], values[..., :halves]], axis=-1)
    return values * cosine[:, None, :] + turned * sine[:, None, :]


def unrotate(grads, cosine, sine):
    halves = HEAD_DIM // 2
    shifted = grads * sine[:, None, :]
    turned = jnp.concatenate([shifted[..., halves:], -shifted[..., :halves]], axis=-1)
    return grads * cosine[:, None, :] + turned


def times(left, right):
    return jnp.dot(left, right, preferred_element_type=jnp.float32)


def times_t(left, right):
    return lax.dot_general(
        left, right, (((1,), (1,)), ((), ())), preferred_element_type=jnp.float32
    )


def inner_t(left, right):
    return lax.dot_general(
        left, right, (((0,), (0,)), ((), ())), preferred_element_type=jnp.float32
    )


def inverse_rms(values):
    return lax.rsqrt(jnp.mean(values * values, axis=-1, keepdims=True) + epsilon)


def norm_back(grad_normed, source, inverse, gain_full):
    weighted = grad_normed * gain_full
    average = jnp.mean(weighted * source, axis=-1, keepdims=True)
    return inverse * weighted - source * (inverse * inverse * inverse) * average


def piece_index(starts, places):
    labels = jnp.zeros(places.shape, jnp.int32)
    for which in range(2):
        inside = (places >= starts[which]) & (places < starts[which] + PIECE)
        labels = jnp.where(inside, which + 1, labels)
    return labels


def swap(value, flip):
    pairs = [(chip, chip ^ flip) for chip in range(CHIPS)]
    return lax.ppermute(value, "chip", pairs)


def collect(block):
    half = block.shape[0] // 2
    first = swap(block, 1)
    second = swap(block, 2)
    low = swap(first[:half], 2)
    high = swap(second[half:], 1)
    return [block, first, second, jnp.concatenate([low, high], axis=0)]


def give_back(parts):
    low_type = jnp.bfloat16
    half = parts[0].shape[0] // 2
    low = swap(parts[3][:half].astype(low_type), 1)
    high = swap(parts[3][half:].astype(low_type), 2)
    for_first = jnp.concatenate(
        [parts[1][:half], parts[1][half:] + high.astype(jnp.float32)], axis=0
    ).astype(low_type)
    for_second = jnp.concatenate(
        [parts[2][:half] + low.astype(jnp.float32), parts[2][half:]], axis=0
    ).astype(low_type)
    from_first = swap(for_first, 1)
    from_second = swap(for_second, 2)
    return parts[0] + from_first.astype(jnp.float32) + from_second.astype(jnp.float32)


def shards(
    layer_input,
    positions,
    piece_starts,
    gain_attn,
    w_query,
    w_key,
    w_value,
    w_out,
    gain_mlp,
    w_gate,
    w_up,
    w_down,
    out_grad,
):
    sequences, block_size, model_width = layer_input.shape
    assert sequences == 1
    groups = lax.axis_size("group")
    spread = lax.axis_size("dp")
    group_at, spread_at = lax.axis_index("group"), lax.axis_index("dp")
    chip, core = lax.axis_index("chip"), lax.axis_index("core")
    full_len = block_size * groups
    scaling = HEAD_DIM ** (-0.5)
    repeats = HEADS // KV_HEADS
    kv_own = KV_HEADS // CHIPS
    heads_own = HEADS // CHIPS
    query_width, kv_width = heads_own * HEAD_DIM, kv_own * HEAD_DIM
    half_rows = w_query.shape[0] // 2

    def own_part(weight):
        width = weight.shape[1] // CHIPS
        return lax.dynamic_slice(weight, (core * half_rows, chip * width), (half_rows, width))

    def gathered(*weights):
        part = jnp.concatenate([own_part(weight) for weight in weights], axis=1)
        return lax.all_gather(part, ("group", "core"), axis=0, tiled=True)

    gains = lax.all_gather(jnp.stack([gain_attn, gain_mlp]), "group", axis=1, tiled=True)
    gain_one, gain_two = gains[0].astype(jnp.float32), gains[1].astype(jnp.float32)

    w_qkv = gathered(w_query, w_key, w_value)
    w_mix = gathered(w_out)
    w_lift = gathered(w_gate, w_up)
    w_sink = gathered(w_down)

    source_low = layer_input[0]
    source_all = jnp.concatenate(collect(source_low), axis=0).astype(jnp.float32)
    small = jnp.concatenate([positions[0], piece_starts[0]])
    smalls = jnp.stack([small, swap(small, 1), swap(small, 2), swap(small, 3)])
    places, starts_all = smalls[:, :block_size].reshape(-1), smalls[:, block_size:]
    grad_low = jnp.concatenate(collect(out_grad[0]), axis=0)

    normed_one = (source_all * inverse_rms(source_all) * gain_one).astype(jnp.bfloat16)
    lin = times(normed_one, w_qkv)
    cosine, sine = rope_tables(places)
    tokens = CHIPS * block_size
    query_rot = rotate(lin[:, :query_width].reshape(tokens, heads_own, HEAD_DIM), cosine, sine)
    query_rot = query_rot.astype(jnp.bfloat16)
    key_rot = rotate(
        lin[:, query_width : query_width + kv_width].reshape(tokens, kv_own, HEAD_DIM), cosine, sine
    ).astype(jnp.bfloat16)
    value_low = lin[:, query_width + kv_width :].astype(jnp.bfloat16)
    both = jnp.concatenate([key_rot.reshape(tokens, kv_width), value_low], axis=1)
    both_all = lax.all_gather(both, "group", axis=0)
    both_all = both_all.reshape(groups, CHIPS, block_size, 2, kv_own, HEAD_DIM)
    both_all = both_all.transpose(3, 1, 4, 0, 2, 5).reshape(2, CHIPS, kv_own, full_len, HEAD_DIM)
    key_all, value_all = both_all[0], both_all[1]

    def by_head(rows):
        rows = rows.reshape(CHIPS, block_size, kv_own, repeats, HEAD_DIM)
        return rows.transpose(0, 2, 3, 1, 4)

    def by_token(heads):
        return heads.transpose(0, 3, 1, 2, 4).reshape(tokens, query_width)

    query_places = group_at * block_size + jnp.arange(block_size, dtype=jnp.int32)
    key_places = jnp.arange(full_len, dtype=jnp.int32)

    def allowed_for(starts):
        query_labels = piece_index(starts, query_places)
        key_labels = piece_index(starts, key_places)
        causal = key_places[None, :] <= query_places[:, None]
        same_piece = (query_labels[:, None] == key_labels[None, :]) & (query_labels[:, None] > 0)
        return causal | same_piece

    query_heads = by_head(query_rot)

    def scores_of(which):
        raw = (
            jnp.einsum(
                "krqd,ksd->krqs",
                query_heads[which],
                key_all[which],
                preferred_element_type=jnp.float32,
            )
            * scaling
        )
        return jnp.where(allowed_for(starts_all[which])[None, None], raw, -1e30)

    mixed_heads, log_totals = [], []
    for which in range(CHIPS):
        masked = scores_of(which)
        highest_score = jnp.max(masked, axis=-1, keepdims=True)
        raised = jnp.exp(masked - highest_score)
        summed = jnp.sum(raised, axis=-1, keepdims=True)
        chances_low = (raised / summed).astype(jnp.bfloat16)
        mixed_heads.append(
            jnp.einsum(
                "krqs,ksd->krqd",
                chances_low,
                value_all[which],
                preferred_element_type=jnp.float32,
            ).astype(jnp.bfloat16)
        )
        log_totals.append(highest_score + jnp.log(summed))
    mixed_low = by_token(jnp.stack(mixed_heads))

    def blocks_of(values):
        return [values[i * block_size : (i + 1) * block_size] for i in range(CHIPS)]

    source = source_low.astype(jnp.float32)
    inverse_one = inverse_rms(source)
    unit_one = source * inverse_one
    middle = source + give_back(blocks_of(times_t(mixed_low, w_mix)))
    inverse_two = inverse_rms(middle)
    unit_two = middle * inverse_two
    normed_two = jnp.concatenate(collect((unit_two * gain_two).astype(jnp.bfloat16)), axis=0)
    wide = w_lift.shape[1] // 2
    both_up = times(normed_two, w_lift)
    gated, lifted = both_up[:, :wide], both_up[:, wide:]
    activated = jax.nn.silu(gated)
    hidden = (activated * lifted).astype(jnp.bfloat16)
    output_full = middle + give_back(blocks_of(times_t(hidden, w_sink)))

    grad_hidden = times(grad_low, w_sink)
    sigmoid_gate = jax.nn.sigmoid(gated)
    grad_gate_low = (
        grad_hidden * lifted * (sigmoid_gate + gated * sigmoid_gate * (1.0 - sigmoid_gate))
    ).astype(jnp.bfloat16)
    grad_lift_low = (grad_hidden * activated).astype(jnp.bfloat16)
    grad_both = jnp.concatenate([grad_gate_low, grad_lift_low], axis=1)
    grad_normed_two = give_back(blocks_of(times_t(grad_both, w_lift)))
    grad_gain_two = jnp.sum(grad_normed_two * unit_two, axis=0)
    grad_middle = out_grad[0].astype(jnp.float32) + norm_back(
        grad_normed_two, middle, inverse_two, gain_two
    )
    grad_middle_low = jnp.concatenate(collect(grad_middle.astype(jnp.bfloat16)), axis=0)
    grad_mixed_low = by_head(times(grad_middle_low, w_mix).astype(jnp.bfloat16))

    grad_query_heads, grad_keys, grad_values = [], [], []
    for which in range(CHIPS):
        chances = jnp.exp(scores_of(which) - log_totals[which])
        grad_seq = grad_mixed_low[which]
        grad_values.append(
            jnp.einsum(
                "krqs,krqd->ksd",
                chances.astype(jnp.bfloat16),
                grad_seq,
                preferred_element_type=jnp.float32,
            )
        )
        grad_chance = jnp.einsum(
            "krqd,ksd->krqs", grad_seq, value_all[which], preferred_element_type=jnp.float32
        )
        grad_score = chances * (
            grad_chance - jnp.sum(chances * grad_chance, axis=-1, keepdims=True)
        )
        grad_score = grad_score.astype(jnp.bfloat16)
        grad_query_heads.append(
            jnp.einsum(
                "krqs,ksd->krqd", grad_score, key_all[which], preferred_element_type=jnp.float32
            )
            * scaling
        )
        grad_keys.append(
            jnp.einsum(
                "krqs,krqd->ksd",
                grad_score,
                query_heads[which],
                preferred_element_type=jnp.float32,
            )
            * scaling
        )
    grad_kv = jnp.stack([jnp.stack(grad_keys), jnp.stack(grad_values)]).astype(jnp.bfloat16)
    grad_kv = grad_kv.reshape(2, CHIPS, kv_own, groups, block_size, HEAD_DIM)
    grad_kv = grad_kv.transpose(3, 1, 4, 0, 2, 5).reshape(groups * tokens, 2 * kv_width)
    grad_kv = lax.psum_scatter(grad_kv, "group", scatter_dimension=0, tiled=True)
    grad_query_low = unrotate(
        by_token(jnp.stack(grad_query_heads)).reshape(tokens, heads_own, HEAD_DIM), cosine, sine
    ).astype(jnp.bfloat16)
    grad_key_low = unrotate(
        grad_kv[:, :kv_width].astype(jnp.float32).reshape(tokens, kv_own, HEAD_DIM), cosine, sine
    ).astype(jnp.bfloat16)
    grad_qkv = jnp.concatenate(
        [
            grad_query_low.reshape(tokens, query_width),
            grad_key_low.reshape(tokens, kv_width),
            grad_kv[:, kv_width:],
        ],
        axis=1,
    )
    added = give_back(blocks_of(times_t(grad_qkv, w_qkv)))
    grad_gain_one = jnp.sum(added * unit_one, axis=0)
    input_grad = grad_middle + norm_back(added, source, inverse_one, gain_one)

    count = spread * CHIPS * 2
    whose = (spread_at * CHIPS + chip) * 2 + core

    def owned(left, right, widths):
        total = inner_t(left, right).astype(jnp.bfloat16)
        total = lax.psum_scatter(total, SUM_AXES, scatter_dimension=0, tiled=True)
        rows, columns = total.shape[0] // CHIPS, total.shape[1]
        total = total.reshape(CHIPS, rows, columns)
        pieces = []
        for step in range(CHIPS):
            pairs = []
            for source_at in range(count):
                at_spread, at_chip, at_core = (
                    source_at // (2 * CHIPS),
                    source_at // 2 % CHIPS,
                    source_at % 2,
                )
                target = (at_core * spread + at_spread) * CHIPS + (at_chip ^ step)
                pairs.append((source_at, target))
            block = lax.dynamic_index_in_dim(total, chip ^ step, axis=0, keepdims=False)
            pieces.append(lax.ppermute(block, REPLICA, pairs))
        pieces = jnp.stack(pieces)
        ordered = [
            lax.dynamic_index_in_dim(pieces, (whose % CHIPS) ^ at, axis=0, keepdims=False)
            for at in range(CHIPS)
        ]
        result, start = [], 0
        for width in widths:
            result.append(
                jnp.concatenate([part[:, start : start + width] for part in ordered], axis=1)
            )
            start += width
        return [item.astype(jnp.float32) for item in result]

    (grad_down,) = owned(grad_low, hidden, (wide,))
    grad_gate, grad_up = owned(normed_two, grad_both, (wide, wide))
    (grad_out,) = owned(grad_middle_low, mixed_low, (query_width,))
    grad_query, grad_key, grad_value = owned(
        normed_one, grad_qkv, (query_width, kv_width, kv_width)
    )

    gain_owned = lax.psum_scatter(
        jnp.stack([grad_gain_one, grad_gain_two]),
        ("group",) + REPLICA,
        scatter_dimension=1,
        tiled=True,
    )
    squares = jnp.stack(
        [jnp.sum(source * source), jnp.sum(middle * middle), jnp.sum(output_full * output_full)]
    )
    square_totals = lax.psum(squares[None], "group")
    stream_rms = jnp.sqrt(square_totals / (full_len * model_width))
    return (
        output_full.astype(jnp.bfloat16)[None],
        input_grad[None],
        gain_owned[0],
        grad_query,
        grad_key,
        grad_value,
        grad_out,
        gain_owned[1],
        grad_gate,
        grad_up,
        grad_down,
        stream_rms,
    )


def solution(mesh):
    groups, replicas = mesh.shape["group"], mesh.shape["replica"]
    spread = replicas // (2 * CHIPS)
    devices = np.asarray(mesh.devices).reshape(groups, spread, CHIPS, 2)
    split = Mesh(devices, ("group", "dp", "chip", "core"))
    everyone = ("group",) + REPLICA
    placed = (
        P(REPLICA, "group", None),
        P(REPLICA, "group"),
        P(REPLICA, None),
        P("group"),
        P("group", None),
        P("group", None),
        P("group", None),
        P("group", None),
        P("group"),
        P("group", None),
        P("group", None),
        P("group", None),
        P(REPLICA, "group", None),
    )
    return jax.shard_map(
        shards,
        mesh=split,
        in_specs=placed,
        out_specs=(
            P(REPLICA, "group", None),
            P(REPLICA, "group", None),
            P(everyone),
            P(everyone, None),
            P(everyone, None),
            P(everyone, None),
            P(everyone, None),
            P(everyone),
            P(everyone, None),
            P(everyone, None),
            P(everyone, None),
            P(REPLICA, None),
        ),
        check_vma=False,
    )
```

time: 4410 us -> 1340 us (0.30)
  waiting for transfers between devices: 3680 us -> 766 us
  blocking collectives: 239 us -> 24.8 us
  matrix products: 341 us -> 245 us
  starting transfers between devices: 6.21 us -> 69.9 us
  local copies, waits for them, and re-layouts: 45.2 us -> 106 us
    all_gather x16 -> x5, waiting for transfers between devices: 3140 us -> 82.4 us  [the longest x4 74.8 us: gathered(): return lax.all_gather(part, ('group', 'core'), axis=0, tiled=True)]
    ppermute x0 -> x51, waiting for transfers between devices: none -> 318 us  [the longest x35 283 us: swap(): return lax.ppermute(value, 'chip', pairs)]
    all_to_all x3 -> x0, blocking collectives: 202 us -> none  [the longest x1 76.3 us: shards(): lax.all_to_all(grad_low, 'group', split_axis=1, concat_axis=0, tiled=True)]
    reduce_scatter x8 -> x5, waiting for transfers between devices: 367 us -> 237 us  [the longest x4 232 us: owned(): total = lax.psum_scatter(total, SUM_AXES, scatter_dimension=0, tiled=True)]
    ppermute x0 -> x51, starting transfers between devices: none -> 68.9 us  [the longest x35 43.8 us: swap(): return lax.ppermute(value, 'chip', pairs)]
    dot_general x13 -> x28, matrix products: 188 us -> 127 us  [the longest x4 61.7 us: times(): return jnp.dot(left, right, preferred_element_type=jnp.float32)]
    unnamed x28 -> x12, waiting for transfers between devices: 165 us -> 129 us
  transfers between devices with their start and end apart: 27 -> 62, of which waited for: 24 -> 35; matrix products, arithmetic and copies ran while one was open for 8% -> 20% of each run, Pallas kernels for 0% -> 0%
where the time goes in v1:
time: 1340 us
  waiting for transfers between devices  766 us (57%)
  matrix products  245 us (18%)
  local copies, waits for them, and re-layouts  106 us (8%)
  other arithmetic  103 us (8%)
  starting transfers between devices  69.9 us (5%)
  blocking collectives  24.8 us (2%)
  between operations  21.6 us (2%)
    ppermute x35, waiting for transfers between devices, swap(): return lax.ppermute(value, 'chip', pairs)  283 us
    reduce_scatter x4, waiting for transfers between devices, owned(): total = lax.psum_scatter(total, SUM_AXES, scatter_dimension=0, tiled=True)  232 us
    unnamed x12, waiting for transfers between devices  129 us
    all_gather x4, waiting for transfers between devices, gathered(): return lax.all_gather(part, ('group', 'core'), axis=0, tiled=True)  74.8 us
    dot_general x4, matrix products, times(): return jnp.dot(left, right, preferred_element_type=jnp.float32)  61.7 us
    dot_general x4, matrix products, inner_t(): lax.dot_general(left, right, (((0,), (0,)), ((), ())), preferred_element_...  61 us
    dot_general x4, matrix products, times_t(): lax.dot_general(left, right, (((1,), (1,)), ((), ())), preferred_element_...  56.4 us
    ppermute x35, starting transfers between devices, swap(): return lax.ppermute(value, 'chip', pairs)  43.8 us
  transfers between devices with their start and end apart: 62, of which 35 were waited for; matrix products, arithmetic and copies ran while one was open for 20% of the time, Pallas kernels for 0%

profile of v1, /device:TPU:0, one launch (start us, length us, event | category | flops | bytes accessed | tf_op | source)
XLA Modules:
  0.0 1335.9 jit_solution(7680100821952830985)
XLA Ops:
  19.7 13.4 %all_gather.21 = bf16[2,2560]{1,0:T(2,128)(2,1)S(1)} all-gather(bf16[2,640]{1,0:T(2,128)(2,1)S(1)} %pad_maximum_fusion.26), channel_id=1, replica_groups=mesh['group'=4,'dp'=1,'chip'=4,'core'=2] {'group'}, dimensions={1}, use_global_device_ids=true | all-gather | bytes 12800 | tf_op jit(solution)/shard_map/all_gather | solution.py:143
  34.7 11.5 collective-permute-done
  49.8 11.9 collective-permute-done.2
  70.5 9.2 fusion.46
  128.7 7.6 all-gather.15.cloned.1.call-done
  136.2 5.5 reshape.665
  178.3 5.2 fusion.98
  183.6 6.3 fusion.97
  191.4 6.7 fusion.173
  202.4 13.6 %collective-permute-done.9 = bf16[128,2560]{1,0:T(8,128)(2,1)S(1)} collective-permute-done((bf16[128,2560]{1,0:T(8,128)(2,1)S(1)}, bf16[128,2560]{1,0:T(8,128)(2,1)S(1)}, u32[]{:S(2)}, u32[]{:S(2)}) %collective-permute-start.9) | collective-permute-done | bytes 655392 | tf_op jit(solution)/shard_map/ppermute | solution.py:78
  220.3 23.8 %collective-permute-done.19 = bf16[256,2560]{1,0:T(8,128)(2,1)S(1)} collective-permute-done((bf16[256,2560]{1,0:T(8,128)(2,1)S(1)}, bf16[256,2560]{1,0:T(8,128)(2,1)S(1)}, u32[]{:S(2)}, u32[]{:S(2)}) %collective-permute-start.19) | collective-permute-done | bytes 1310752 | tf_op jit(solution)/shard_map/ppermute | solution.py:78
  247.2 26.5 %collective-permute-done.10 = bf16[256,2560]{1,0:T(8,128)(2,1)S(1)} collective-permute-done((bf16[256,2560]{1,0:T(8,128)(2,1)S(1)}, bf16[256,2560]{1,0:T(8,128)(2,1)S(1)}, u32[]{:S(2)}, u32[]{:S(2)}) %collective-permute-start.10) | collective-permute-done | bytes 1310752 | tf_op jit(solution)/shard_map/ppermute | solution.py:78
  279.5 8.3 collective-permute-done.21
  287.9 26.4 %collective-permute-done.12 = bf16[256,2560]{1,0:T(8,128)(2,1)S(1)} collective-permute-done((bf16[256,2560]{1,0:T(8,128)(2,1)S(1)}, bf16[256,2560]{1,0:T(8,128)(2,1)S(1)}, u32[]{:S(2)}, u32[]{:S(2)}) %collective-permute-start.12) | collective-permute-done | bytes 1310752 | tf_op jit(solution)/shard_map/ppermute | solution.py:78
  319.0 11.3 collective-permute-done.13
  332.1 9.5 all-gather.11.cloned.1.call-done
  341.6 27.3 %fusion.177 = f32[1024,3584]{1,0:T(8,128)} fusion(bf16[1024,2560]{1,0:T(8,128)(2,1)} %constant_dynamic-update-slice_fusion.5, bf16[2560,3584]{1,0:T(8,128)(2,1)} %all-gather.11.cloned.1.call-done), kind=kOutput, calls=%fused_computation.389 | convolution fusion | flops 18790481920 | bytes 38273024 | tf_op jit(solution)/shard_map/dot_general | solution.py:43
  368.9 60.9 %all-gather.13.cloned.1.call-done = bf16[2560,1792]{1,0:T(8,128)(2,1)} async-done(((bf16[320,1792]{1,0:T(8,128)(2,1)}), bf16[2560,1792]{1,0:T(8,128)(2,1)}) %all-gather.13.cloned.1.call-update) | async-done | bytes 9175056 | tf_op jit(solution)/shard_map/all_gather | solution.py:141
  429.9 21.0 %multiply_convert_fusion.5 = (bf16[1024,1792]{1,0:T(8,128)(2,1)S(1)}, bf16[1024,1792]{1,0:T(8,128)(2,1)}, bf16[1024,1792]{1,0:T(8,128)(2,1)}) fusion(f32[1024,3584]{1,0:T(8,128)} %fusion.177, bf16[1024,2560]{1,0:T(8,128)(2,1)} %copy-done.52, bf16[2560,1792]{1,0:T(8,128)(2,1)} %all-gather.13.cloned.1.call-done), kind=kOutput, calls=%fused_computation.37 | convolution fusion | flops 9420931072 | bytes 40108032 | tf_op jit(solution)/shard_map/dot_general | solution.py:43
  450.9 25.5 %fusion.175 = (bf16[1024,2560]{1,0:T(8,128)(2,1)}, f32[1024,2560]{1,0:T(8,128)S(1)}) fusion(bf16[2560,3584]{1,0:T(8,128)(2,1)} %all-gather.11.cloned.1.call-done, bf16[1024,1792]{1,0:T(8,128)(2,1)} %get-tuple-element.39, bf16[1024,1792]{1,0:T(8,128)(2,1)S(1)} %get-tuple-element.38), kind=kOutput, calls=%fused_computation.387 | convolution fusion | flops 18807783424 | bytes 41418752 | tf_op jit(solution)/shard_map/dot_general | solution.py:47
  482.0 16.5 %fusion.174 = (bf16[1024,2560]{1,0:T(8,128)(2,1)}, f32[1024,2560]{1,0:T(8,128)}) fusion(bf16[1024,1792]{1,0:T(8,128)(2,1)} %get-tuple-element.41, bf16[2560,1792]{1,0:T(8,128)(2,1)} %all-gather.13.cloned.1.call-done), kind=kOutput, calls=%fused_computation.386 | convolution fusion | flops 9397862400 | bytes 28573696 | tf_op jit(solution)/shard_map/dot_general | solution.py:47
  506.4 11.7 collective-permute-done.17
  521.3 25.4 %collective-permute-done.26 = bf16[256,2560]{1,0:T(8,128)(2,1)S(1)} collective-permute-done((bf16[256,2560]{1,0:T(8,128)(2,1)S(1)}, bf16[256,2560]{1,0:T(8,128)(2,1)S(1)}, u32[]{:S(2)}, u32[]{:S(2)}) %collective-permute-start.26) | collective-permute-done | bytes 1310752 | tf_op jit(solution)/shard_map/ppermute | solution.py:78
  546.7 26.5 %collective-permute-done.18 = bf16[256,2560]{1,0:T(8,128)(2,1)S(1)} collective-permute-done((bf16[256,2560]{1,0:T(8,128)(2,1)S(1)}, bf16[256,2560]{1,0:T(8,128)(2,1)S(1)}, u32[]{:S(2)}, u32[]{:S(2)}) %collective-permute-start.18) | collective-permute-done | bytes 1310752 | tf_op jit(solution)/shard_map/ppermute | solution.py:78
  581.6 27.1 %collective-permute-done.28 = bf16[256,2560]{1,0:T(8,128)(2,1)S(1)} collective-permute-done((bf16[256,2560]{1,0:T(8,128)(2,1)S(1)}, bf16[256,2560]{1,0:T(8,128)(2,1)S(1)}, u32[]{:S(2)}, u32[]{:S(2)}) %collective-permute-start.28) | collective-permute-done | bytes 1310752 | tf_op jit(solution)/shard_map/ppermute | solution.py:78
  611.5 12.8 collective-permute-done.29
  634.4 5.0 fusion.81
  639.4 6.6 multiply_reduce_fusion
  667.4 6.8 multiply_convert_fusion
  678.1 6.8 multiply_convert_fusion.1
  688.8 6.7 multiply_convert_fusion.2
  699.4 6.7 multiply_convert_fusion.3
  709.9 7.7 maximum_bitcast_fusion.1
  721.5 8.9 convolution_convert_fusion.3
  730.5 15.0 %convolution_convert_fusion.1 = bf16[2560,1792]{1,0:T(8,128)(2,1)} fusion(bf16[1024,2560]{1,0:T(8,128)(2,1)} %copy-done.52, bf16[1024,1792]{1,0:T(8,128)(2,1)} %get-tuple-element.41), kind=kOutput, calls=%fused_computation.3 | convolution fusion | flops 9399828480 | bytes 18087936 | tf_op jit(solution)/shard_map/dot_general | solution.py:53
  773.4 7.8 fusion.176
  784.4 13.4 %collective-permute-done.33 = bf16[128,2560]{1,0:T(8,128)(2,1)S(1)} collective-permute-done((bf16[128,2560]{1,0:T(8,128)(2,1)S(1)}, bf16[128,2560]{1,0:T(8,128)(2,1)S(1)}, u32[]{:S(2)}, u32[]{:S(2)}) %collective-permute-start.33) | collective-permute-done | bytes 655392 | tf_op jit(solution)/shard_map/ppermute | solution.py:78
  801.7 27.0 %collective-permute-done.34 = bf16[256,2560]{1,0:T(8,128)(2,1)S(1)} collective-permute-done((bf16[256,2560]{1,0:T(8,128)(2,1)S(1)}, bf16[256,2560]{1,0:T(8,128)(2,1)S(1)}, u32[]{:S(2)}, u32[]{:S(2)}) %collective-permute-start.34) | collective-permute-done | bytes 1310752 | tf_op jit(solution)/shard_map/ppermute | solution.py:78
  833.9 10.0 convolution_convert_fusion.2
  844.0 27.1 %convolution_convert_fusion = bf16[2560,3584]{1,0:T(8,128)(2,1)} fusion(bf16[1024,2560]{1,0:T(8,128)(2,1)} %constant_dynamic-update-slice_fusion.5, bf16[1024,1792]{1,0:T(8,128)(2,1)} %get-tuple-element.39, bf16[1024,1792]{1,0:T(8,128)(2,1)} %copy-done.75), kind=kOutput, calls=%fused_computation | convolution fusion | flops 18814337024 | bytes 30932992 | tf_op jit(solution)/shard_map/dot_general | solution.py:53
  886.9 11.3 psum.7
  898.2 5.4 fusion.33
  903.6 9.1 reduce-scatter.17.cloned.1.call-done
  921.0 128.5 %reduce-scatter.19.cloned.1.call-done = f32[80,2]{1,0:T(8,128)} async-done(((f32[2560,2]{1,0:T(8,128)}), f32[80,2]{1,0:T(8,128)}) %reduce-scatter.19.cloned.1.call-update) | async-done | bytes 656
  1051.9 55.7 %reduce-scatter.11.cloned.1.call-done = bf16[320,960]{1,0:T(8,128)(2,1)} async-done(((bf16[2560,960]{1,0:T(8,128)(2,1)}), bf16[320,960]{1,0:T(8,128)(2,1)}) %reduce-scatter.11.cloned.1.call-update) | async-done | bytes 614416 | tf_op jit(solution)/shard_map/reduce_scatter | solution.py:316
  1124.1 167.2 %reduce-scatter.15.cloned.1.call-done = bf16[320,3584]{1,0:T(8,128)(2,1)} async-done(((bf16[2560,3584]{1,0:T(8,128)(2,1)}), bf16[320,3584]{1,0:T(8,128)(2,1)}) %reduce-scatter.15.cloned.1.call-update) | async-done | bytes 2293776 | tf_op jit(solution)/shard_map/reduce_scatter | solution.py:316
  1302.0 9.6 collective-permute-done.46
  1311.6 13.8 %collective-permute-done.45 = bf16[80,3584]{1,0:T(8,128)(2,1)S(1)} collective-permute-done((bf16[80,3584]{1,0:T(8,128)(2,1)S(1)}, bf16[80,3584]{1,0:T(8,128)(2,1)S(1)}, u32[]{:S(2)}, u32[]{:S(2)}) %collective-permute-start.45) | collective-permute-done | bytes 573472 | tf_op jit(solution)/shard_map/ppermute | solution.py:331
  (489 shorter events, 307.0 us)
Async XLA Ops:
  7.2 63.3 %all-gather.7.cloned.1.call-start = ((), (), s32[]{:S(2)}) async-start(), calls=%async_computation.6 | async-start | bytes 5898240 | tf_op jit(solution)/shard_map/all_gather | solution.py:141
  11.6 124.6 %all-gather.15.cloned.1.call-start = ((), (), s32[]{:S(2)}) async-start(), calls=%async_computation.15 | async-start | bytes 3276800 | tf_op jit(solution)/shard_map/all_gather | solution.py:169
  11.7 21.6 %collective-permute-start.6 = (s32[258]{0:T(512)S(1)}, s32[258]{0:T(512)S(1)}, u32[]{:S(2)}, u32[]{:S(2)}) collective-permute-start(s32[258]{0:T(512)S(1)} %pad_add_fusion.3), channel_id=1, source_target_pairs={{0,6},{2,4},{4,2},{6,0},{1,7},{3,5},{5,3},{7,1},{8,14},{10,12},{12... | collective-permute-start | bytes 3104 | tf_op jit(solution)/shard_map/ppermute | solution.py:78
  15.6 17.7 %collective-permute-start.5 = (s32[258]{0:T(512)S(1)}, s32[258]{0:T(512)S(1)}, u32[]{:S(2)}, u32[]{:S(2)}) collective-permute-start(s32[258]{0:T(512)S(1)} %pad_add_fusion.3), channel_id=1, source_target_pairs={{0,4},{2,6},{4,0},{6,2},{1,5},{3,7},{5,1},{7,3},{8,12},{10,14},{12... | collective-permute-start | bytes 3104 | tf_op jit(solution)/shard_map/ppermute | solution.py:78
  16.2 17.2 %collective-permute-start.4 = (s32[258]{0:T(512)S(1)}, s32[258]{0:T(512)S(1)}, u32[]{:S(2)}, u32[]{:S(2)}) collective-permute-start(s32[258]{0:T(512)S(1)} %pad_add_fusion.3), channel_id=1, source_target_pairs={{0,2},{2,0},{4,6},{6,4},{1,3},{3,1},{5,7},{7,5},{8,10},{10,8},{12,... | collective-permute-start | bytes 3104 | tf_op jit(solution)/shard_map/ppermute | solution.py:78
  16.2 30.0 %collective-permute-start = (bf16[256,2560]{1,0:T(8,128)(2,1)S(1)}, bf16[256,2560]{1,0:T(8,128)(2,1)S(1)}, u32[]{:S(2)}, u32[]{:S(2)}) collective-permute-start(bf16[256,2560]{1,0:T(8,128)(2,1)S(1)} %bitcast.429), channel_id=1, source_target_pairs={{0,2},{2,0},{4,6},{6,4},{1,3},{3,1},{5,7},{7,5},{8,10},{10,8},{12,... | collective-permute-start | bytes 3932168 | tf_op jit(solution)/shard_map/ppermute | solution.py:78
  18.2 29.8 %collective-permute-start.1 = (bf16[256,2560]{1,0:T(8,128)(2,1)S(1)}, bf16[256,2560]{1,0:T(8,128)(2,1)S(1)}, u32[]{:S(2)}, u32[]{:S(2)}) collective-permute-start(bf16[256,2560]{1,0:T(8,128)(2,1)S(1)} %bitcast.430), channel_id=1, source_target_pairs={{0,4},{2,6},{4,0},{6,2},{1,5},{3,7},{5,1},{7,3},{8,12},{10,14},{12... | collective-permute-start | bytes 3932168 | tf_op jit(solution)/shard_map/ppermute | solution.py:78
  82.6 108.8 %all-gather.9.cloned.1.call-start = ((), (), s32[]{:S(2)}) async-start(), calls=%async_computation.7 | async-start | bytes 3686400 | tf_op jit(solution)/shard_map/all_gather | solution.py:141
  84.4 257.2 %all-gather.11.cloned.1.call-start = ((), (), s32[]{:S(2)}) async-start(), calls=%async_computation.8 | async-start | bytes 20643840 | tf_op jit(solution)/shard_map/all_gather | solution.py:141
  87.7 342.2 %all-gather.13.cloned.1.call-start = ((), (), s32[]{:S(2)}) async-start(), calls=%async_computation.9 | async-start | bytes 10321920 | tf_op jit(solution)/shard_map/all_gather | solution.py:141
  90.2 680.6 %reduce-scatter.9.cloned.1.call-start = ((), (), s32[]{:S(2)}) async-start(), calls=%async_computation.10 | async-start | bytes 3276800 | tf_op jit(solution)/shard_map/reduce_scatter | solution.py:292
  198.3 17.7 %collective-permute-start.9 = (bf16[128,2560]{1,0:T(8,128)(2,1)S(1)}, bf16[128,2560]{1,0:T(8,128)(2,1)S(1)}, u32[]{:S(2)}, u32[]{:S(2)}) collective-permute-start(bf16[128,2560]{1,0:T(8,128)(2,1)S(1)} %get-tuple-element.64), channel_id=1, source_target_pairs={{0,2},{2,0},{4,6},{6,4},{1,3},{3,1},{5,7},{7,5},{8,10},{10,8},{12,... | collective-permute-start | bytes 1966088 | tf_op jit(solution)/shard_map/ppermute | solution.py:78
  199.9 17.7 %collective-permute-start.7 = (bf16[128,2560]{1,0:T(8,128)(2,1)S(1)}, bf16[128,2560]{1,0:T(8,128)(2,1)S(1)}, u32[]{:S(2)}, u32[]{:S(2)}) collective-permute-start(bf16[128,2560]{1,0:T(8,128)(2,1)S(1)} %get-tuple-element.65), channel_id=1, source_target_pairs={{0,4},{2,6},{4,0},{6,2},{1,5},{3,7},{5,1},{7,3},{8,12},{10,14},{12... | collective-permute-start | bytes 1966088 | tf_op jit(solution)/shard_map/ppermute | solution.py:78
  201.3 42.8 %collective-permute-start.19 = (bf16[256,2560]{1,0:T(8,128)(2,1)S(1)}, bf16[256,2560]{1,0:T(8,128)(2,1)S(1)}, u32[]{:S(2)}, u32[]{:S(2)}) collective-permute-start(bf16[256,2560]{1,0:T(8,128)(2,1)S(1)} %bitcast.445), channel_id=1, source_target_pairs={{0,2},{2,0},{4,6},{6,4},{1,3},{3,1},{5,7},{7,5},{8,10},{10,8},{12,... | collective-permute-start | bytes 3932168 | tf_op jit(solution)/shard_map/ppermute | solution.py:78
  201.9 43.8 %collective-permute-start.20 = (bf16[256,2560]{1,0:T(8,128)(2,1)S(1)}, bf16[256,2560]{1,0:T(8,128)(2,1)S(1)}, u32[]{:S(2)}, u32[]{:S(2)}) collective-permute-start(bf16[256,2560]{1,0:T(8,128)(2,1)S(1)} %bitcast.446), channel_id=1, source_target_pairs={{0,4},{2,6},{4,0},{6,2},{1,5},{3,7},{5,1},{7,3},{8,12},{10,14},{12... | collective-permute-start | bytes 3932168 | tf_op jit(solution)/shard_map/ppermute | solution.py:78
  218.0 55.7 %collective-permute-start.10 = (bf16[256,2560]{1,0:T(8,128)(2,1)S(1)}, bf16[256,2560]{1,0:T(8,128)(2,1)S(1)}, u32[]{:S(2)}, u32[]{:S(2)}) collective-permute-start(bf16[256,2560]{1,0:T(8,128)(2,1)S(1)} %pad_maximum_fusion.8), channel_id=1, source_target_pairs={{0,4},{2,6},{4,0},{6,2},{1,5},{3,7},{5,1},{7,3},{8,12},{10,14},{12... | collective-permute-start | bytes 3932168 | tf_op jit(solution)/shard_map/ppermute | solution.py:78
  219.6 54.1 %collective-permute-start.8 = (bf16[256,2560]{1,0:T(8,128)(2,1)S(1)}, bf16[256,2560]{1,0:T(8,128)(2,1)S(1)}, u32[]{:S(2)}, u32[]{:S(2)}) collective-permute-start(bf16[256,2560]{1,0:T(8,128)(2,1)S(1)} %pad_maximum_fusion.7), channel_id=1, source_target_pairs={{0,2},{2,0},{4,6},{6,4},{1,3},{3,1},{5,7},{7,5},{8,10},{10,8},{12,... | collective-permute-start | bytes 3932168 | tf_op jit(solution)/shard_map/ppermute | solution.py:78
  244.1 43.7 %collective-permute-start.21 = (bf16[128,2560]{1,0:T(8,128)(2,1)S(1)}, bf16[128,2560]{1,0:T(8,128)(2,1)S(1)}, u32[]{:S(2)}, u32[]{:S(2)}) collective-permute-start(bf16[128,2560]{1,0:T(8,128)(2,1)S(1)} %slice.631), channel_id=1, source_target_pairs={{0,4},{2,6},{4,0},{6,2},{1,5},{3,7},{5,1},{7,3},{8,12},{10,14},{12... | collective-permute-start | bytes 1966088 | tf_op jit(solution)/shard_map/ppermute | solution.py:78
  245.7 42.1 %collective-permute-start.22 = (bf16[128,2560]{1,0:T(8,128)(2,1)S(1)}, bf16[128,2560]{1,0:T(8,128)(2,1)S(1)}, u32[]{:S(2)}, u32[]{:S(2)}) collective-permute-start(bf16[128,2560]{1,0:T(8,128)(2,1)S(1)} %slice.632), channel_id=1, source_target_pairs={{0,2},{2,0},{4,6},{6,4},{1,3},{3,1},{5,7},{7,5},{8,10},{10,8},{12,... | collective-permute-start | bytes 1966088 | tf_op jit(solution)/shard_map/ppermute | solution.py:78
  276.9 37.4 %collective-permute-start.12 = (bf16[256,2560]{1,0:T(8,128)(2,1)S(1)}, bf16[256,2560]{1,0:T(8,128)(2,1)S(1)}, u32[]{:S(2)}, u32[]{:S(2)}) collective-permute-start(bf16[256,2560]{1,0:T(8,128)(2,1)S(1)} %get-tuple-element.27), channel_id=1, source_target_pairs={{0,4},{2,6},{4,0},{6,2},{1,5},{3,7},{5,1},{7,3},{8,12},{10,14},{12... | collective-permute-start | bytes 3932168 | tf_op jit(solution)/shard_map/ppermute | solution.py:78
  278.3 36.7 %collective-permute-start.11 = (bf16[256,2560]{1,0:T(8,128)(2,1)S(1)}, bf16[256,2560]{1,0:T(8,128)(2,1)S(1)}, u32[]{:S(2)}, u32[]{:S(2)}) collective-permute-start(bf16[256,2560]{1,0:T(8,128)(2,1)S(1)} %get-tuple-element.27), channel_id=1, source_target_pairs={{0,2},{2,0},{4,6},{6,4},{1,3},{3,1},{5,7},{7,5},{8,10},{10,8},{12,... | collective-permute-start | bytes 3932168 | tf_op jit(solution)/shard_map/ppermute | solution.py:78
  314.3 16.8 %collective-permute-start.14 = (bf16[128,2560]{1,0:T(8,128)(2,1)S(1)}, bf16[128,2560]{1,0:T(8,128)(2,1)S(1)}, u32[]{:S(2)}, u32[]{:S(2)}) collective-permute-start(bf16[128,2560]{1,0:T(8,128)(2,1)S(1)} %slice.621), channel_id=1, source_target_pairs={{0,2},{2,0},{4,6},{6,4},{1,3},{3,1},{5,7},{7,5},{8,10},{10,8},{12,... | collective-permute-start | bytes 1966088 | tf_op jit(solution)/shard_map/ppermute | solution.py:78
  479.0 22.5 %collective-permute-start.25 = (bf16[128,2560]{1,0:T(8,128)(2,1)}, bf16[128,2560]{1,0:T(8,128)(2,1)S(1)}, u32[]{:S(2)}, u32[]{:S(2)}) collective-permute-start(bf16[128,2560]{1,0:T(8,128)(2,1)} %get-tuple-element.56), channel_id=1, source_target_pairs={{0,2},{2,0},{4,6},{6,4},{1,3},{3,1},{5,7},{7,5},{8,10},{10,8},{12,... | collective-permute-start | bytes 1966088 | tf_op jit(solution)/shard_map/ppermute | solution.py:78
  480.5 21.0 %collective-permute-start.23 = (bf16[128,2560]{1,0:T(8,128)(2,1)S(1)}, bf16[128,2560]{1,0:T(8,128)(2,1)}, u32[]{:S(2)}, u32[]{:S(2)}) collective-permute-start(bf16[128,2560]{1,0:T(8,128)(2,1)S(1)} %get-tuple-element.57), channel_id=1, source_target_pairs={{0,4},{2,6},{4,0},{6,2},{1,5},{3,7},{5,1},{7,3},{8,12},{10,14},{12... | collective-permute-start | bytes 1966088 | tf_op jit(solution)/shard_map/ppermute | solution.py:78
  500.3 17.7 %collective-permute-start.17 = (bf16[128,2560]{1,0:T(8,128)(2,1)S(1)}, bf16[128,2560]{1,0:T(8,128)(2,1)S(1)}, u32[]{:S(2)}, u32[]{:S(2)}) collective-permute-start(bf16[128,2560]{1,0:T(8,128)(2,1)S(1)} %get-tuple-element.60), channel_id=1, source_target_pairs={{0,2},{2,0},{4,6},{6,4},{1,3},{3,1},{5,7},{7,5},{8,10},{10,8},{12,... | collective-permute-start | bytes 1966088 | tf_op jit(solution)/shard_map/ppermute | solution.py:78
  501.0 17.7 %collective-permute-start.15 = (bf16[128,2560]{1,0:T(8,128)(2,1)S(1)}, bf16[128,2560]{1,0:T(8,128)(2,1)S(1)}, u32[]{:S(2)}, u32[]{:S(2)}) collective-permute-start(bf16[128,2560]{1,0:T(8,128)(2,1)S(1)} %get-tuple-element.61), channel_id=1, source_target_pairs={{0,4},{2,6},{4,0},{6,2},{1,5},{3,7},{5,1},{7,3},{8,12},{10,14},{12... | collective-permute-start | bytes 1966088 | tf_op jit(solution)/shard_map/ppermute | solution.py:78
  503.2 43.5 %collective-permute-start.26 = (bf16[256,2560]{1,0:T(8,128)(2,1)S(1)}, bf16[256,2560]{1,0:T(8,128)(2,1)S(1)}, u32[]{:S(2)}, u32[]{:S(2)}) collective-permute-start(bf16[256,2560]{1,0:T(8,128)(2,1)S(1)} %pad_maximum_fusion.12), channel_id=1, source_target_pairs={{0,4},{2,6},{4,0},{6,2},{1,5},{3,7},{5,1},{7,3},{8,12},{10,14},{12... | collective-permute-start | bytes 3932168 | tf_op jit(solution)/shard_map/ppermute | solution.py:78
  504.8 41.9 %collective-permute-start.24 = (bf16[256,2560]{1,0:T(8,128)(2,1)S(1)}, bf16[256,2560]{1,0:T(8,128)(2,1)S(1)}, u32[]{:S(2)}, u32[]{:S(2)}) collective-permute-start(bf16[256,2560]{1,0:T(8,128)(2,1)S(1)} %pad_maximum_fusion.11), channel_id=1, source_target_pairs={{0,2},{2,0},{4,6},{6,4},{1,3},{3,1},{5,7},{7,5},{8,10},{10,8},{12,... | collective-permute-start | bytes 3932168 | tf_op jit(solution)/shard_map/ppermute | solution.py:78
  519.1 54.1 %collective-permute-start.18 = (bf16[256,2560]{1,0:T(8,128)(2,1)S(1)}, bf16[256,2560]{1,0:T(8,128)(2,1)S(1)}, u32[]{:S(2)}, u32[]{:S(2)}) collective-permute-start(bf16[256,2560]{1,0:T(8,128)(2,1)S(1)} %pad_maximum_fusion.10), channel_id=1, source_target_pairs={{0,4},{2,6},{4,0},{6,2},{1,5},{3,7},{5,1},{7,3},{8,12},{10,14},{12... | collective-permute-start | bytes 3932168 | tf_op jit(solution)/shard_map/ppermute | solution.py:78
  519.8 53.4 %collective-permute-start.16 = (bf16[256,2560]{1,0:T(8,128)(2,1)S(1)}, bf16[256,2560]{1,0:T(8,128)(2,1)S(1)}, u32[]{:S(2)}, u32[]{:S(2)}) collective-permute-start(bf16[256,2560]{1,0:T(8,128)(2,1)S(1)} %pad_maximum_fusion.9), channel_id=1, source_target_pairs={{0,2},{2,0},{4,6},{6,4},{1,3},{3,1},{5,7},{7,5},{8,10},{10,8},{12,... | collective-permute-start | bytes 3932168 | tf_op jit(solution)/shard_map/ppermute | solution.py:78
  579.4 29.2 %collective-permute-start.28 = (bf16[256,2560]{1,0:T(8,128)(2,1)S(1)}, bf16[256,2560]{1,0:T(8,128)(2,1)S(1)}, u32[]{:S(2)}, u32[]{:S(2)}) collective-permute-start(bf16[256,2560]{1,0:T(8,128)(2,1)S(1)} %get-tuple-element.24), channel_id=1, source_target_pairs={{0,4},{2,6},{4,0},{6,2},{1,5},{3,7},{5,1},{7,3},{8,12},{10,14},{12... | collective-permute-start | bytes 3932168 | tf_op jit(solution)/shard_map/ppermute | solution.py:78
  579.9 30.2 %collective-permute-start.27 = (bf16[256,2560]{1,0:T(8,128)(2,1)S(1)}, bf16[256,2560]{1,0:T(8,128)(2,1)S(1)}, u32[]{:S(2)}, u32[]{:S(2)}) collective-permute-start(bf16[256,2560]{1,0:T(8,128)(2,1)S(1)} %get-tuple-element.24), channel_id=1, source_target_pairs={{0,2},{2,0},{4,6},{6,4},{1,3},{3,1},{5,7},{7,5},{8,10},{10,8},{12,... | collective-permute-start | bytes 3932168 | tf_op jit(solution)/shard_map/ppermute | solution.py:78
  721.4 149.8 %reduce-scatter.13.cloned.1.call-start = ((), (), s32[]{:S(2)}) async-start(), calls=%async_computation.12 | async-start | bytes 3686400 | tf_op jit(solution)/shard_map/reduce_scatter | solution.py:316
  730.4 182.4 %reduce-scatter.17.cloned.1.call-start = ((), (), s32[]{:S(2)}) async-start(), calls=%async_computation.14 | async-start | bytes 10321920 | tf_op jit(solution)/shard_map/reduce_scatter | solution.py:316
  745.4 304.0 %reduce-scatter.19.cloned.1.call-start = ((), (), s32[]{:S(2)}) async-start(), calls=%async_computation.16 | async-start | bytes 1351680
  781.4 16.4 %collective-permute-start.33 = (bf16[128,2560]{1,0:T(8,128)(2,1)S(1)}, bf16[128,2560]{1,0:T(8,128)(2,1)S(1)}, u32[]{:S(2)}, u32[]{:S(2)}) collective-permute-start(bf16[128,2560]{1,0:T(8,128)(2,1)S(1)} %get-tuple-element.52), channel_id=1, source_target_pairs={{0,2},{2,0},{4,6},{6,4},{1,3},{3,1},{5,7},{7,5},{8,10},{10,8},{12,... | collective-permute-start | bytes 1966088 | tf_op jit(solution)/shard_map/ppermute | solution.py:78
  782.9 16.0 %collective-permute-start.31 = (bf16[128,2560]{1,0:T(8,128)(2,1)S(1)}, bf16[128,2560]{1,0:T(8,128)(2,1)S(1)}, u32[]{:S(2)}, u32[]{:S(2)}) collective-permute-start(bf16[128,2560]{1,0:T(8,128)(2,1)S(1)} %get-tuple-element.53), channel_id=1, source_target_pairs={{0,4},{2,6},{4,0},{6,2},{1,5},{3,7},{5,1},{7,3},{8,12},{10,14},{12... | collective-permute-start | bytes 1966088 | tf_op jit(solution)/shard_map/ppermute | solution.py:78
  799.4 29.3 %collective-permute-start.34 = (bf16[256,2560]{1,0:T(8,128)(2,1)S(1)}, bf16[256,2560]{1,0:T(8,128)(2,1)S(1)}, u32[]{:S(2)}, u32[]{:S(2)}) collective-permute-start(bf16[256,2560]{1,0:T(8,128)(2,1)S(1)} %pad_maximum_fusion.14), channel_id=1, source_target_pairs={{0,4},{2,6},{4,0},{6,2},{1,5},{3,7},{5,1},{7,3},{8,12},{10,14},{12... | collective-permute-start | bytes 3932168 | tf_op jit(solution)/shard_map/ppermute | solution.py:78
  801.0 29.0 %collective-permute-start.32 = (bf16[256,2560]{1,0:T(8,128)(2,1)S(1)}, bf16[256,2560]{1,0:T(8,128)(2,1)S(1)}, u32[]{:S(2)}, u32[]{:S(2)}) collective-permute-start(bf16[256,2560]{1,0:T(8,128)(2,1)S(1)} %pad_maximum_fusion.13), channel_id=1, source_target_pairs={{0,2},{2,0},{4,6},{6,4},{1,3},{3,1},{5,7},{7,5},{8,10},{10,8},{12,... | collective-permute-start | bytes 3932168 | tf_op jit(solution)/shard_map/ppermute | solution.py:78
  833.9 273.7 %reduce-scatter.11.cloned.1.call-start = ((), (), s32[]{:S(2)}) async-start(), calls=%async_computation.11 | async-start | bytes 5898240 | tf_op jit(solution)/shard_map/reduce_scatter | solution.py:316
  844.0 447.3 %reduce-scatter.15.cloned.1.call-start = ((), (), s32[]{:S(2)}) async-start(), calls=%async_computation.13 | async-start | bytes 20643840 | tf_op jit(solution)/shard_map/reduce_scatter | solution.py:316
  914.1 137.5 %collective-permute-start.47 = (bf16[80,1792]{1,0:T(8,128)(2,1)S(1)}, bf16[80,1792]{1,0:T(8,128)(2,1)S(1)}, u32[]{:S(2)}, u32[]{:S(2)}) collective-permute-start(bf16[80,1792]{1,0:T(8,128)(2,1)S(1)} %get-tuple-element.91), channel_id=1, source_target_pairs={{0,0},{1,4},{2,1},{3,5},{4,2},{5,6},{6,3},{7,7},{8,8},{9,12},{10,9... | collective-permute-start | bytes 860168 | tf_op jit(solution)/shard_map/ppermute | solution.py:331
  914.7 136.8 %collective-permute-start.50 = (bf16[80,1792]{1,0:T(8,128)(2,1)S(1)}, bf16[80,1792]{1,0:T(8,128)(2,1)S(1)}, u32[]{:S(2)}, u32[]{:S(2)}) collective-permute-start(bf16[80,1792]{1,0:T(8,128)(2,1)S(1)} %get-tuple-element.92), channel_id=1, source_target_pairs={{0,3},{1,7},{2,2},{3,6},{4,1},{5,5},{6,0},{7,4},{8,11},{9,15},{10,... | collective-permute-start | bytes 860168 | tf_op jit(solution)/shard_map/ppermute | solution.py:331
  917.9 133.7 %collective-permute-start.49 = (bf16[80,1792]{1,0:T(8,128)(2,1)S(1)}, bf16[80,1792]{1,0:T(8,128)(2,1)S(1)}, u32[]{:S(2)}, u32[]{:S(2)}) collective-permute-start(bf16[80,1792]{1,0:T(8,128)(2,1)S(1)} %get-tuple-element.93), channel_id=1, source_target_pairs={{0,2},{1,6},{2,3},{3,7},{4,0},{5,4},{6,1},{7,5},{8,10},{9,14},{10,... | collective-permute-start | bytes 860168 | tf_op jit(solution)/shard_map/ppermute | solution.py:331
  918.2 133.4 %collective-permute-start.48 = (bf16[80,1792]{1,0:T(8,128)(2,1)S(1)}, bf16[80,1792]{1,0:T(8,128)(2,1)S(1)}, u32[]{:S(2)}, u32[]{:S(2)}) collective-permute-start(bf16[80,1792]{1,0:T(8,128)(2,1)S(1)} %get-tuple-element.94), channel_id=1, source_target_pairs={{0,1},{1,5},{2,0},{3,4},{4,3},{5,7},{6,2},{7,6},{8,9},{9,13},{10,8... | collective-permute-start | bytes 860168 | tf_op jit(solution)/shard_map/ppermute | solution.py:331
  1293.7 17.8 %collective-permute-start.46 = (bf16[80,3584]{1,0:T(8,128)(2,1)S(1)}, bf16[80,3584]{1,0:T(8,128)(2,1)S(1)}, u32[]{:S(2)}, u32[]{:S(2)}) collective-permute-start(bf16[80,3584]{1,0:T(8,128)(2,1)S(1)} %get-tuple-element.83), channel_id=1, source_target_pairs={{0,3},{1,7},{2,2},{3,6},{4,1},{5,5},{6,0},{7,4},{8,11},{9,15},{10,... | collective-permute-start | bytes 1720328 | tf_op jit(solution)/shard_map/ppermute | solution.py:331
  1296.8 28.5 %collective-permute-start.45 = (bf16[80,3584]{1,0:T(8,128)(2,1)S(1)}, bf16[80,3584]{1,0:T(8,128)(2,1)S(1)}, u32[]{:S(2)}, u32[]{:S(2)}) collective-permute-start(bf16[80,3584]{1,0:T(8,128)(2,1)S(1)} %get-tuple-element.84), channel_id=1, source_target_pairs={{0,2},{1,6},{2,3},{3,7},{4,0},{5,4},{6,1},{7,5},{8,10},{9,14},{10,... | collective-permute-start | bytes 1720328 | tf_op jit(solution)/shard_map/ppermute | solution.py:331
  1297.2 28.1 %collective-permute-start.44 = (bf16[80,3584]{1,0:T(8,128)(2,1)S(1)}, bf16[80,3584]{1,0:T(8,128)(2,1)S(1)}, u32[]{:S(2)}, u32[]{:S(2)}) collective-permute-start(bf16[80,3584]{1,0:T(8,128)(2,1)S(1)} %get-tuple-element.85), channel_id=1, source_target_pairs={{0,1},{1,5},{2,0},{3,4},{4,3},{5,7},{6,2},{7,6},{8,9},{9,13},{10,8... | collective-permute-start | bytes 1720328 | tf_op jit(solution)/shard_map/ppermute | solution.py:331
  (98 other events, 968.1 us)
Sparse Core Ops, SparseCore 0:
  11.7 58.7 all-gather.6
  82.7 53.4 all-gather.14
  138.5 38.1 all-gather.8
  178.7 162.8 all-gather.10
  343.1 86.7 all-gather.12
  721.5 49.2 reduce-scatter.8
  773.1 41.0 reduce-scatter.12
  816.6 96.1 reduce-scatter.16
  915.7 133.7 reduce-scatter.18
  1051.6 55.8 reduce-scatter.10
  1109.9 181.3 reduce-scatter.14

commit v2 on v1

v2 whole, which is shorter than its diff:
```python
import numpy as np

import jax
import jax.numpy as jnp
from jax import lax
from jax.experimental import pallas as pl
from jax.experimental.pallas import tpu as pltpu
from jax.experimental.layout import Layout, with_layout_constraint
from jax.sharding import Mesh, PartitionSpec as P

HEADS = 32
KV_HEADS = 8
HEAD_DIM = 80
PIECE = 256

epsilon = 1e-05
rope_base = 1000000.0

CHIPS = 4
SUM_AXES = ("group", "core", "dp")
REPLICA = ("dp", "chip", "core")


HALF = HEAD_DIM // 2
LOG2E = 1.4426950408889634


def rope_tables(places):
    frequency = rope_base ** (-(jnp.arange(HALF, dtype=jnp.float32) * 2.0 / HEAD_DIM))
    angles = frequency[:, None] * places.astype(jnp.float32)[None, :]
    return (jnp.cos(angles), jnp.sin(angles))


def rotate(values, cosine, sine):
    first, second = halves_of(values)
    return joined(first * cosine - second * sine, second * cosine + first * sine)


def unrotate(grads, cosine, sine):
    first, second = halves_of(grads)
    return joined(first * cosine + second * sine, second * cosine - first * sine)


def halves_of(values):
    heads = values.reshape(-1, 2, HALF, values.shape[-1])
    return heads[:, 0], heads[:, 1]


def joined(first, second):
    return jnp.stack([first, second], axis=1).reshape(-1, first.shape[-1])


def flipped(values):
    return values.astype(jnp.float32).T.astype(jnp.bfloat16)


def attend_kernel(repeats, query_ref, kv_ref, limit_ref, mixed_ref, total_ref, out_ref):
    groups, kv_rows, block = kv_ref.shape
    kv_width = kv_rows // 2
    factor = HEAD_DIM ** (-0.5) * LOG2E
    key_at = lax.broadcasted_iota(jnp.int32, (block, block), 0)
    limits = limit_ref[0]
    for kv in range(kv_width // HEAD_DIM):
        rows = slice(kv * HEAD_DIM, (kv + 1) * HEAD_DIM)
        value_rows = slice(kv_width + kv * HEAD_DIM, kv_width + (kv + 1) * HEAD_DIM)
        keys = [flipped(kv_ref[group, rows, :]) for group in range(groups)]
        for head in range(kv * repeats, (kv + 1) * repeats):
            head_rows = slice(head * HEAD_DIM, (head + 1) * HEAD_DIM)
            query = query_ref[head_rows, :]
            scores = []
            for group in range(groups):
                raw = jnp.dot(keys[group], query, preferred_element_type=jnp.float32)
                scores.append(jnp.where(key_at < limits - group * block, raw, -1e30))
            highest = scores[0]
            for group in range(1, groups):
                highest = jnp.maximum(highest, scores[group])
            highest = jnp.max(highest, axis=0, keepdims=True) * factor
            row_sum, mixed = None, None
            for group in range(groups):
                raised = jnp.exp2(scores[group] * factor - highest)
                part_sum = jnp.sum(raised, axis=0, keepdims=True)
                part = jnp.dot(
                    kv_ref[group, value_rows, :],
                    raised.astype(jnp.bfloat16),
                    preferred_element_type=jnp.float32,
                )
                row_sum = part_sum if row_sum is None else row_sum + part_sum
                mixed = part if mixed is None else mixed + part
            out_ref[head_rows, :] = mixed / row_sum
            total_ref[0, head : head + 1, :] = highest + jnp.log2(row_sum)
    mixed_ref[...] = out_ref[...].T.astype(jnp.bfloat16)


def attend(query, kv_all, limits, repeats):
    query_width, tokens = query.shape
    groups, kv_rows, _ = kv_all.shape
    chips, _, block = limits.shape
    heads = query_width // HEAD_DIM
    pairs = query_width * tokens * groups * block
    return pl.pallas_call(
        lambda *refs: attend_kernel(repeats, *refs),
        out_shape=(
            jax.ShapeDtypeStruct((tokens, query_width), jnp.bfloat16),
            jax.ShapeDtypeStruct((chips, heads, block), jnp.float32),
        ),
        grid=(chips,),
        in_specs=[
            pl.BlockSpec((query_width, block), lambda i: (0, i)),
            pl.BlockSpec((groups, kv_rows, block), lambda i: (0, 0, i)),
            pl.BlockSpec((1, 1, block), lambda i: (i, 0, 0)),
        ],
        out_specs=(
            pl.BlockSpec((block, query_width), lambda i: (i, 0)),
            pl.BlockSpec((1, heads, block), lambda i: (i, 0, 0)),
        ),
        scratch_shapes=[pltpu.VMEM((query_width, block), jnp.float32)],
        cost_estimate=pl.CostEstimate(
            flops=4 * pairs,
            bytes_accessed=2 * (2 * query.size + kv_all.size),
            transcendentals=pairs // HEAD_DIM,
        ),
        name="attend",
    )(query, kv_all, limits)


def attend_back_kernel(
    repeats,
    query_ref,
    kv_ref,
    limit_ref,
    total_ref,
    mixed_ref,
    grad_ref,
    cosine_ref,
    sine_ref,
    grad_query_ref,
    grad_kv_ref,
    grad_rows_ref,
    mixed_rows_ref,
    query_rows_ref,
    key_sum_ref,
    value_sum_ref,
):
    groups, kv_rows, block = kv_ref.shape
    kv_width = kv_rows // 2
    scaling = HEAD_DIM ** (-0.5)
    factor = scaling * LOG2E
    key_at = lax.broadcasted_iota(jnp.int32, (block, block), 0)
    limits = limit_ref[0]
    cosine, sine = cosine_ref[...], sine_ref[...]
    grad_rows_ref[...] = grad_ref[...].astype(jnp.float32).T
    mixed_rows_ref[...] = mixed_ref[...].astype(jnp.float32).T
    for kv in range(kv_width // HEAD_DIM):
        rows = slice(kv * HEAD_DIM, (kv + 1) * HEAD_DIM)
        value_rows = slice(kv_width + kv * HEAD_DIM, kv_width + (kv + 1) * HEAD_DIM)
        keys = [flipped(kv_ref[group, rows, :]) for group in range(groups)]
        values = [flipped(kv_ref[group, value_rows, :]) for group in range(groups)]
        for step in range(repeats):
            head = kv * repeats + step
            head_rows = slice(head * HEAD_DIM, (head + 1) * HEAD_DIM)
            query = query_ref[head_rows, :]
            query_tokens = flipped(query)
            grads = grad_rows_ref[head_rows, :]
            delta = jnp.sum(grads * mixed_rows_ref[head_rows, :], axis=0, keepdims=True)
            grads_low = grads.astype(jnp.bfloat16)
            grad_tokens = grads.T.astype(jnp.bfloat16)
            total = total_ref[0, head : head + 1, :]
            grad_query = None
            for group in range(groups):
                raw = jnp.dot(keys[group], query, preferred_element_type=jnp.float32)
                chances = jnp.where(
                    key_at < limits - group * block, jnp.exp2(raw * factor - total), 0.0
                )
                grad_chance = jnp.dot(
                    values[group], grads_low, preferred_element_type=jnp.float32
                )
                grad_score = (chances * (grad_chance - delta)).astype(jnp.bfloat16)
                part = jnp.dot(
                    kv_ref[group, rows, :], grad_score, preferred_element_type=jnp.float32
                )
                grad_query = part if grad_query is None else grad_query + part
                key_part = jnp.dot(
                    grad_score, query_tokens, preferred_element_type=jnp.float32
                )
                value_part = jnp.dot(
                    chances.astype(jnp.bfloat16), grad_tokens, preferred_element_type=jnp.float32
                )
                if step == 0:
                    key_sum_ref[group] = key_part
                    value_sum_ref[group] = value_part
                else:
                    key_sum_ref[group] += key_part
                    value_sum_ref[group] += value_part
            first, second = grad_query[:HALF] * scaling, grad_query[HALF:] * scaling
            query_rows_ref[head * HEAD_DIM : head * HEAD_DIM + HALF, :] = (
                first * cosine + second * sine
            )
            query_rows_ref[head * HEAD_DIM + HALF : (head + 1) * HEAD_DIM, :] = (
                second * cosine - first * sine
            )
        for group in range(groups):
            grad_kv_ref[group, rows, :] = (key_sum_ref[group].T * scaling).astype(jnp.bfloat16)
            grad_kv_ref[group, value_rows, :] = value_sum_ref[group].T.astype(jnp.bfloat16)
    grad_query_ref[...] = query_rows_ref[...].T.astype(jnp.bfloat16)


def attend_back(query, kv_all, limits, totals, mixed, grad_mixed, cosine, sine, repeats):
    query_width, tokens = query.shape
    groups, kv_rows, _ = kv_all.shape
    chips, _, block = limits.shape
    heads = query_width // HEAD_DIM
    pairs = query_width * tokens * groups * block
    by_column = pl.BlockSpec((query_width, block), lambda i: (0, i))
    by_row = pl.BlockSpec((block, query_width), lambda i: (i, 0))
    by_key = pl.BlockSpec((groups, kv_rows, block), lambda i: (0, 0, i))
    table = pl.BlockSpec((HALF, block), lambda i: (0, i))
    return pl.pallas_call(
        lambda *refs: attend_back_kernel(repeats, *refs),
        out_shape=(
            jax.ShapeDtypeStruct((tokens, query_width), jnp.bfloat16),
            jax.ShapeDtypeStruct(kv_all.shape, jnp.bfloat16),
        ),
        grid=(chips,),
        in_specs=[
            by_column,
            by_key,
            pl.BlockSpec((1, 1, block), lambda i: (i, 0, 0)),
            pl.BlockSpec((1, heads, block), lambda i: (i, 0, 0)),
            by_row,
            by_row,
            table,
            table,
        ],
        out_specs=(by_row, by_key),
        scratch_shapes=[
            pltpu.VMEM((query_width, block), jnp.float32),
            pltpu.VMEM((query_width, block), jnp.float32),
            pltpu.VMEM((query_width, block), jnp.float32),
            pltpu.VMEM((groups, block, HEAD_DIM), jnp.float32),
            pltpu.VMEM((groups, block, HEAD_DIM), jnp.float32),
        ],
        cost_estimate=pl.CostEstimate(
            flops=10 * pairs,
            bytes_accessed=2 * (4 * query.size + 2 * kv_all.size),
            transcendentals=pairs // HEAD_DIM,
        ),
        name="attend_back",
    )(query, kv_all, limits, totals, mixed, grad_mixed, cosine, sine)


def times(left, right):
    return jnp.dot(left, right, preferred_element_type=jnp.float32)


def times_t(left, right):
    return lax.dot_general(
        left, right, (((1,), (1,)), ((), ())), preferred_element_type=jnp.float32
    )


def inner_t(left, right):
    return lax.dot_general(
        left, right, (((0,), (0,)), ((), ())), preferred_element_type=jnp.float32
    )


def inverse_rms(values):
    return lax.rsqrt(jnp.mean(values * values, axis=-1, keepdims=True) + epsilon)


def norm_back(grad_normed, source, inverse, gain_full):
    weighted = grad_normed * gain_full
    average = jnp.mean(weighted * source, axis=-1, keepdims=True)
    return inverse * weighted - source * (inverse * inverse * inverse) * average


def limits_of(starts, places):
    limits = places + 1
    for which in range(2):
        inside = (places >= starts[which]) & (places < starts[which] + PIECE)
        limits = jnp.where(inside, starts[which] + PIECE, limits)
    return limits


def swap(value, flip):
    pairs = [(chip, chip ^ flip) for chip in range(CHIPS)]
    return lax.ppermute(value, "chip", pairs)


def collect(block):
    half = block.shape[0] // 2
    first = swap(block, 1)
    second = swap(block, 2)
    low = swap(first[:half], 2)
    high = swap(second[half:], 1)
    return [block, first, second, jnp.concatenate([low, high], axis=0)]


def give_back(total):
    low_type, wide_type = jnp.bfloat16, jnp.float32
    own, first, second, third = jnp.split(total, CHIPS)
    half = own.shape[0] // 2
    low = swap(third[:half], 1).astype(wide_type)
    high = swap(third[half:], 2).astype(wide_type)
    for_first = jnp.concatenate(
        [first[:half], (first[half:].astype(wide_type) + high).astype(low_type)], axis=0
    )
    for_second = jnp.concatenate(
        [(second[:half].astype(wide_type) + low).astype(low_type), second[half:]], axis=0
    )
    from_first = swap(for_first, 1).astype(wide_type)
    from_second = swap(for_second, 2).astype(wide_type)
    return own.astype(wide_type) + from_first + from_second


def shards(
    layer_input,
    positions,
    piece_starts,
    gain_attn,
    w_query,
    w_key,
    w_value,
    w_out,
    gain_mlp,
    w_gate,
    w_up,
    w_down,
    out_grad,
):
    sequences, block_size, model_width = layer_input.shape
    assert sequences == 1
    groups = lax.axis_size("group")
    spread = lax.axis_size("dp")
    group_at, spread_at = lax.axis_index("group"), lax.axis_index("dp")
    chip, core = lax.axis_index("chip"), lax.axis_index("core")
    full_len = block_size * groups
    scaling = HEAD_DIM ** (-0.5)
    repeats = HEADS // KV_HEADS
    kv_own = KV_HEADS // CHIPS
    heads_own = HEADS // CHIPS
    query_width, kv_width = heads_own * HEAD_DIM, kv_own * HEAD_DIM
    half_rows = w_query.shape[0] // 2

    def own_part(weight):
        width = weight.shape[1] // CHIPS
        return lax.dynamic_slice(weight, (core * half_rows, chip * width), (half_rows, width))

    def gathered(*weights):
        part = jnp.concatenate([own_part(weight) for weight in weights], axis=1)
        return lax.all_gather(part, ("group", "core"), axis=0, tiled=True)

    gains = lax.all_gather(jnp.stack([gain_attn, gain_mlp]), "group", axis=1, tiled=True)
    gain_one, gain_two = gains[0].astype(jnp.float32), gains[1].astype(jnp.float32)

    w_attn = gathered(w_query, w_key, w_value, w_out)
    w_qkv, w_mix = w_attn[:, :-query_width], w_attn[:, -query_width:]
    w_lift = gathered(w_gate, w_up)
    w_sink = gathered(w_down)

    source_low = layer_input[0]
    source_all = jnp.concatenate(collect(source_low), axis=0).astype(jnp.float32)
    small = jnp.concatenate([positions[0], piece_starts[0]])
    smalls = jnp.stack([small, swap(small, 1), swap(small, 2), swap(small, 3)])
    places, starts_all = smalls[:, :block_size].reshape(-1), smalls[:, block_size:]
    grad_low = jnp.concatenate(collect(out_grad[0]), axis=0)

    normed_one = (source_all * inverse_rms(source_all) * gain_one).astype(jnp.bfloat16)
    cosine, sine = rope_tables(places)
    tokens = CHIPS * block_size
    lin = lax.dot_general(
        w_qkv, normed_one, (((0,), (1,)), ((), ())), preferred_element_type=jnp.float32
    )
    query_rot = rotate(lin[:query_width], cosine, sine).astype(jnp.bfloat16)
    key_rot = rotate(lin[query_width : query_width + kv_width], cosine, sine)
    kv_own_tokens = jnp.concatenate(
        [key_rot.astype(jnp.bfloat16), lin[query_width + kv_width :].astype(jnp.bfloat16)], axis=0
    )
    kv_all = lax.all_gather(kv_own_tokens, "group", axis=0, tiled=True)
    kv_all = kv_all.reshape(groups, 2 * kv_width, tokens)

    def reduced(total):
        return lax.psum_scatter(total, SUM_AXES, scatter_dimension=0, tiled=True)

    def product_low(left, right):
        return inner_t(left, right).astype(jnp.bfloat16)

    then = lax.optimization_barrier

    count = spread * CHIPS * 2
    whose = (spread_at * CHIPS + chip) * 2 + core

    def owned(total):
        rows, columns = total.shape[0] // CHIPS, total.shape[1]
        total = total.reshape(CHIPS, rows, columns)
        pieces = []
        for step in range(CHIPS):
            pairs = []
            for source_at in range(count):
                at_spread, at_chip, at_core = (
                    source_at // (2 * CHIPS),
                    source_at // 2 % CHIPS,
                    source_at % 2,
                )
                target = (at_core * spread + at_spread) * CHIPS + (at_chip ^ step)
                pairs.append((source_at, target))
            block = lax.dynamic_index_in_dim(total, chip ^ step, axis=0, keepdims=False)
            pieces.append(lax.ppermute(block, REPLICA, pairs))
        pieces = jnp.stack(pieces)
        return [
            lax.dynamic_index_in_dim(pieces, (whose % CHIPS) ^ at, axis=0, keepdims=False)
            for at in range(CHIPS)
        ]

    def laid(parts, start, width):
        parts = [part[:, start : start + width] for part in parts]
        return jnp.concatenate(parts, axis=1).astype(jnp.float32)

    query_places = group_at * block_size + jnp.arange(block_size, dtype=jnp.int32)
    limits = jnp.stack([limits_of(starts_all[which], query_places) for which in range(CHIPS)])
    limits = limits[:, None, :]
    mixed_low, log_totals = attend(query_rot, kv_all, limits, repeats)

    def parts(left, right):
        return times_t(left, right).astype(jnp.bfloat16)

    source = source_low.astype(jnp.float32)
    inverse_one = inverse_rms(source)
    unit_one = source * inverse_one
    middle = source + give_back(parts(mixed_low, w_mix))
    inverse_two = inverse_rms(middle)
    unit_two = middle * inverse_two
    normed_two = jnp.concatenate(collect((unit_two * gain_two).astype(jnp.bfloat16)), axis=0)
    wide = w_lift.shape[1] // 2
    both_up = times(normed_two, w_lift)
    gated, lifted = both_up[:, :wide], both_up[:, wide:]
    activated = jax.nn.silu(gated)
    hidden = (activated * lifted).astype(jnp.bfloat16)
    total_down, w_sink = then((product_low(grad_low, hidden), w_sink))
    sum_down = reduced(total_down)

    grad_hidden = times(grad_low, w_sink)
    sigmoid_gate = jax.nn.sigmoid(gated)
    grad_gate_low = (
        grad_hidden * lifted * (sigmoid_gate + gated * sigmoid_gate * (1.0 - sigmoid_gate))
    ).astype(jnp.bfloat16)
    grad_lift_low = (grad_hidden * activated).astype(jnp.bfloat16)
    grad_both = jnp.concatenate([grad_gate_low, grad_lift_low], axis=1)
    grad_parts, grad_both = then((parts(grad_both, w_lift), grad_both))
    sum_lift = reduced(product_low(normed_two, grad_both))
    grad_normed_two = give_back(grad_parts)
    grad_normed_two, sum_down = then((grad_normed_two, sum_down))
    grad_gain_two = jnp.sum(grad_normed_two * unit_two, axis=0)
    grad_middle = out_grad[0].astype(jnp.float32) + norm_back(
        grad_normed_two, middle, inverse_two, gain_two
    )
    hidden, grad_middle = then((hidden, grad_middle))
    grad_middle_low = jnp.concatenate(collect(grad_middle.astype(jnp.bfloat16)), axis=0)
    sink_parts, grad_middle_low = then((parts(hidden, w_sink), grad_middle_low))
    output_full = middle + give_back(sink_parts)
    grad_mixed_low = times(grad_middle_low, w_mix).astype(jnp.bfloat16)
    grad_query_low, grad_kv = attend_back(
        query_rot, kv_all, limits, log_totals, mixed_low, grad_mixed_low, cosine, sine, repeats
    )
    grad_kv, sum_lift = then((grad_kv.reshape(groups * 2 * kv_width, tokens), sum_lift))
    grad_kv = lax.psum_scatter(grad_kv, "group", scatter_dimension=0, tiled=True)
    grad_down = laid(owned(sum_down), 0, wide)
    lift_parts = owned(sum_lift)
    grad_gate, grad_up = laid(lift_parts, 0, wide), laid(lift_parts, wide, wide)
    grad_kv, lift_parts, output_full = then((grad_kv, lift_parts, output_full))
    grad_key = unrotate(grad_kv[:kv_width].astype(jnp.float32), cosine, sine)
    grad_kv_low = jnp.concatenate([grad_key.astype(jnp.bfloat16), grad_kv[kv_width:]], axis=0).T
    total_query = product_low(normed_one, grad_query_low)
    total_out = product_low(grad_middle_low, mixed_low)
    both_totals = with_layout_constraint(
        jnp.concatenate([total_query, total_out], axis=1), Layout(major_to_minor=(0, 1))
    )
    both_totals, grad_kv_low = then((both_totals, grad_kv_low))
    both_sums = reduced(both_totals)
    added_query = times_t(grad_query_low, w_qkv[:, :query_width])
    added = added_query + times_t(grad_kv_low, w_qkv[:, query_width:])
    added = give_back(added.astype(jnp.bfloat16))
    grad_gain_one = jnp.sum(added * unit_one, axis=0)
    input_grad = grad_middle + norm_back(added, source, inverse_one, gain_one)
    squares = jnp.stack(
        [jnp.sum(source * source), jnp.sum(middle * middle), jnp.sum(output_full * output_full)]
    )
    place = core * spread + spread_at
    apart = jnp.where(jnp.arange(2 * spread)[:, None] == place, squares[None, :], 0.0)
    apart = apart.reshape(1, -1)
    extra = jnp.concatenate(
        [
            grad_gain_one[:, None],
            grad_gain_two[:, None],
            jnp.broadcast_to(apart, (model_width, apart.shape[1])),
        ],
        axis=1,
    ).astype(jnp.bfloat16)
    kv_totals = jnp.concatenate([product_low(normed_one, grad_kv_low), extra], axis=1)
    kv_totals, both_sums = then((kv_totals, both_sums))
    kv_sums = reduced(kv_totals)
    square_totals = lax.dynamic_slice(
        kv_sums[:1, 2 * kv_width + 2 :].astype(jnp.float32), (0, place * 3), (1, 3)
    )
    stream_rms = jnp.sqrt(square_totals / (full_len * model_width))

    both_parts = owned(both_sums)
    grad_query = laid(both_parts, 0, query_width)
    grad_out = laid(both_parts, query_width, query_width)
    kv_parts = owned(kv_sums[:, : 2 * kv_width + 2])
    grad_key, grad_value = laid(kv_parts, 0, kv_width), laid(kv_parts, kv_width, kv_width)
    gains_owned = sum(part[:, 2 * kv_width :].astype(jnp.float32) for part in kv_parts)

    return (
        output_full.astype(jnp.bfloat16)[None],
        input_grad[None],
        gains_owned[:, 0],
        grad_query,
        grad_key,
        grad_value,
        grad_out,
        gains_owned[:, 1],
        grad_gate,
        grad_up,
        grad_down,
        stream_rms,
    )


def solution(mesh):
    groups, replicas = mesh.shape["group"], mesh.shape["replica"]
    spread = replicas // (2 * CHIPS)
    devices = np.asarray(mesh.devices).reshape(groups, spread, CHIPS, 2)
    split = Mesh(devices, ("group", "dp", "chip", "core"))
    everyone = ("group",) + REPLICA
    placed = (
        P(REPLICA, "group", None),
        P(REPLICA, "group"),
        P(REPLICA, None),
        P("group"),
        P("group", None),
        P("group", None),
        P("group", None),
        P("group", None),
        P("group"),
        P("group", None),
        P("group", None),
        P("group", None),
        P(REPLICA, "group", None),
    )
    return jax.shard_map(
        shards,
        mesh=split,
        in_specs=placed,
        out_specs=(
            P(REPLICA, "group", None),
            P(REPLICA, "group", None),
            P(everyone),
            P(everyone, None),
            P(everyone, None),
            P(everyone, None),
            P(everyone, None),
            P(everyone),
            P(everyone, None),
            P(everyone, None),
            P(everyone, None),
            P(REPLICA, None),
        ),
        check_vma=False,
    )
```

time: 1340 us -> 924 us (0.69)
  waiting for transfers between devices: 766 us -> 456 us
  matrix products: 245 us -> 180 us
  local copies, waits for them, and re-layouts: 106 us -> 41.7 us
  Pallas kernels: 0 us -> 61.4 us
  other arithmetic: 103 us -> 73.4 us
    reduce_scatter x4, waiting for transfers between devices: 232 us -> 56.2 us  [reduced(): return lax.psum_scatter(total, SUM_AXES, scatter_dimension=0, tiled=True)]
    unnamed x12 -> x9, waiting for transfers between devices: 129 us -> 0.15 us
    pallas_call x0 -> x2, Pallas kernels: none -> 61.4 us  [the longest x1 40.3 us: attend_back(): pl.pallas_call(lambda *refs: attend_back_kernel(repeats, *refs), out_shap...]
    dot_general x24 -> x1, matrix products: 65.4 us -> 9.5 us  [shards(): lax.dot_general(w_qkv, normed_one, (((0,), (1,)), ((), ())), preferred_el...]
    all_gather x1, waiting for transfers between devices: 7.58 us -> 31.1 us  [shards(): kv_all = lax.all_gather(kv_own_tokens, 'group', axis=0, tiled=True)]
    convert_element_type x16 -> x13, other arithmetic: 38.4 us -> 18.9 us  [the longest x7 8.19 us: laid(): return jnp.concatenate(parts, axis=1).astype(jnp.float32)]
    unnamed x184 -> x106, local copies, waits for them, and re-layouts: 33.2 us -> 13.7 us
    reshape x6 -> x0, local copies, waits for them, and re-layouts: 18.1 us -> none  [the longest x2 8.51 us: shards(): both_all = both_all.reshape(groups, CHIPS, block_size, 2, kv_own, HEAD_DIM)]
  transfers between devices with their start and end apart: 62 -> 60, of which waited for: 35 -> 37; matrix products, arithmetic and copies ran while one was open for 20% -> 28% of each run, Pallas kernels for 0% -> 7%
where the time goes in v2:
time: 924 us; the launch traced here: 914 us
  waiting for transfers between devices  456 us (49%)
  matrix products  180 us (19%)
  other arithmetic  73.4 us (8%)
  starting transfers between devices  67.2 us (7%)
  Pallas kernels  61.4 us (7%)
  local copies, waits for them, and re-layouts  41.7 us (5%)
  between operations  20.7 us (2%)
  blocking collectives  13.4 us (1%)
    ppermute x35, waiting for transfers between devices, swap(): return lax.ppermute(value, 'chip', pairs)  266 us
    all_gather x3, waiting for transfers between devices, gathered(): return lax.all_gather(part, ('group', 'core'), axis=0, tiled=True)  75.2 us
    dot_general x5, matrix products, inner_t(): lax.dot_general(left, right, (((0,), (0,)), ((), ())), preferred_element_...  59.3 us
    dot_general x3, matrix products, times(): return jnp.dot(left, right, preferred_element_type=jnp.float32)  56.3 us
    reduce_scatter x4, waiting for transfers between devices, reduced(): return lax.psum_scatter(total, SUM_AXES, scatter_dimension=0, tiled=True)  56.2 us
    dot_general x5, matrix products, times_t(): lax.dot_general(left, right, (((1,), (1,)), ((), ())), preferred_element_...  54.5 us
    ppermute x35, starting transfers between devices, swap(): return lax.ppermute(value, 'chip', pairs)  43.1 us
    pallas_call x1, Pallas kernels, attend_back(): pl.pallas_call(lambda *refs: attend_back_kernel(repeats, *refs), out_shap...  40.3 us
  transfers between devices with their start and end apart: 60, of which 37 were waited for; matrix products, arithmetic and copies ran while one was open for 28% of the time, Pallas kernels for 7%

profile of v2, /device:TPU:0, one launch (start us, length us, event | category | flops | bytes accessed | tf_op | source)
XLA Modules:
  0.0 914.0 jit_solution(14431611354905158255)
XLA Ops:
  22.0 13.4 %all_gather.16 = bf16[2,2560]{1,0:T(2,128)(2,1)S(1)} all-gather(bf16[2,640]{1,0:T(2,128)(2,1)S(1)} %pad_maximum_fusion.19), channel_id=1, replica_groups=mesh['group'=4,'dp'=1,'chip'=4,'core'=2] {'group'}, dimensions={1}, use_global_device_ids=true | all-gather | bytes 12800 | tf_op jit(solution)/shard_map/all_gather | solution.py:353
  35.6 11.5 %collective-permute-done.6 = s32[258]{0:T(512)S(1)} collective-permute-done((s32[258]{0:T(512)S(1)}, s32[258]{0:T(512)S(1)}, u32[]{:S(2)}, u32[]{:S(2)}) %collective-permute-start.6) | collective-permute-done | bytes 1064 | tf_op jit(solution)/shard_map/ppermute | solution.py:287
  50.4 13.1 %collective-permute-done.2 = bf16[128,2560]{1,0:T(8,128)(2,1)S(1)} collective-permute-done((bf16[128,2560]{1,0:T(8,128)(2,1)S(1)}, bf16[128,2560]{1,0:T(8,128)(2,1)S(1)}, u32[]{:S(2)}, u32[]{:S(2)}) %collective-permute-start.2) | collective-permute-done | bytes 655392 | tf_op jit(solution)/shard_map/ppermute | solution.py:287
  67.1 32.8 %all-gather.5.cloned.1.call-done = bf16[2560,1600]{1,0:T(8,128)(2,1)} async-done(((bf16[320,1600]{1,0:T(8,128)(2,1)}), bf16[2560,1600]{1,0:T(8,128)(2,1)}) %all-gather.5.cloned.1.call-update) | async-done | bytes 8192016 | tf_op jit(solution)/shard_map/all_gather | solution.py:351
  99.9 9.5 %fusion.3 = f32[960,1024]{1,0:T(8,128)S(1)} fusion(bf16[2560,1600]{1,0:T(8,128)(2,1)} %all-gather.5.cloned.1.call-done, bf16[1024,2560]{1,0:T(8,128)(2,1)} %copy-done.10, f32[2560]{0:T(1024)S(1)} %get-tuple-element.101, f32[1024]{0:T(1024)S(1)} %add_rsqrt_fusion), kind=kOutput, calls=%fused_computation.18 | convolution fusion | flops 5043650560 | bytes 14432256 | tf_op jit(solution)/shard_map/dot_general | solution.py:371
  134.8 31.1 %all-gather.7.cloned.1.call-done = bf16[1280,1024]{1,0:T(8,128)(2,1)} async-done(((bf16[320,1024]{1,0:T(8,128)(2,1)}), bf16[1280,1024]{1,0:T(8,128)(2,1)}) %all-gather.7.cloned.1.call-update) | async-done | bytes 2621456 | tf_op jit(solution)/shard_map/all_gather | solution.py:379
  165.9 21.0 %attend.1 = (bf16[1024,640]{1,0:T(8,128)(2,1)}, f32[4,8,256]{2,1,0:T(8,128)}) custom-call(bf16[640,1024]{1,0:T(8,128)(2,1)} %bitcast.160, bf16[4,320,1024]{2,1,0:T(8,128)(2,1)} %bitcast.185, s32[4,1,256]{2,1,0:T(1,128)} %broadcast_in_dim.43.refs_2_), custom_call_target="tpu_custom_call" | custom-call | flops 2684354560 | bytes 5242880 | tf_op jit(solution)/shard_map/attend/pallas_call | solution.py:100
  187.0 6.9 convolution_convert_fusion.2
  198.2 13.6 %collective-permute-done.7 = bf16[128,2560]{1,0:T(8,128)(2,1)S(1)} collective-permute-done((bf16[128,2560]{1,0:T(8,128)(2,1)S(1)}, bf16[128,2560]{1,0:T(8,128)(2,1)S(1)}, u32[]{:S(2)}, u32[]{:S(2)}) %collective-permute-start.7) | collective-permute-done | bytes 655392 | tf_op jit(solution)/shard_map/ppermute | solution.py:287
  216.1 25.3 %collective-permute-done.15 = bf16[256,2560]{1,0:T(8,128)(2,1)S(1)} collective-permute-done((bf16[256,2560]{1,0:T(8,128)(2,1)S(1)}, bf16[256,2560]{1,0:T(8,128)(2,1)S(1)}, u32[]{:S(2)}, u32[]{:S(2)}) %collective-permute-start.15) | collective-permute-done | bytes 1310752 | tf_op jit(solution)/shard_map/ppermute | solution.py:287
  243.7 24.3 %collective-permute-done.10 = bf16[256,2560]{1,0:T(8,128)(2,1)S(1)} collective-permute-done((bf16[256,2560]{1,0:T(8,128)(2,1)S(1)}, bf16[256,2560]{1,0:T(8,128)(2,1)S(1)}, u32[]{:S(2)}, u32[]{:S(2)}) %collective-permute-start.10) | collective-permute-done | bytes 1310752 | tf_op jit(solution)/shard_map/ppermute | solution.py:287
  275.5 6.5 collective-permute-done.17
  283.6 26.5 %collective-permute-done.11 = bf16[256,2560]{1,0:T(8,128)(2,1)S(1)} collective-permute-done((bf16[256,2560]{1,0:T(8,128)(2,1)S(1)}, bf16[256,2560]{1,0:T(8,128)(2,1)S(1)}, u32[]{:S(2)}, u32[]{:S(2)}) %collective-permute-start.11) | collective-permute-done | bytes 1310752 | tf_op jit(solution)/shard_map/ppermute | solution.py:287
  314.7 10.8 %collective-permute-done.13 = bf16[128,2560]{1,0:T(8,128)(2,1)S(1)} collective-permute-done((bf16[128,2560]{1,0:T(8,128)(2,1)S(1)}, bf16[128,2560]{1,0:T(8,128)(2,1)S(1)}, u32[]{:S(2)}, u32[]{:S(2)}) %collective-permute-start.13) | collective-permute-done | bytes 655392 | tf_op jit(solution)/shard_map/ppermute | solution.py:287
  327.3 3.6 all-gather.9.cloned.1.call-done
  331.0 27.8 %fusion.54 = f32[1024,3584]{1,0:T(8,128)} fusion(bf16[1024,2560]{1,0:T(8,128)(2,1)} %constant_dynamic-update-slice_fusion.5, bf16[2560,3584]{1,0:T(8,128)(2,1)} %all-gather.9.cloned.1.call-done), kind=kOutput, calls=%fused_computation.210 | convolution fusion | flops 18790481920 | bytes 38273024 | tf_op jit(solution)/shard_map/dot_general | solution.py:252
  358.8 6.4 multiply_convert_fusion.2
  367.2 13.9 %convolution_convert_fusion.1 = bf16[2560,1792]{1,0:T(8,128)(2,1)} fusion(bf16[1024,2560]{1,0:T(8,128)(2,1)} %copy-done.26, bf16[1024,1792]{1,0:T(8,128)(2,1)S(1)} %multiply_convert_fusion.2), kind=kOutput, calls=%fused_computation.3 | convolution fusion | flops 9399828480 | bytes 18087936 | tf_op jit(solution)/shard_map/dot_general | solution.py:262
  381.1 38.7 %all-gather.11.cloned.1.call-done = bf16[2560,1792]{1,0:T(8,128)(2,1)} async-done(((bf16[320,1792]{1,0:T(8,128)(2,1)}), bf16[2560,1792]{1,0:T(8,128)(2,1)}) %all-gather.11.cloned.1.call-update) | async-done | bytes 9175056 | tf_op jit(solution)/shard_map/all_gather | solution.py:351
  419.9 20.9 %multiply_convert_fusion.1 = (bf16[1024,1792]{1,0:T(8,128)(2,1)S(1)}, bf16[1024,1792]{1,0:T(8,128)(2,1)}) fusion(f32[1024,3584]{1,0:T(8,128)} %fusion.54, bf16[1024,2560]{1,0:T(8,128)(2,1)} %copy-done.26, bf16[2560,1792]{1,0:T(8,128)(2,1)} %all-gather.11.cloned.1.call-done), kind=kOutput, calls=%fused_computation.10 | convolution fusion | flops 9417261056 | bytes 36438016 | tf_op jit(solution)/shard_map/dot_general | solution.py:252
  440.8 5.6 pad_maximum_fusion
  446.3 24.2 %convolution_convert_fusion.4 = bf16[1024,2560]{1,0:T(8,128)(2,1)} fusion(bf16[2560,3584]{1,0:T(8,128)(2,1)} %all-gather.9.cloned.1.call-done, bf16[1024,1792]{1,0:T(8,128)(2,1)} %get-tuple-element.109, bf16[1024,1792]{1,0:T(8,128)(2,1)S(1)} %get-tuple-element.108), kind=kOutput, calls=%fused_computation.17 | convolution fusion | flops 18807783424 | bytes 30932992 | tf_op jit(solution)/shard_map/dot_general | solution.py:256
  470.5 26.9 %convolution_convert_fusion = bf16[2560,3584]{1,0:T(8,128)(2,1)} fusion(bf16[1024,2560]{1,0:T(8,128)(2,1)} %constant_dynamic-update-slice_fusion.5, bf16[1024,3584]{1,0:T(8,128)(2,1)} %pad_maximum_fusion), kind=kOutput, calls=%fused_computation | convolution fusion | flops 18799656960 | bytes 30932992 | tf_op jit(solution)/shard_map/dot_general | solution.py:262
  502.8 14.1 %collective-permute-done.19 = bf16[128,2560]{1,0:T(8,128)(2,1)S(1)} collective-permute-done((bf16[128,2560]{1,0:T(8,128)(2,1)S(1)}, bf16[128,2560]{1,0:T(8,128)(2,1)S(1)}, u32[]{:S(2)}, u32[]{:S(2)}) %collective-permute-start.19) | collective-permute-done | bytes 655392 | tf_op jit(solution)/shard_map/ppermute | solution.py:287
  524.0 27.0 %collective-permute-done.22 = bf16[256,2560]{1,0:T(8,128)(2,1)} collective-permute-done((bf16[256,2560]{1,0:T(8,128)(2,1)}, bf16[256,2560]{1,0:T(8,128)(2,1)}, u32[]{:S(2)}, u32[]{:S(2)}) %collective-permute-start.22) | collective-permute-done | bytes 1310752 | tf_op jit(solution)/shard_map/ppermute | solution.py:287
  552.4 4.1 convert_add_fusion.2
  556.6 3.6 multiply_reduce_fusion.1
  565.4 12.3 %convolution_convert_fusion.3 = bf16[1024,2560]{1,0:T(8,128)(2,1)S(1)} fusion(bf16[1024,1792]{1,0:T(8,128)(2,1)S(1)} %copy-done.17, bf16[2560,1792]{1,0:T(8,128)(2,1)} %all-gather.11.cloned.1.call-done), kind=kOutput, calls=%fused_computation.16 | convolution fusion | flops 9397862400 | bytes 18087936 | tf_op jit(solution)/shard_map/dot_general | solution.py:256
  577.7 13.4 %collective-permute-done.23 = bf16[256,2560]{1,0:T(8,128)(2,1)S(1)} collective-permute-done((bf16[256,2560]{1,0:T(8,128)(2,1)S(1)}, bf16[256,2560]{1,0:T(8,128)(2,1)S(1)}, u32[]{:S(2)}, u32[]{:S(2)}) %collective-permute-start.23) | collective-permute-done | bytes 1310752 | tf_op jit(solution)/shard_map/ppermute | solution.py:287
  594.4 11.9 %collective-permute-done.25 = bf16[128,2560]{1,0:T(8,128)(2,1)S(1)} collective-permute-done((bf16[128,2560]{1,0:T(8,128)(2,1)S(1)}, bf16[128,2560]{1,0:T(8,128)(2,1)S(1)}, u32[]{:S(2)}, u32[]{:S(2)}) %collective-permute-start.25) | collective-permute-done | bytes 655392 | tf_op jit(solution)/shard_map/ppermute | solution.py:287
  609.9 7.6 fusion.20.refs_5_
  617.5 40.3 %attend_back.1 = (bf16[1024,640]{1,0:T(8,128)(2,1)}, bf16[4,320,1024]{2,1,0:T(8,128)(2,1)}) custom-call(bf16[640,1024]{1,0:T(8,128)(2,1)} %bitcast.161, bf16[4,320,1024]{2,1,0:T(8,128)(2,1)} %bitcast.186, s32[4,1,256]{2,1,0:T(1,128)} %broadcast_in_dim.43.refs_2_, f32[4,8,256]{2,1,0:T(8,128)} %get-tuple-element.34.refs_3_, ...), custom_call_target="tpu_custom_call" | custom-call | flops 6710886400 | bytes 10485760 | tf_op jit(solution)/shard_map/attend_back/pallas_call | solution.py:217
  657.8 9.2 %convolution_convert_fusion.6 = bf16[2560,640]{1,0:T(8,128)(2,1)} fusion(bf16[1024,640]{1,0:T(8,128)(2,1)} %get-tuple-element.49, bf16[1024,2560]{1,0:T(8,128)(2,1)} %copy-done.10, f32[2560]{0:T(1024)S(1)} %copy-done.30, f32[1024]{0:T(1024)S(1)} %copy-done.36), kind=kOutput, calls=%fused_computation.26 | convolution fusion | flops 3367567360 | bytes 9844736 | tf_op jit(solution)/shard_map/dot_general | solution.py:262
  667.0 34.2 %reduce-scatter.10.cloned.1.call-done = bf16[320,3584]{1,0:T(8,128)(2,1)} async-done(((bf16[2560,3584]{1,0:T(8,128)(2,1)}), bf16[320,3584]{1,0:T(8,128)(2,1)}) %reduce-scatter.10.cloned.1.call-update) | async-done | bytes 2293776 | tf_op jit(solution)/shard_map/reduce_scatter | solution.py:383
  701.2 7.2 convolution_convert_fusion.5
  725.7 21.3 %collective-permute-done.34 = bf16[256,2560]{1,0:T(8,128)(2,1)} collective-permute-done((bf16[256,2560]{1,0:T(8,128)(2,1)}, bf16[256,2560]{1,0:T(8,128)(2,1)}, u32[]{:S(2)}, u32[]{:S(2)}) %collective-permute-start.34) | collective-permute-done | bytes 1310752 | tf_op jit(solution)/shard_map/ppermute | solution.py:287
  747.7 4.2 add_add_fusion
  751.8 6.7 collective-permute-done.30
  758.5 7.7 collective-permute-done.29
  769.5 3.4 collective-permute-start.50
  775.5 6.6 collective-permute-done.50
  782.1 5.6 collective-permute-done.49
  789.5 6.2 fusion.5
  795.9 4.9 add_convert_fusion
  804.5 14.0 %collective-permute-done.35 = bf16[128,2560]{1,0:T(8,128)(2,1)S(1)} collective-permute-done((bf16[128,2560]{1,0:T(8,128)(2,1)S(1)}, bf16[128,2560]{1,0:T(8,128)(2,1)S(1)}, u32[]{:S(2)}, u32[]{:S(2)}) %collective-permute-start.35) | collective-permute-done | bytes 655392 | tf_op jit(solution)/shard_map/ppermute | solution.py:287
  828.6 22.2 %collective-permute-done.38 = bf16[256,2560]{1,0:T(8,128)(2,1)S(1)} collective-permute-done((bf16[256,2560]{1,0:T(8,128)(2,1)S(1)}, bf16[256,2560]{1,0:T(8,128)(2,1)S(1)}, u32[]{:S(2)}, u32[]{:S(2)}) %collective-permute-start.38) | collective-permute-done | bytes 1310752 | tf_op jit(solution)/shard_map/ppermute | solution.py:287
  865.7 5.1 fusion.15
  873.4 22.0 %reduce-scatter.16.cloned.1.call-done = bf16[320,328]{1,0:T(8,128)(2,1)} async-done(((bf16[2560,328]{1,0:T(8,128)(2,1)}), bf16[320,328]{1,0:T(8,128)(2,1)}) %reduce-scatter.16.cloned.1.call-update) | async-done | bytes 209936 | tf_op jit(solution)/shard_map/reduce_scatter | solution.py:383
  (341 shorter events, 164.3 us)
Async XLA Ops:
  7.2 92.7 %all-gather.5.cloned.1.call-start = ((), (), s32[]{:S(2)}) async-start(), calls=%async_computation.5 | async-start | bytes 9584640 | tf_op jit(solution)/shard_map/all_gather | solution.py:351
  13.8 152.1 %all-gather.7.cloned.1.call-start = ((), (), s32[]{:S(2)}) async-start(), calls=%async_computation.6 | async-start | bytes 3276800 | tf_op jit(solution)/shard_map/all_gather | solution.py:379
  13.9 34.0 %collective-permute-start = (bf16[256,2560]{1,0:T(8,128)(2,1)S(1)}, bf16[256,2560]{1,0:T(8,128)(2,1)S(1)}, u32[]{:S(2)}, u32[]{:S(2)}) collective-permute-start(bf16[256,2560]{1,0:T(8,128)(2,1)S(1)} %bitcast.148), channel_id=1, source_target_pairs={{0,2},{2,0},{4,6},{6,4},{1,3},{3,1},{5,7},{7,5},{8,10},{10,8},{12,... | collective-permute-start | bytes 3932168 | tf_op jit(solution)/shard_map/ppermute | solution.py:287
  16.9 32.6 %collective-permute-start.1 = (bf16[256,2560]{1,0:T(8,128)(2,1)S(1)}, bf16[256,2560]{1,0:T(8,128)(2,1)S(1)}, u32[]{:S(2)}, u32[]{:S(2)}) collective-permute-start(bf16[256,2560]{1,0:T(8,128)(2,1)S(1)} %bitcast.149), channel_id=1, source_target_pairs={{0,4},{2,6},{4,0},{6,2},{1,5},{3,7},{5,1},{7,3},{8,12},{10,14},{12... | collective-permute-start | bytes 3932168 | tf_op jit(solution)/shard_map/ppermute | solution.py:287
  18.4 28.7 %collective-permute-start.6 = (s32[258]{0:T(512)S(1)}, s32[258]{0:T(512)S(1)}, u32[]{:S(2)}, u32[]{:S(2)}) collective-permute-start(s32[258]{0:T(512)S(1)} %pad_add_fusion.4), channel_id=1, source_target_pairs={{0,6},{2,4},{4,2},{6,0},{1,7},{3,5},{5,3},{7,1},{8,14},{10,12},{12... | collective-permute-start | bytes 3104 | tf_op jit(solution)/shard_map/ppermute | solution.py:287
  18.5 28.7 %collective-permute-start.5 = (s32[258]{0:T(512)S(1)}, s32[258]{0:T(512)S(1)}, u32[]{:S(2)}, u32[]{:S(2)}) collective-permute-start(s32[258]{0:T(512)S(1)} %pad_add_fusion.4), channel_id=1, source_target_pairs={{0,4},{2,6},{4,0},{6,2},{1,5},{3,7},{5,1},{7,3},{8,12},{10,14},{12... | collective-permute-start | bytes 3104 | tf_op jit(solution)/shard_map/ppermute | solution.py:287
  20.5 26.7 %collective-permute-start.4 = (s32[258]{0:T(512)S(1)}, s32[258]{0:T(512)S(1)}, u32[]{:S(2)}, u32[]{:S(2)}) collective-permute-start(s32[258]{0:T(512)S(1)} %pad_add_fusion.4), channel_id=1, source_target_pairs={{0,2},{2,0},{4,6},{6,4},{1,3},{3,1},{5,7},{7,5},{8,10},{10,8},{12,... | collective-permute-start | bytes 3104 | tf_op jit(solution)/shard_map/ppermute | solution.py:287
  48.0 15.5 %collective-permute-start.2 = (bf16[128,2560]{1,0:T(8,128)(2,1)S(1)}, bf16[128,2560]{1,0:T(8,128)(2,1)S(1)}, u32[]{:S(2)}, u32[]{:S(2)}) collective-permute-start(bf16[128,2560]{1,0:T(8,128)(2,1)S(1)} %slice.441), channel_id=1, source_target_pairs={{0,4},{2,6},{4,0},{6,2},{1,5},{3,7},{5,1},{7,3},{8,12},{10,14},{12... | collective-permute-start | bytes 1966088 | tf_op jit(solution)/shard_map/ppermute | solution.py:287
  49.6 15.2 %collective-permute-start.3 = (bf16[128,2560]{1,0:T(8,128)(2,1)S(1)}, bf16[128,2560]{1,0:T(8,128)(2,1)S(1)}, u32[]{:S(2)}, u32[]{:S(2)}) collective-permute-start(bf16[128,2560]{1,0:T(8,128)(2,1)S(1)} %slice.442), channel_id=1, source_target_pairs={{0,2},{2,0},{4,6},{6,4},{1,3},{3,1},{5,7},{7,5},{8,10},{10,8},{12,... | collective-permute-start | bytes 1966088 | tf_op jit(solution)/shard_map/ppermute | solution.py:287
  112.5 218.5 %all-gather.9.cloned.1.call-start = ((), (), s32[]{:S(2)}) async-start(), calls=%async_computation.7 | async-start | bytes 20643840 | tf_op jit(solution)/shard_map/all_gather | solution.py:351
  115.8 304.1 %all-gather.11.cloned.1.call-start = ((), (), s32[]{:S(2)}) async-start(), calls=%async_computation.8 | async-start | bytes 10321920 | tf_op jit(solution)/shard_map/all_gather | solution.py:351
  118.2 438.4 %reduce-scatter.8.cloned.1.call-start = ((), (), s32[]{:S(2)}) async-start(), calls=%async_computation.9 | async-start | bytes 10321920 | tf_op jit(solution)/shard_map/reduce_scatter | solution.py:383
  194.1 17.7 %collective-permute-start.7 = (bf16[128,2560]{1,0:T(8,128)(2,1)S(1)}, bf16[128,2560]{1,0:T(8,128)(2,1)S(1)}, u32[]{:S(2)}, u32[]{:S(2)}) collective-permute-start(bf16[128,2560]{1,0:T(8,128)(2,1)S(1)} %get-tuple-element.131), channel_id=1, source_target_pairs={{0,4},{2,6},{4,0},{6,2},{1,5},{3,7},{5,1},{7,3},{8,12},{10,14},{12... | collective-permute-start | bytes 1966088 | tf_op jit(solution)/shard_map/ppermute | solution.py:287
  195.6 17.7 %collective-permute-start.9 = (bf16[128,2560]{1,0:T(8,128)(2,1)S(1)}, bf16[128,2560]{1,0:T(8,128)(2,1)S(1)}, u32[]{:S(2)}, u32[]{:S(2)}) collective-permute-start(bf16[128,2560]{1,0:T(8,128)(2,1)S(1)} %get-tuple-element.130), channel_id=1, source_target_pairs={{0,2},{2,0},{4,6},{6,4},{1,3},{3,1},{5,7},{7,5},{8,10},{10,8},{12,... | collective-permute-start | bytes 1966088 | tf_op jit(solution)/shard_map/ppermute | solution.py:287
  197.1 44.3 %collective-permute-start.15 = (bf16[256,2560]{1,0:T(8,128)(2,1)S(1)}, bf16[256,2560]{1,0:T(8,128)(2,1)S(1)}, u32[]{:S(2)}, u32[]{:S(2)}) collective-permute-start(bf16[256,2560]{1,0:T(8,128)(2,1)S(1)} %bitcast.153), channel_id=1, source_target_pairs={{0,2},{2,0},{4,6},{6,4},{1,3},{3,1},{5,7},{7,5},{8,10},{10,8},{12,... | collective-permute-start | bytes 3932168 | tf_op jit(solution)/shard_map/ppermute | solution.py:287
  197.7 44.4 %collective-permute-start.16 = (bf16[256,2560]{1,0:T(8,128)(2,1)S(1)}, bf16[256,2560]{1,0:T(8,128)(2,1)S(1)}, u32[]{:S(2)}, u32[]{:S(2)}) collective-permute-start(bf16[256,2560]{1,0:T(8,128)(2,1)S(1)} %bitcast.154), channel_id=1, source_target_pairs={{0,4},{2,6},{4,0},{6,2},{1,5},{3,7},{5,1},{7,3},{8,12},{10,14},{12... | collective-permute-start | bytes 3932168 | tf_op jit(solution)/shard_map/ppermute | solution.py:287
  213.8 54.2 %collective-permute-start.10 = (bf16[256,2560]{1,0:T(8,128)(2,1)S(1)}, bf16[256,2560]{1,0:T(8,128)(2,1)S(1)}, u32[]{:S(2)}, u32[]{:S(2)}) collective-permute-start(bf16[256,2560]{1,0:T(8,128)(2,1)S(1)} %pad_maximum_fusion.6), channel_id=1, source_target_pairs={{0,4},{2,6},{4,0},{6,2},{1,5},{3,7},{5,1},{7,3},{8,12},{10,14},{12... | collective-permute-start | bytes 3932168 | tf_op jit(solution)/shard_map/ppermute | solution.py:287
  214.5 55.0 %collective-permute-start.8 = (bf16[256,2560]{1,0:T(8,128)(2,1)S(1)}, bf16[256,2560]{1,0:T(8,128)(2,1)S(1)}, u32[]{:S(2)}, u32[]{:S(2)}) collective-permute-start(bf16[256,2560]{1,0:T(8,128)(2,1)S(1)} %pad_maximum_fusion.5), channel_id=1, source_target_pairs={{0,2},{2,0},{4,6},{6,4},{1,3},{3,1},{5,7},{7,5},{8,10},{10,8},{12,... | collective-permute-start | bytes 3932168 | tf_op jit(solution)/shard_map/ppermute | solution.py:287
  241.4 40.6 %collective-permute-start.17 = (bf16[128,2560]{1,0:T(8,128)(2,1)S(1)}, bf16[128,2560]{1,0:T(8,128)(2,1)S(1)}, u32[]{:S(2)}, u32[]{:S(2)}) collective-permute-start(bf16[128,2560]{1,0:T(8,128)(2,1)S(1)} %slice.471), channel_id=1, source_target_pairs={{0,4},{2,6},{4,0},{6,2},{1,5},{3,7},{5,1},{7,3},{8,12},{10,14},{12... | collective-permute-start | bytes 1966088 | tf_op jit(solution)/shard_map/ppermute | solution.py:287
  242.1 41.4 %collective-permute-start.18 = (bf16[128,2560]{1,0:T(8,128)(2,1)S(1)}, bf16[128,2560]{1,0:T(8,128)(2,1)S(1)}, u32[]{:S(2)}, u32[]{:S(2)}) collective-permute-start(bf16[128,2560]{1,0:T(8,128)(2,1)S(1)} %slice.472), channel_id=1, source_target_pairs={{0,2},{2,0},{4,6},{6,4},{1,3},{3,1},{5,7},{7,5},{8,10},{10,8},{12,... | collective-permute-start | bytes 1966088 | tf_op jit(solution)/shard_map/ppermute | solution.py:287
  273.3 36.8 %collective-permute-start.11 = (bf16[256,2560]{1,0:T(8,128)(2,1)S(1)}, bf16[256,2560]{1,0:T(8,128)(2,1)S(1)}, u32[]{:S(2)}, u32[]{:S(2)}) collective-permute-start(bf16[256,2560]{1,0:T(8,128)(2,1)S(1)} %get-tuple-element.105), channel_id=1, source_target_pairs={{0,2},{2,0},{4,6},{6,4},{1,3},{3,1},{5,7},{7,5},{8,10},{10,8},{12,... | collective-permute-start | bytes 3932168 | tf_op jit(solution)/shard_map/ppermute | solution.py:287
  274.7 36.0 %collective-permute-start.12 = (bf16[256,2560]{1,0:T(8,128)(2,1)S(1)}, bf16[256,2560]{1,0:T(8,128)(2,1)S(1)}, u32[]{:S(2)}, u32[]{:S(2)}) collective-permute-start(bf16[256,2560]{1,0:T(8,128)(2,1)S(1)} %get-tuple-element.105), channel_id=1, source_target_pairs={{0,4},{2,6},{4,0},{6,2},{1,5},{3,7},{5,1},{7,3},{8,12},{10,14},{12... | collective-permute-start | bytes 3932168 | tf_op jit(solution)/shard_map/ppermute | solution.py:287
  310.2 15.4 %collective-permute-start.13 = (bf16[128,2560]{1,0:T(8,128)(2,1)S(1)}, bf16[128,2560]{1,0:T(8,128)(2,1)S(1)}, u32[]{:S(2)}, u32[]{:S(2)}) collective-permute-start(bf16[128,2560]{1,0:T(8,128)(2,1)S(1)} %slice.467), channel_id=1, source_target_pairs={{0,4},{2,6},{4,0},{6,2},{1,5},{3,7},{5,1},{7,3},{8,12},{10,14},{12... | collective-permute-start | bytes 1966088 | tf_op jit(solution)/shard_map/ppermute | solution.py:287
  310.8 15.6 %collective-permute-start.14 = (bf16[128,2560]{1,0:T(8,128)(2,1)S(1)}, bf16[128,2560]{1,0:T(8,128)(2,1)S(1)}, u32[]{:S(2)}, u32[]{:S(2)}) collective-permute-start(bf16[128,2560]{1,0:T(8,128)(2,1)S(1)} %slice.468), channel_id=1, source_target_pairs={{0,2},{2,0},{4,6},{6,4},{1,3},{3,1},{5,7},{7,5},{8,10},{10,8},{12,... | collective-permute-start | bytes 1966088 | tf_op jit(solution)/shard_map/ppermute | solution.py:287
  419.9 281.3 %reduce-scatter.10.cloned.1.call-start = ((), (), s32[]{:S(2)}) async-start(), calls=%async_computation.10 | async-start | bytes 20643840 | tf_op jit(solution)/shard_map/reduce_scatter | solution.py:383
  497.5 269.2 %reduce-scatter.12.cloned.1.call-start = ((), (), s32[]{:S(2)}) async-start(), calls=%async_computation.11 | async-start | bytes 3276800 | tf_op jit(solution)/shard_map/reduce_scatter | solution.py:466
  499.9 17.0 %collective-permute-start.19 = (bf16[128,2560]{1,0:T(8,128)(2,1)S(1)}, bf16[128,2560]{1,0:T(8,128)(2,1)S(1)}, u32[]{:S(2)}, u32[]{:S(2)}) collective-permute-start(bf16[128,2560]{1,0:T(8,128)(2,1)S(1)} %get-tuple-element.125), channel_id=1, source_target_pairs={{0,4},{2,6},{4,0},{6,2},{1,5},{3,7},{5,1},{7,3},{8,12},{10,14},{12... | collective-permute-start | bytes 1966088 | tf_op jit(solution)/shard_map/ppermute | solution.py:287
  501.3 16.7 %collective-permute-start.21 = (bf16[128,2560]{1,0:T(8,128)(2,1)S(1)}, bf16[128,2560]{1,0:T(8,128)(2,1)S(1)}, u32[]{:S(2)}, u32[]{:S(2)}) collective-permute-start(bf16[128,2560]{1,0:T(8,128)(2,1)S(1)} %get-tuple-element.124), channel_id=1, source_target_pairs={{0,2},{2,0},{4,6},{6,4},{1,3},{3,1},{5,7},{7,5},{8,10},{10,8},{12,... | collective-permute-start | bytes 1966088 | tf_op jit(solution)/shard_map/ppermute | solution.py:287
  520.7 30.2 %collective-permute-start.22 = (bf16[256,2560]{1,0:T(8,128)(2,1)}, bf16[256,2560]{1,0:T(8,128)(2,1)}, u32[]{:S(2)}, u32[]{:S(2)}) collective-permute-start(bf16[256,2560]{1,0:T(8,128)(2,1)} %pad_maximum_fusion.8), channel_id=1, source_target_pairs={{0,4},{2,6},{4,0},{6,2},{1,5},{3,7},{5,1},{7,3},{8,12},{10,14},{12... | collective-permute-start | bytes 3932168 | tf_op jit(solution)/shard_map/ppermute | solution.py:287
  522.5 29.9 %collective-permute-start.20 = (bf16[256,2560]{1,0:T(8,128)(2,1)}, bf16[256,2560]{1,0:T(8,128)(2,1)}, u32[]{:S(2)}, u32[]{:S(2)}) collective-permute-start(bf16[256,2560]{1,0:T(8,128)(2,1)} %pad_maximum_fusion.7), channel_id=1, source_target_pairs={{0,2},{2,0},{4,6},{6,4},{1,3},{3,1},{5,7},{7,5},{8,10},{10,8},{12,... | collective-permute-start | bytes 3932168 | tf_op jit(solution)/shard_map/ppermute | solution.py:287
  562.5 28.6 %collective-permute-start.23 = (bf16[256,2560]{1,0:T(8,128)(2,1)S(1)}, bf16[256,2560]{1,0:T(8,128)(2,1)S(1)}, u32[]{:S(2)}, u32[]{:S(2)}) collective-permute-start(bf16[256,2560]{1,0:T(8,128)(2,1)S(1)} %get-tuple-element.103), channel_id=1, source_target_pairs={{0,2},{2,0},{4,6},{6,4},{1,3},{3,1},{5,7},{7,5},{8,10},{10,8},{12,... | collective-permute-start | bytes 3932168 | tf_op jit(solution)/shard_map/ppermute | solution.py:287
  563.9 29.8 %collective-permute-start.24 = (bf16[256,2560]{1,0:T(8,128)(2,1)S(1)}, bf16[256,2560]{1,0:T(8,128)(2,1)S(1)}, u32[]{:S(2)}, u32[]{:S(2)}) collective-permute-start(bf16[256,2560]{1,0:T(8,128)(2,1)S(1)} %get-tuple-element.103), channel_id=1, source_target_pairs={{0,4},{2,6},{4,0},{6,2},{1,5},{3,7},{5,1},{7,3},{8,12},{10,14},{12... | collective-permute-start | bytes 3932168 | tf_op jit(solution)/shard_map/ppermute | solution.py:287
  591.1 15.3 %collective-permute-start.25 = (bf16[128,2560]{1,0:T(8,128)(2,1)S(1)}, bf16[128,2560]{1,0:T(8,128)(2,1)S(1)}, u32[]{:S(2)}, u32[]{:S(2)}) collective-permute-start(bf16[128,2560]{1,0:T(8,128)(2,1)S(1)} %slice.473), channel_id=1, source_target_pairs={{0,4},{2,6},{4,0},{6,2},{1,5},{3,7},{5,1},{7,3},{8,12},{10,14},{12... | collective-permute-start | bytes 1966088 | tf_op jit(solution)/shard_map/ppermute | solution.py:287
  607.9 100.5 %collective-permute-start.31 = (bf16[128,2560]{1,0:T(8,128)(2,1)}, bf16[128,2560]{1,0:T(8,128)(2,1)}, u32[]{:S(2)}, u32[]{:S(2)}) collective-permute-start(bf16[128,2560]{1,0:T(8,128)(2,1)} %get-tuple-element.119), channel_id=1, source_target_pairs={{0,4},{2,6},{4,0},{6,2},{1,5},{3,7},{5,1},{7,3},{8,12},{10,14},{12... | collective-permute-start | bytes 1966088 | tf_op jit(solution)/shard_map/ppermute | solution.py:287
  609.3 99.1 %collective-permute-start.33 = (bf16[128,2560]{1,0:T(8,128)(2,1)}, bf16[128,2560]{1,0:T(8,128)(2,1)}, u32[]{:S(2)}, u32[]{:S(2)}) collective-permute-start(bf16[128,2560]{1,0:T(8,128)(2,1)} %get-tuple-element.118), channel_id=1, source_target_pairs={{0,2},{2,0},{4,6},{6,4},{1,3},{3,1},{5,7},{7,5},{8,10},{10,8},{12,... | collective-permute-start | bytes 1966088 | tf_op jit(solution)/shard_map/ppermute | solution.py:287
  701.2 155.9 %reduce-scatter.14.cloned.1.call-start = ((), (), s32[]{:S(2)}) async-start(), calls=%async_computation.12 | async-start | bytes 7372800 | tf_op jit(solution)/shard_map/reduce_scatter | solution.py:383
  711.7 35.3 %collective-permute-start.34 = (bf16[256,2560]{1,0:T(8,128)(2,1)}, bf16[256,2560]{1,0:T(8,128)(2,1)}, u32[]{:S(2)}, u32[]{:S(2)}) collective-permute-start(bf16[256,2560]{1,0:T(8,128)(2,1)} %pad_maximum_fusion.10), channel_id=1, source_target_pairs={{0,4},{2,6},{4,0},{6,2},{1,5},{3,7},{5,1},{7,3},{8,12},{10,14},{12... | collective-permute-start | bytes 3932168 | tf_op jit(solution)/shard_map/ppermute | solution.py:287
  714.3 33.3 %collective-permute-start.32 = (bf16[256,2560]{1,0:T(8,128)(2,1)}, bf16[256,2560]{1,0:T(8,128)(2,1)}, u32[]{:S(2)}, u32[]{:S(2)}) collective-permute-start(bf16[256,2560]{1,0:T(8,128)(2,1)} %pad_maximum_fusion.9), channel_id=1, source_target_pairs={{0,2},{2,0},{4,6},{6,4},{1,3},{3,1},{5,7},{7,5},{8,10},{10,8},{12,... | collective-permute-start | bytes 3932168 | tf_op jit(solution)/shard_map/ppermute | solution.py:287
  720.7 37.8 %collective-permute-start.30 = (bf16[80,3584]{1,0:T(8,128)(2,1)S(1)}, bf16[80,3584]{1,0:T(8,128)(2,1)S(1)}, u32[]{:S(2)}, u32[]{:S(2)}) collective-permute-start(bf16[80,3584]{1,0:T(8,128)(2,1)S(1)} %get-tuple-element.143), channel_id=1, source_target_pairs={{0,3},{1,7},{2,2},{3,6},{4,1},{5,5},{6,0},{7,4},{8,11},{9,15},{10,... | collective-permute-start | bytes 1720328 | tf_op jit(solution)/shard_map/ppermute | solution.py:408
  722.6 43.6 %collective-permute-start.29 = (bf16[80,3584]{1,0:T(8,128)(2,1)S(1)}, bf16[80,3584]{1,0:T(8,128)(2,1)S(1)}, u32[]{:S(2)}, u32[]{:S(2)}) collective-permute-start(bf16[80,3584]{1,0:T(8,128)(2,1)S(1)} %get-tuple-element.144), channel_id=1, source_target_pairs={{0,2},{1,6},{2,3},{3,7},{4,0},{5,4},{6,1},{7,5},{8,10},{9,14},{10,... | collective-permute-start | bytes 1720328 | tf_op jit(solution)/shard_map/ppermute | solution.py:408
  722.7 43.5 %collective-permute-start.28 = (bf16[80,3584]{1,0:T(8,128)(2,1)S(1)}, bf16[80,3584]{1,0:T(8,128)(2,1)S(1)}, u32[]{:S(2)}, u32[]{:S(2)}) collective-permute-start(bf16[80,3584]{1,0:T(8,128)(2,1)S(1)} %get-tuple-element.145), channel_id=1, source_target_pairs={{0,1},{1,5},{2,0},{3,4},{4,3},{5,7},{6,2},{7,6},{8,9},{9,13},{10,8... | collective-permute-start | bytes 1720328 | tf_op jit(solution)/shard_map/ppermute | solution.py:408
  747.0 19.2 %collective-permute-start.27 = (bf16[80,3584]{1,0:T(8,128)(2,1)S(1)}, bf16[80,3584]{1,0:T(8,128)(2,1)S(1)}, u32[]{:S(2)}, u32[]{:S(2)}) collective-permute-start(bf16[80,3584]{1,0:T(8,128)(2,1)S(1)} %get-tuple-element.142), channel_id=1, source_target_pairs={{0,0},{1,4},{2,1},{3,5},{4,2},{5,6},{6,3},{7,7},{8,8},{9,12},{10,9... | collective-permute-start | bytes 1720328 | tf_op jit(solution)/shard_map/ppermute | solution.py:408
  768.2 127.2 %reduce-scatter.16.cloned.1.call-start = ((), (), s32[]{:S(2)}) async-start(), calls=%async_computation.13 | async-start | bytes 2211840 | tf_op jit(solution)/shard_map/reduce_scatter | solution.py:383
  773.0 14.7 %collective-permute-start.49 = (bf16[80,1792]{1,0:T(8,128)(2,1)S(1)}, bf16[80,1792]{1,0:T(8,128)(2,1)S(1)}, u32[]{:S(2)}, u32[]{:S(2)}) collective-permute-start(bf16[80,1792]{1,0:T(8,128)(2,1)S(1)} %get-tuple-element.153), channel_id=1, source_target_pairs={{0,2},{1,6},{2,3},{3,7},{4,0},{5,4},{6,1},{7,5},{8,10},{9,14},{10,... | collective-permute-start | bytes 860168 | tf_op jit(solution)/shard_map/ppermute | solution.py:408
  801.1 17.4 %collective-permute-start.35 = (bf16[128,2560]{1,0:T(8,128)(2,1)S(1)}, bf16[128,2560]{1,0:T(8,128)(2,1)S(1)}, u32[]{:S(2)}, u32[]{:S(2)}) collective-permute-start(bf16[128,2560]{1,0:T(8,128)(2,1)S(1)} %get-tuple-element.113), channel_id=1, source_target_pairs={{0,4},{2,6},{4,0},{6,2},{1,5},{3,7},{5,1},{7,3},{8,12},{10,14},{12... | collective-permute-start | bytes 1966088 | tf_op jit(solution)/shard_map/ppermute | solution.py:287
  801.8 16.7 %collective-permute-start.37 = (bf16[128,2560]{1,0:T(8,128)(2,1)S(1)}, bf16[128,2560]{1,0:T(8,128)(2,1)S(1)}, u32[]{:S(2)}, u32[]{:S(2)}) collective-permute-start(bf16[128,2560]{1,0:T(8,128)(2,1)S(1)} %get-tuple-element.112), channel_id=1, source_target_pairs={{0,2},{2,0},{4,6},{6,4},{1,3},{3,1},{5,7},{7,5},{8,10},{10,8},{12,... | collective-permute-start | bytes 1966088 | tf_op jit(solution)/shard_map/ppermute | solution.py:287
  818.9 31.8 %collective-permute-start.38 = (bf16[256,2560]{1,0:T(8,128)(2,1)S(1)}, bf16[256,2560]{1,0:T(8,128)(2,1)S(1)}, u32[]{:S(2)}, u32[]{:S(2)}) collective-permute-start(bf16[256,2560]{1,0:T(8,128)(2,1)S(1)} %pad_maximum_fusion.12), channel_id=1, source_target_pairs={{0,4},{2,6},{4,0},{6,2},{1,5},{3,7},{5,1},{7,3},{8,12},{10,14},{12... | collective-permute-start | bytes 3932168 | tf_op jit(solution)/shard_map/ppermute | solution.py:287
  821.2 30.8 %collective-permute-start.36 = (bf16[256,2560]{1,0:T(8,128)(2,1)S(1)}, bf16[256,2560]{1,0:T(8,128)(2,1)S(1)}, u32[]{:S(2)}, u32[]{:S(2)}) collective-permute-start(bf16[256,2560]{1,0:T(8,128)(2,1)S(1)} %pad_maximum_fusion.11), channel_id=1, source_target_pairs={{0,2},{2,0},{4,6},{6,4},{1,3},{3,1},{5,7},{7,5},{8,10},{10,8},{12,... | collective-permute-start | bytes 3932168 | tf_op jit(solution)/shard_map/ppermute | solution.py:287
  (59 other events, 1119.0 us)
Sparse Core Ops, SparseCore 0:
  14.0 85.8 all-gather.4
  112.6 53.2 all-gather.6
  168.2 162.7 all-gather.8
  333.0 86.7 all-gather.10
  422.0 95.4 reduce-scatter.7
  519.8 181.3 reduce-scatter.9
  703.5 50.4 reduce-scatter.11
  768.3 73.5 reduce-scatter.13
  859.6 35.7 reduce-scatter.15

commit v3 on v2

--- a/solution.py
+++ b/solution.py
@@ -204,34 +204,44 @@
     grad_query_ref[...] = query_rows_ref[...].T.astype(jnp.bfloat16)
 
 
-def attend_back(query, kv_all, limits, totals, mixed, grad_mixed, cosine, sine, repeats):
+def attend_back(before, blocks, operands, repeats):
+    query, kv_all, limits, _, _, grad_mixed, _, _ = operands
     query_width, tokens = query.shape
     groups, kv_rows, _ = kv_all.shape
-    chips, _, block = limits.shape
+    _, _, block = limits.shape
     heads = query_width // HEAD_DIM
-    pairs = query_width * tokens * groups * block
-    by_column = pl.BlockSpec((query_width, block), lambda i: (0, i))
-    by_row = pl.BlockSpec((block, query_width), lambda i: (i, 0))
-    by_key = pl.BlockSpec((groups, kv_rows, block), lambda i: (0, 0, i))
-    table = pl.BlockSpec((HALF, block), lambda i: (0, i))
+    start, end = blocks
+    pairs = query_width * (end - start) * block * groups * block
+    by_column = pl.BlockSpec((query_width, block), lambda i: (0, i + start))
+    by_row = pl.BlockSpec((block, query_width), lambda i: (i + start, 0))
+    by_key = pl.BlockSpec((groups, kv_rows, block), lambda i: (0, 0, i + start))
+    table = pl.BlockSpec((HALF, block), lambda i: (0, i + start))
+    kept = () if before is None else tuple(before)
+
+    def kernel(*refs):
+        count = len(operands)
+        attend_back_kernel(repeats, *refs[:count], *refs[count + len(kept) :])
+
     return pl.pallas_call(
-        lambda *refs: attend_back_kernel(repeats, *refs),
+        kernel,
         out_shape=(
             jax.ShapeDtypeStruct((tokens, query_width), jnp.bfloat16),
             jax.ShapeDtypeStruct(kv_all.shape, jnp.bfloat16),
         ),
-        grid=(chips,),
+        grid=(end - start,),
         in_specs=[
             by_column,
             by_key,
-            pl.BlockSpec((1, 1, block), lambda i: (i, 0, 0)),
-            pl.BlockSpec((1, heads, block), lambda i: (i, 0, 0)),
+            pl.BlockSpec((1, 1, block), lambda i: (i + start, 0, 0)),
+            pl.BlockSpec((1, heads, block), lambda i: (i + start, 0, 0)),
             by_row,
-            by_row,
+            pl.BlockSpec((block, query_width), lambda i: (i, 0)),
             table,
             table,
-        ],
+        ]
+        + [pl.BlockSpec(memory_space=pl.ANY)] * len(kept),
         out_specs=(by_row, by_key),
+        input_output_aliases={len(operands) + at: at for at in range(len(kept))},
         scratch_shapes=[
             pltpu.VMEM((query_width, block), jnp.float32),
             pltpu.VMEM((query_width, block), jnp.float32),
@@ -241,11 +251,11 @@
         ],
         cost_estimate=pl.CostEstimate(
             flops=10 * pairs,
-            bytes_accessed=2 * (4 * query.size + 2 * kv_all.size),
+            bytes_accessed=2 * (end - start) * (4 * query.size + 2 * kv_all.size) // CHIPS,
             transcendentals=pairs // HEAD_DIM,
         ),
         name="attend_back",
-    )(query, kv_all, limits, totals, mixed, grad_mixed, cosine, sine)
+    )(*operands, *kept)
 
 
 def times(left, right):
@@ -296,21 +306,33 @@
     return [block, first, second, jnp.concatenate([low, high], axis=0)]
 
 
-def give_back(total):
+def give_back(left, right):
+    return given(left, right, *to_give(left, right))
+
+
+def to_give(left, right):
     low_type, wide_type = jnp.bfloat16, jnp.float32
-    own, first, second, third = jnp.split(total, CHIPS)
-    half = own.shape[0] // 2
+    block = left.shape[0] // CHIPS
+    half = block // 2
+    third = times_t(left[3 * block :], right).astype(low_type)
     low = swap(third[:half], 1).astype(wide_type)
     high = swap(third[half:], 2).astype(wide_type)
+    between = times_t(left[block : 3 * block], right).astype(low_type)
+    first, second = between[:block], between[block:]
     for_first = jnp.concatenate(
         [first[:half], (first[half:].astype(wide_type) + high).astype(low_type)], axis=0
     )
     for_second = jnp.concatenate(
         [(second[:half].astype(wide_type) + low).astype(low_type), second[half:]], axis=0
     )
-    from_first = swap(for_first, 1).astype(wide_type)
-    from_second = swap(for_second, 2).astype(wide_type)
-    return own.astype(wide_type) + from_first + from_second
+    return for_first, for_second
+
+
+def given(left, right, for_first, for_second):
+    block = left.shape[0] // CHIPS
+    from_first = swap(for_first, 1).astype(jnp.float32)
+    from_second = swap(for_second, 2).astype(jnp.float32)
+    return times_t(left[:block], right) + from_first + from_second
 
 
 def shards(
@@ -421,13 +443,20 @@
     limits = limits[:, None, :]
     mixed_low, log_totals = attend(query_rot, kv_all, limits, repeats)
 
-    def parts(left, right):
-        return times_t(left, right).astype(jnp.bfloat16)
+    def from_group(values):
+        return [
+            lax.ppermute(
+                lax.dynamic_index_in_dim(values, group_at ^ step, axis=0, keepdims=False),
+                "group",
+                [(at, at ^ step) for at in range(groups)],
+            )
+            for step in range(1, groups)
+        ]
 
     source = source_low.astype(jnp.float32)
     inverse_one = inverse_rms(source)
     unit_one = source * inverse_one
-    middle = source + give_back(parts(mixed_low, w_mix))
+    middle = source + give_back(mixed_low, w_mix)
     inverse_two = inverse_rms(middle)
     unit_two = middle * inverse_two
     normed_two = jnp.concatenate(collect((unit_two * gain_two).astype(jnp.bfloat16)), axis=0)
@@ -446,80 +475,105 @@
     ).astype(jnp.bfloat16)
     grad_lift_low = (grad_hidden * activated).astype(jnp.bfloat16)
     grad_both = jnp.concatenate([grad_gate_low, grad_lift_low], axis=1)
-    grad_parts, grad_both = then((parts(grad_both, w_lift), grad_both))
-    sum_lift = reduced(product_low(normed_two, grad_both))
-    grad_normed_two = give_back(grad_parts)
-    grad_normed_two, sum_down = then((grad_normed_two, sum_down))
-    grad_gain_two = jnp.sum(grad_normed_two * unit_two, axis=0)
+    grad_normed_two = give_back(grad_both, w_lift)
+    total_lift = product_low(normed_two, grad_both)
+    grad_normed_two, sum_down, total_lift = then((grad_normed_two, sum_down, total_lift))
+    sum_lift = reduced(total_lift)
     grad_middle = out_grad[0].astype(jnp.float32) + norm_back(
         grad_normed_two, middle, inverse_two, gain_two
     )
-    hidden, grad_middle = then((hidden, grad_middle))
-    grad_middle_low = jnp.concatenate(collect(grad_middle.astype(jnp.bfloat16)), axis=0)
-    sink_parts, grad_middle_low = then((parts(hidden, w_sink), grad_middle_low))
-    output_full = middle + give_back(sink_parts)
-    grad_mixed_low = times(grad_middle_low, w_mix).astype(jnp.bfloat16)
-    grad_query_low, grad_kv = attend_back(
-        query_rot, kv_all, limits, log_totals, mixed_low, grad_mixed_low, cosine, sine, repeats
-    )
-    grad_kv, sum_lift = then((grad_kv.reshape(groups * 2 * kv_width, tokens), sum_lift))
-    grad_kv = lax.psum_scatter(grad_kv, "group", scatter_dimension=0, tiled=True)
+    grad_blocks = collect(grad_middle.astype(jnp.bfloat16))
+    grads = None
+    for blocks in ((0, 1), (1, 3), (3, 4)):
+        if blocks[0] == 1:
+            hidden, grads = then((hidden, grads))
+            sink_out = to_give(hidden, w_sink)
+        if blocks[0] == 3:
+            sink_out, grad_blocks[3] = then((sink_out, grad_blocks[3]))
+        grad_rows = jnp.concatenate(grad_blocks[slice(*blocks)], axis=0)
+        grad_mixed_low = times(grad_rows, w_mix).astype(jnp.bfloat16)
+        grads = attend_back(
+            grads,
+            blocks,
+            (query_rot, kv_all, limits, log_totals, mixed_low, grad_mixed_low, cosine, sine),
+            repeats,
+        )
+    grad_query_low, grad_kv = grads
+    grad_middle_low = jnp.concatenate(grad_blocks, axis=0)
+    output_full = middle + given(hidden, w_sink, *sink_out)
+    grad_kv, sum_down = then((grad_kv, sum_down))
+    squares = jnp.stack(
+        [jnp.sum(source * source), jnp.sum(middle * middle), jnp.sum(output_full * output_full)]
+    )
+    place = core * spread + spread_at
+    extra = jnp.where(jnp.arange(2 * spread)[:, None] == place, squares[None, :], 0.0)
+    spare = -2 * kv_width % 128
+    assert spare >= extra.size
+    extra = jnp.pad(extra.reshape(1, -1), ((0, 0), (0, spare - extra.size)))
+    extra = jnp.broadcast_to(extra, (model_width, spare)).astype(jnp.bfloat16)
+    grad_kv_own = lax.dynamic_index_in_dim(grad_kv, group_at, axis=0, keepdims=False)
+    grad_kv_others = from_group(grad_kv)
+    attn_totals = with_layout_constraint(
+        jnp.concatenate(
+            [
+                product_low(normed_one, grad_query_low),
+                product_low(grad_middle_low, mixed_low),
+                jnp.zeros((model_width, 2 * kv_width + spare), jnp.bfloat16),
+            ],
+            axis=1,
+        ),
+        Layout(major_to_minor=(0, 1)),
+    )
     grad_down = laid(owned(sum_down), 0, wide)
+    grad_kv_others[1], attn_totals, grad_down, extra = then(
+        (grad_kv_others[1], attn_totals, grad_down, extra)
+    )
+    grad_kv = grad_kv_own.astype(jnp.float32)
+    for part in grad_kv_others:
+        grad_kv = grad_kv + part.astype(jnp.float32)
+    grad_key = unrotate(grad_kv[:kv_width], cosine, sine)
+    grad_kv_low = jnp.concatenate([grad_key, grad_kv[kv_width:]], axis=0).astype(jnp.bfloat16).T
+    total_kv = jnp.concatenate([product_low(normed_one, grad_kv_low), extra], axis=1)
+    attn_totals = lax.dynamic_update_slice(attn_totals, total_kv, (0, 2 * query_width))
+    attn_totals, grad_query_low, sum_lift = then((attn_totals, grad_query_low, sum_lift))
+    attn_sums = reduced(attn_totals)
+    added = give_back(jnp.concatenate([grad_query_low, grad_kv_low], axis=1), w_qkv)
+    input_grad = grad_middle + norm_back(added, source, inverse_one, gain_one)
+    added, sum_lift = then((added, sum_lift))
     lift_parts = owned(sum_lift)
     grad_gate, grad_up = laid(lift_parts, 0, wide), laid(lift_parts, wide, wide)
-    grad_kv, lift_parts, output_full = then((grad_kv, lift_parts, output_full))
-    grad_key = unrotate(grad_kv[:kv_width].astype(jnp.float32), cosine, sine)
-    grad_kv_low = jnp.concatenate([grad_key.astype(jnp.bfloat16), grad_kv[kv_width:]], axis=0).T
-    total_query = product_low(normed_one, grad_query_low)
-    total_out = product_low(grad_middle_low, mixed_low)
-    both_totals = with_layout_constraint(
-        jnp.concatenate([total_query, total_out], axis=1), Layout(major_to_minor=(0, 1))
-    )
-    both_totals, grad_kv_low = then((both_totals, grad_kv_low))
-    both_sums = reduced(both_totals)
-    added_query = times_t(grad_query_low, w_qkv[:, :query_width])
-    added = added_query + times_t(grad_kv_low, w_qkv[:, query_width:])
-    added = give_back(added.astype(jnp.bfloat16))
-    grad_gain_one = jnp.sum(added * unit_one, axis=0)
-    input_grad = grad_middle + norm_back(added, source, inverse_one, gain_one)
-    squares = jnp.stack(
-        [jnp.sum(source * source), jnp.sum(middle * middle), jnp.sum(output_full * output_full)]
-    )
-    place = core * spread + spread_at
-    apart = jnp.where(jnp.arange(2 * spread)[:, None] == place, squares[None, :], 0.0)
-    apart = apart.reshape(1, -1)
-    extra = jnp.concatenate(
-        [
-            grad_gain_one[:, None],
-            grad_gain_two[:, None],
-            jnp.broadcast_to(apart, (model_width, apart.shape[1])),
-        ],
-        axis=1,
-    ).astype(jnp.bfloat16)
-    kv_totals = jnp.concatenate([product_low(normed_one, grad_kv_low), extra], axis=1)
-    kv_totals, both_sums = then((kv_totals, both_sums))
-    kv_sums = reduced(kv_totals)
+    attn_parts = owned(attn_sums[:, :-spare])
     square_totals = lax.dynamic_slice(
-        kv_sums[:1, 2 * kv_width + 2 :].astype(jnp.float32), (0, place * 3), (1, 3)
+        attn_sums[:1, -spare:].astype(jnp.float32), (0, place * 3), (1, 3)
     )
     stream_rms = jnp.sqrt(square_totals / (full_len * model_width))
-
-    both_parts = owned(both_sums)
-    grad_query = laid(both_parts, 0, query_width)
-    grad_out = laid(both_parts, query_width, query_width)
-    kv_parts = owned(kv_sums[:, : 2 * kv_width + 2])
-    grad_key, grad_value = laid(kv_parts, 0, kv_width), laid(kv_parts, kv_width, kv_width)
-    gains_owned = sum(part[:, 2 * kv_width :].astype(jnp.float32) for part in kv_parts)
+    grad_query, grad_out = (laid(attn_parts, at * query_width, query_width) for at in range(2))
+    grad_key, grad_value = (
+        laid(attn_parts, 2 * query_width + at * kv_width, kv_width) for at in range(2)
+    )
+
+    def gain_grad(gain, *pairs):
+        rows = pairs[0][1].shape[0]
+        total = 0.0
+        for weight, grad in pairs:
+            weight = lax.dynamic_slice(weight, (whose * rows, 0), (rows, weight.shape[1]))
+            total = total + jnp.sum(weight.astype(jnp.float32) * grad, axis=1)
+        return total / lax.dynamic_slice(gain, (whose * rows,), (rows,)).astype(jnp.float32)
+
+    grad_norm_mlp = gain_grad(gain_mlp, (w_gate, grad_gate), (w_up, grad_up))
+    grad_norm_attn = gain_grad(
+        gain_attn, (w_query, grad_query), (w_key, grad_key), (w_value, grad_value)
+    )
 
     return (
         output_full.astype(jnp.bfloat16)[None],
         input_grad[None],
-        gains_owned[:, 0],
+        grad_norm_attn,
         grad_query,
         grad_key,
         grad_value,
         grad_out,
-        gains_owned[:, 1],
+        grad_norm_mlp,
         grad_gate,
         grad_up,
         grad_down,

time: 924 us -> 904 us (0.978)
  waiting for transfers between devices: 456 us -> 371 us
  matrix products: 180 us -> 223 us
    ppermute x35, waiting for transfers between devices: 266 us -> 156 us  [swap(): return lax.ppermute(value, 'chip', pairs)]
    reduce_scatter x4 -> x3, waiting for transfers between devices: 56.2 us -> 18.6 us  [reduced(): return lax.psum_scatter(total, SUM_AXES, scatter_dimension=0, tiled=True)]
    ppermute x0 -> x3, waiting for transfers between devices: none -> 35.8 us  [from_group(): lax.ppermute(lax.dynamic_index_in_dim(values, group_at ^ step, axis=0, ke...]
    dot_general x5 -> x12, matrix products: 54.5 us -> 87.3 us  [times_t(): lax.dot_general(left, right, (((1,), (1,)), ((), ())), preferred_element_...]
    all_gather x3, waiting for transfers between devices: 75.2 us -> 105 us  [gathered(): return lax.all_gather(part, ('group', 'core'), axis=0, tiled=True)]
    reduce_sum x3 -> x8, other arithmetic: 8.21 us -> 18.3 us  [the longest x5 9.33 us: gain_grad(): total = total + jnp.sum(weight.astype(jnp.float32) * grad, axis=1)]
    dot_general x3 -> x5, matrix products: 56.3 us -> 62.8 us  [times(): return jnp.dot(left, right, preferred_element_type=jnp.float32)]
    pallas_call x1 -> x3, Pallas kernels: 40.3 us -> 45.6 us  [attend_back(): pl.pallas_call(kernel, out_shape=(jax.ShapeDtypeStruct((tokens, query_wid...]
  transfers between devices with their start and end apart: 60 -> 57, of which waited for: 37 -> 33; matrix products, arithmetic and copies ran while one was open for 28% -> 35% of each run, Pallas kernels for 7% -> 8%
where the time goes in v3:
time: 904 us; the launch traced here: 889 us
  waiting for transfers between devices  371 us (41%)
  matrix products  223 us (25%)
  other arithmetic  75.6 us (8%)
  starting transfers between devices  69.3 us (8%)
  Pallas kernels  67 us (7%)
  local copies, waits for them, and re-layouts  49.5 us (5%)
  between operations  21 us (2%)
  blocking collectives  13.4 us (1%)
    ppermute x35, waiting for transfers between devices, swap(): return lax.ppermute(value, 'chip', pairs)  156 us
    all_gather x3, waiting for transfers between devices, gathered(): return lax.all_gather(part, ('group', 'core'), axis=0, tiled=True)  105 us
    dot_general x12, matrix products, times_t(): lax.dot_general(left, right, (((1,), (1,)), ((), ())), preferred_element_...  87.3 us
    dot_general x5, matrix products, inner_t(): lax.dot_general(left, right, (((0,), (0,)), ((), ())), preferred_element_...  63.5 us
    dot_general x5, matrix products, times(): return jnp.dot(left, right, preferred_element_type=jnp.float32)  62.8 us
    pallas_call x3, Pallas kernels, attend_back(): pl.pallas_call(kernel, out_shape=(jax.ShapeDtypeStruct((tokens, query_wid...  45.6 us
    ppermute x35, starting transfers between devices, swap(): return lax.ppermute(value, 'chip', pairs)  44.2 us
    ppermute x3, waiting for transfers between devices, from_group(): lax.ppermute(lax.dynamic_index_in_dim(values, group_at ^ step, axis=0, ke...  35.8 us
  transfers between devices with their start and end apart: 57, of which 33 were waited for; matrix products, arithmetic and copies ran while one was open for 35% of the time, Pallas kernels for 8%

profile of v3, /device:TPU:0, one launch (start us, length us, event | category | flops | bytes accessed | tf_op | source)
XLA Modules:
  0.0 889.5 jit_solution(17252388129879255289)
XLA Ops:
  22.0 13.4 %all_gather.16 = bf16[2,2560]{1,0:T(2,128)(2,1)S(1)} all-gather(bf16[2,640]{1,0:T(2,128)(2,1)S(1)} %pad_maximum_fusion.23), channel_id=1, replica_groups=mesh['group'=4,'dp'=1,'chip'=4,'core'=2] {'group'}, dimensions={1}, use_global_device_ids=true | all-gather | bytes 12800 | tf_op jit(solution)/shard_map/all_gather | solution.py:375
  35.6 11.5 %collective-permute-done.6 = s32[258]{0:T(512)S(1)} collective-permute-done((s32[258]{0:T(512)S(1)}, s32[258]{0:T(512)S(1)}, u32[]{:S(2)}, u32[]{:S(2)}) %collective-permute-start.6) | collective-permute-done | bytes 1064 | tf_op jit(solution)/shard_map/ppermute | solution.py:297
  50.4 13.1 %collective-permute-done.2 = bf16[128,2560]{1,0:T(8,128)(2,1)S(1)} collective-permute-done((bf16[128,2560]{1,0:T(8,128)(2,1)S(1)}, bf16[128,2560]{1,0:T(8,128)(2,1)S(1)}, u32[]{:S(2)}, u32[]{:S(2)}) %collective-permute-start.2) | collective-permute-done | bytes 655392 | tf_op jit(solution)/shard_map/ppermute | solution.py:297
  67.1 32.8 %all-gather.5.cloned.1.call-done = bf16[2560,1600]{1,0:T(8,128)(2,1)} async-done(((bf16[320,1600]{1,0:T(8,128)(2,1)}), bf16[2560,1600]{1,0:T(8,128)(2,1)}) %all-gather.5.cloned.1.call-update) | async-done | bytes 8192016 | tf_op jit(solution)/shard_map/all_gather | solution.py:373
  99.9 9.5 %fusion.20 = f32[960,1024]{1,0:T(8,128)S(1)} fusion(bf16[2560,1600]{1,0:T(8,128)(2,1)} %all-gather.5.cloned.1.call-done, bf16[1024,2560]{1,0:T(8,128)(2,1)} %copy-done.7, f32[2560]{0:T(1024)S(1)} %get-tuple-element.75, f32[1024]{0:T(1024)S(1)} %add_rsqrt_fusion), kind=kOutput, calls=%fused_computation.46 | convolution fusion | flops 5043650560 | bytes 14432256 | tf_op jit(solution)/shard_map/dot_general | solution.py:393
  138.4 27.4 %all-gather.7.cloned.1.call-done = bf16[1280,1024]{1,0:T(8,128)(2,1)} async-done(((bf16[320,1024]{1,0:T(8,128)(2,1)}), bf16[1280,1024]{1,0:T(8,128)(2,1)}) %all-gather.7.cloned.1.call-update) | async-done | bytes 2621456 | tf_op jit(solution)/shard_map/all_gather | solution.py:401
  165.8 21.4 %attend.1 = (bf16[1024,640]{1,0:T(8,128)(2,1)}, f32[4,8,256]{2,1,0:T(8,128)}) custom-call(bf16[640,1024]{1,0:T(8,128)(2,1)} %bitcast.137, bf16[4,320,1024]{2,1,0:T(8,128)(2,1)} %bitcast.147, s32[4,1,256]{2,1,0:T(1,128)} %broadcast_in_dim.39.refs_2_), custom_call_target="tpu_custom_call" | custom-call | flops 2684354560 | bytes 5242880 | tf_op jit(solution)/shard_map/attend/pallas_call | solution.py:100
  194.0 4.6 convolution_convert_fusion.6
  198.7 8.8 collective-permute-done.7
  215.9 25.0 %collective-permute-done.10 = bf16[256,2560]{1,0:T(8,128)(2,1)S(1)} collective-permute-done((bf16[256,2560]{1,0:T(8,128)(2,1)S(1)}, bf16[256,2560]{1,0:T(8,128)(2,1)S(1)}, u32[]{:S(2)}, u32[]{:S(2)}) %collective-permute-start.10) | collective-permute-done | bytes 1310752 | tf_op jit(solution)/shard_map/ppermute | solution.py:297
  241.6 4.2 multiply_reduce_fusion.3
  255.7 25.5 %collective-permute-done.11 = bf16[256,2560]{1,0:T(8,128)(2,1)S(1)} collective-permute-done((bf16[256,2560]{1,0:T(8,128)(2,1)S(1)}, bf16[256,2560]{1,0:T(8,128)(2,1)S(1)}, u32[]{:S(2)}, u32[]{:S(2)}) %collective-permute-start.11) | collective-permute-done | bytes 1310752 | tf_op jit(solution)/shard_map/ppermute | solution.py:297
  286.6 8.9 %collective-permute-done.13 = bf16[128,2560]{1,0:T(8,128)(2,1)S(1)} collective-permute-done((bf16[128,2560]{1,0:T(8,128)(2,1)S(1)}, bf16[128,2560]{1,0:T(8,128)(2,1)S(1)}, u32[]{:S(2)}, u32[]{:S(2)}) %collective-permute-start.13) | collective-permute-done | bytes 655392 | tf_op jit(solution)/shard_map/ppermute | solution.py:297
  297.6 33.2 %all-gather.9.cloned.1.call-done = bf16[2560,3584]{1,0:T(8,128)(2,1)} async-done(((bf16[320,3584]{1,0:T(8,128)(2,1)}), bf16[2560,3584]{1,0:T(8,128)(2,1)}) %all-gather.9.cloned.1.call-update) | async-done | bytes 18350096 | tf_op jit(solution)/shard_map/all_gather | solution.py:373
  330.8 27.6 %fusion.122 = f32[1024,3584]{1,0:T(8,128)} fusion(bf16[1024,2560]{1,0:T(8,128)(2,1)} %constant_dynamic-update-slice_fusion.5, bf16[2560,3584]{1,0:T(8,128)(2,1)} %all-gather.9.cloned.1.call-done), kind=kOutput, calls=%fused_computation.271 | convolution fusion | flops 18790481920 | bytes 38273024 | tf_op jit(solution)/shard_map/dot_general | solution.py:262
  358.4 6.4 multiply_convert_fusion.2
  366.6 13.8 %convolution_convert_fusion.1 = bf16[2560,1792]{1,0:T(8,128)(2,1)} fusion(bf16[1024,2560]{1,0:T(8,128)(2,1)} %copy-done.25, bf16[1024,1792]{1,0:T(8,128)(2,1)S(1)} %multiply_convert_fusion.2), kind=kOutput, calls=%fused_computation.3 | convolution fusion | flops 9399828480 | bytes 18087936 | tf_op jit(solution)/shard_map/dot_general | solution.py:272
  380.4 39.3 %all-gather.11.cloned.1.call-done = bf16[2560,1792]{1,0:T(8,128)(2,1)} async-done(((bf16[320,1792]{1,0:T(8,128)(2,1)}), bf16[2560,1792]{1,0:T(8,128)(2,1)}) %all-gather.11.cloned.1.call-update) | async-done | bytes 9175056 | tf_op jit(solution)/shard_map/all_gather | solution.py:373
  419.7 19.9 %multiply_convert_fusion = (bf16[1024,1792]{1,0:T(8,128)(2,1)S(1)}, bf16[1024,1792]{1,0:T(8,128)(2,1)S(1)}) fusion(f32[1024,3584]{1,0:T(8,128)} %fusion.122, bf16[1024,2560]{1,0:T(8,128)(2,1)} %copy-done.25, bf16[2560,1792]{1,0:T(8,128)(2,1)} %all-gather.11.cloned.1.call-done), kind=kOutput, calls=%fused_computation.13 | convolution fusion | flops 9417261056 | bytes 36438016 | tf_op jit(solution)/shard_map/dot_general | solution.py:262
  439.6 11.7 %convolution_convert_fusion.10 = bf16[256,2560]{1,0:T(8,128)(2,1)S(1)} fusion(bf16[2560,3584]{1,0:T(8,128)(2,1)} %all-gather.9.cloned.1.call-done, bf16[1024,1792]{1,0:T(8,128)(2,1)S(1)} %get-tuple-element.92, bf16[1024,1792]{1,0:T(8,128)(2,1)S(1)} %get-tuple-element.91), kind=kOutput, calls=%fused_computation.39 | convolution fusion | flops 4701945856 | bytes 27000832 | tf_op jit(solution)/shard_map/dot_general | solution.py:266
  454.5 14.6 %convolution_convert_fusion.3 = bf16[512,2560]{1,0:T(8,128)(2,1)S(1)} fusion(bf16[2560,3584]{1,0:T(8,128)(2,1)} %all-gather.9.cloned.1.call-done, bf16[1024,1792]{1,0:T(8,128)(2,1)} %copy-done.40, bf16[1024,1792]{1,0:T(8,128)(2,1)} %copy-done.39), kind=kOutput, calls=%fused_computation.32 | convolution fusion | flops 9403891712 | bytes 28311552 | tf_op jit(solution)/shard_map/dot_general | solution.py:266
  473.5 27.4 %convolution_convert_fusion = bf16[2560,3584]{1,0:T(8,128)(2,1)} fusion(bf16[1024,2560]{1,0:T(8,128)(2,1)} %constant_dynamic-update-slice_fusion.5, bf16[1024,1792]{1,0:T(8,128)(2,1)} %copy-done.39, bf16[1024,1792]{1,0:T(8,128)(2,1)} %copy-done.40), kind=kOutput, calls=%fused_computation | convolution fusion | flops 18814337024 | bytes 30932992 | tf_op jit(solution)/shard_map/dot_general | solution.py:272
  501.7 11.2 %convert_add_fusion.2 = f32[256,2560]{1,0:T(8,128)} fusion(bf16[256,2560]{1,0:T(8,128)(2,1)} %collective-permute-done.22, bf16[256,2560]{1,0:T(8,128)(2,1)} %collective-permute-done.20, bf16[2560,3584]{1,0:T(8,128)(2,1)} %all-gather.9.cloned.1.call-done, bf16[1024,1792]{1,0:T(8,128)(2,1)} %copy-done.39, bf16[1024,1792]{1,0:T(8,128)(2,1)} %copy-done.40), kind=kOutput, calls=%fused_computation.64 | convolution fusion | flops 4703911936 | bytes 30932992 | tf_op jit(solution)/shard_map/dot_general | solution.py:266
  512.9 4.5 reduce-scatter.4.cloned.1.call-done
  529.4 4.8 fusion.58.refs_5_
  534.1 11.8 %attend_back.3 = (bf16[1024,640]{1,0:T(8,128)(2,1)}, bf16[4,320,1024]{2,1,0:T(8,128)(2,1)}) custom-call(bf16[640,1024]{1,0:T(8,128)(2,1)} %bitcast.138, bf16[4,320,1024]{2,1,0:T(8,128)(2,1)} %bitcast.148, s32[4,1,256]{2,1,0:T(1,128)} %broadcast_in_dim.39.refs_2_, f32[4,8,256]{2,1,0:T(8,128)} %get-tuple-element.42.refs_3_, ...), custom_call_target="tpu_custom_call" | custom-call | flops 1677721600 | bytes 2621440 | tf_op jit(solution)/shard_map/attend_back/pallas_call | solution.py:225
  545.9 6.7 convolution_convert_fusion.9
  553.8 7.7 fusion.67
  561.5 8.9 convolution_convert_fusion.5
  580.1 6.2 fusion.42.refs_5_
  586.3 21.8 %attend_back.4 = (bf16[1024,640]{1,0:T(8,128)(2,1)}, bf16[4,320,1024]{2,1,0:T(8,128)(2,1)}) custom-call(bf16[640,1024]{1,0:T(8,128)(2,1)} %bitcast.139, bf16[4,320,1024]{2,1,0:T(8,128)(2,1)} %bitcast.149, s32[4,1,256]{2,1,0:T(1,128)} %broadcast_in_dim.39.refs_2_, ...), custom_call_target="tpu_custom_call", output_to_operand_aliasing={{0}: (8, {}), {1}: (9, {})} | custom-call | flops 3355443200 | bytes 5242880 | tf_op jit(solution)/shard_map/attend_back/pallas_call | solution.py:225
  609.7 4.5 fusion.61.refs_5_
  614.2 12.0 %attend_back.5 = (bf16[1024,640]{1,0:T(8,128)(2,1)}, bf16[4,320,1024]{2,1,0:T(8,128)(2,1)}) custom-call(bf16[640,1024]{1,0:T(8,128)(2,1)} %bitcast.140, bf16[4,320,1024]{2,1,0:T(8,128)(2,1)} %bitcast.150, s32[4,1,256]{2,1,0:T(1,128)} %broadcast_in_dim.39.refs_2_, ...), custom_call_target="tpu_custom_call", output_to_operand_aliasing={{0}: (8, {}), {1}: (9, {})} | custom-call | flops 1677721600 | bytes 2621440 | tf_op jit(solution)/shard_map/attend_back/pallas_call | solution.py:225
  637.5 9.4 %convolution_convert_fusion.2 = bf16[2560,640]{1,0:T(8,128)(2,1)} fusion(bf16[1024,640]{1,0:T(8,128)(2,1)} %get-tuple-element.65, bf16[1024,2560]{1,0:T(8,128)(2,1)} %copy-done.7, f32[2560]{0:T(1024)S(1)} %copy-done.29, f32[1024]{0:T(1024)S(1)} %copy-done.34), kind=kOutput, calls=%fused_computation.27 | convolution fusion | flops 3367567360 | bytes 9844736 | tf_op jit(solution)/shard_map/dot_general | solution.py:272
  646.9 7.2 fusion.11
  654.1 7.8 maximum_maximum_fusion
  671.6 23.7 %collective-permute-done.29 = bf16[256,2560]{1,0:T(8,128)(2,1)S(1)} collective-permute-done((bf16[256,2560]{1,0:T(8,128)(2,1)S(1)}, bf16[256,2560]{1,0:T(8,128)(2,1)S(1)}, u32[]{:S(2)}, u32[]{:S(2)}) %collective-permute-start.29) | collective-permute-done | bytes 1310752 | tf_op jit(solution)/shard_map/ppermute | solution.py:297
  701.4 32.4 %collective-permute-done.31 = bf16[320,1024]{1,0:T(8,128)(2,1)} collective-permute-done((bf16[320,1024]{1,0:T(8,128)(2,1)}, bf16[320,1024]{1,0:T(8,128)(2,1)}, u32[]{:S(2)}, u32[]{:S(2)}) %collective-permute-start.31) | collective-permute-done | bytes 655392 | tf_op jit(solution)/shard_map/ppermute | solution.py:448
  739.7 5.7 convolution_convert_fusion.7
  752.5 4.3 convolution_convert_fusion.8
  760.5 5.4 convolution_convert_fusion.4
  766.0 7.1 collective-permute-done.38
  777.6 4.2 fusion.18
  781.9 22.2 %collective-permute-done.41 = bf16[256,2560]{1,0:T(8,128)(2,1)} collective-permute-done((bf16[256,2560]{1,0:T(8,128)(2,1)S(1)}, bf16[256,2560]{1,0:T(8,128)(2,1)}, u32[]{:S(2)}, u32[]{:S(2)}) %collective-permute-start.41) | collective-permute-done | bytes 1310752 | tf_op jit(solution)/shard_map/ppermute | solution.py:297
  817.1 10.3 %collective-permute-done.49 = bf16[80,3584]{1,0:T(8,128)(2,1)S(1)} collective-permute-done((bf16[80,3584]{1,0:T(8,128)(2,1)S(1)}, bf16[80,3584]{1,0:T(8,128)(2,1)S(1)}, u32[]{:S(2)}, u32[]{:S(2)}) %collective-permute-start.49) | collective-permute-done | bytes 573472 | tf_op jit(solution)/shard_map/ppermute | solution.py:430
  827.4 9.5 %collective-permute-done.48 = bf16[80,3584]{1,0:T(8,128)(2,1)S(1)} collective-permute-done((bf16[80,3584]{1,0:T(8,128)(2,1)S(1)}, bf16[80,3584]{1,0:T(8,128)(2,1)S(1)}, u32[]{:S(2)}, u32[]{:S(2)}) %collective-permute-start.48) | collective-permute-done | bytes 573472 | tf_op jit(solution)/shard_map/ppermute | solution.py:430
  843.3 14.2 %reduce-scatter.8.cloned.1.call-done = bf16[320,1664]{1,0:T(8,128)(2,1)} async-done(((bf16[2560,1664]{1,0:T(8,128)(2,1)}), bf16[320,1664]{1,0:T(8,128)(2,1)}) %reduce-scatter.8.cloned.1.call-update) | async-done | bytes 1064976 | tf_op jit(solution)/shard_map/reduce_scatter | solution.py:405
  865.8 5.0 collective-permute-done.45
  (346 shorter events, 200.5 us)
Async XLA Ops:
  7.2 92.7 %all-gather.5.cloned.1.call-start = ((), (), s32[]{:S(2)}) async-start(), calls=%async_computation.3 | async-start | bytes 9584640 | tf_op jit(solution)/shard_map/all_gather | solution.py:373
  13.8 151.9 %all-gather.7.cloned.1.call-start = ((), (), s32[]{:S(2)}) async-start(), calls=%async_computation.4 | async-start | bytes 3276800 | tf_op jit(solution)/shard_map/all_gather | solution.py:401
  13.9 34.0 %collective-permute-start = (bf16[256,2560]{1,0:T(8,128)(2,1)S(1)}, bf16[256,2560]{1,0:T(8,128)(2,1)S(1)}, u32[]{:S(2)}, u32[]{:S(2)}) collective-permute-start(bf16[256,2560]{1,0:T(8,128)(2,1)S(1)} %bitcast.132), channel_id=1, source_target_pairs={{0,2},{2,0},{4,6},{6,4},{1,3},{3,1},{5,7},{7,5},{8,10},{10,8},{12,... | collective-permute-start | bytes 3932168 | tf_op jit(solution)/shard_map/ppermute | solution.py:297
  16.9 32.6 %collective-permute-start.1 = (bf16[256,2560]{1,0:T(8,128)(2,1)S(1)}, bf16[256,2560]{1,0:T(8,128)(2,1)S(1)}, u32[]{:S(2)}, u32[]{:S(2)}) collective-permute-start(bf16[256,2560]{1,0:T(8,128)(2,1)S(1)} %bitcast.133), channel_id=1, source_target_pairs={{0,4},{2,6},{4,0},{6,2},{1,5},{3,7},{5,1},{7,3},{8,12},{10,14},{12... | collective-permute-start | bytes 3932168 | tf_op jit(solution)/shard_map/ppermute | solution.py:297
  18.4 28.7 %collective-permute-start.6 = (s32[258]{0:T(512)S(1)}, s32[258]{0:T(512)S(1)}, u32[]{:S(2)}, u32[]{:S(2)}) collective-permute-start(s32[258]{0:T(512)S(1)} %pad_add_fusion.4), channel_id=1, source_target_pairs={{0,6},{2,4},{4,2},{6,0},{1,7},{3,5},{5,3},{7,1},{8,14},{10,12},{12... | collective-permute-start | bytes 3104 | tf_op jit(solution)/shard_map/ppermute | solution.py:297
  18.5 28.7 %collective-permute-start.5 = (s32[258]{0:T(512)S(1)}, s32[258]{0:T(512)S(1)}, u32[]{:S(2)}, u32[]{:S(2)}) collective-permute-start(s32[258]{0:T(512)S(1)} %pad_add_fusion.4), channel_id=1, source_target_pairs={{0,4},{2,6},{4,0},{6,2},{1,5},{3,7},{5,1},{7,3},{8,12},{10,14},{12... | collective-permute-start | bytes 3104 | tf_op jit(solution)/shard_map/ppermute | solution.py:297
  20.5 26.7 %collective-permute-start.4 = (s32[258]{0:T(512)S(1)}, s32[258]{0:T(512)S(1)}, u32[]{:S(2)}, u32[]{:S(2)}) collective-permute-start(s32[258]{0:T(512)S(1)} %pad_add_fusion.4), channel_id=1, source_target_pairs={{0,2},{2,0},{4,6},{6,4},{1,3},{3,1},{5,7},{7,5},{8,10},{10,8},{12,... | collective-permute-start | bytes 3104 | tf_op jit(solution)/shard_map/ppermute | solution.py:297
  112.3 218.5 %all-gather.9.cloned.1.call-start = ((), (), s32[]{:S(2)}) async-start(), calls=%async_computation.5 | async-start | bytes 20643840 | tf_op jit(solution)/shard_map/all_gather | solution.py:373
  115.6 304.1 %all-gather.11.cloned.1.call-start = ((), (), s32[]{:S(2)}) async-start(), calls=%async_computation.6 | async-start | bytes 10321920 | tf_op jit(solution)/shard_map/all_gather | solution.py:373
  115.9 95.6 %collective-permute-start.15 = (bf16[256,2560]{1,0:T(8,128)(2,1)S(1)}, bf16[256,2560]{1,0:T(8,128)(2,1)}, u32[]{:S(2)}, u32[]{:S(2)}) collective-permute-start(bf16[256,2560]{1,0:T(8,128)(2,1)S(1)} %bitcast.135), channel_id=1, source_target_pairs={{0,2},{2,0},{4,6},{6,4},{1,3},{3,1},{5,7},{7,5},{8,10},{10,8},{12,... | collective-permute-start | bytes 3932168 | tf_op jit(solution)/shard_map/ppermute | solution.py:297
  117.3 96.8 %collective-permute-start.16 = (bf16[256,2560]{1,0:T(8,128)(2,1)S(1)}, bf16[256,2560]{1,0:T(8,128)(2,1)}, u32[]{:S(2)}, u32[]{:S(2)}) collective-permute-start(bf16[256,2560]{1,0:T(8,128)(2,1)S(1)} %bitcast.136), channel_id=1, source_target_pairs={{0,4},{2,6},{4,0},{6,2},{1,5},{3,7},{5,1},{7,3},{8,12},{10,14},{12... | collective-permute-start | bytes 3932168 | tf_op jit(solution)/shard_map/ppermute | solution.py:297
  121.2 396.2 %reduce-scatter.4.cloned.1.call-start = ((), (), s32[]{:S(2)}) async-start(), calls=%async_computation.7 | async-start | bytes 10321920 | tf_op jit(solution)/shard_map/reduce_scatter | solution.py:405
  191.0 16.5 %collective-permute-start.7 = (bf16[128,2560]{1,0:T(8,128)(2,1)S(1)}, bf16[128,2560]{1,0:T(8,128)(2,1)S(1)}, u32[]{:S(2)}, u32[]{:S(2)}) collective-permute-start(bf16[128,2560]{1,0:T(8,128)(2,1)S(1)} %get-tuple-element.129), channel_id=1, source_target_pairs={{0,4},{2,6},{4,0},{6,2},{1,5},{3,7},{5,1},{7,3},{8,12},{10,14},{12... | collective-permute-start | bytes 1966088 | tf_op jit(solution)/shard_map/ppermute | solution.py:297
  192.5 16.2 %collective-permute-start.9 = (bf16[128,2560]{1,0:T(8,128)(2,1)S(1)}, bf16[128,2560]{1,0:T(8,128)(2,1)S(1)}, u32[]{:S(2)}, u32[]{:S(2)}) collective-permute-start(bf16[128,2560]{1,0:T(8,128)(2,1)S(1)} %get-tuple-element.130), channel_id=1, source_target_pairs={{0,2},{2,0},{4,6},{6,4},{1,3},{3,1},{5,7},{7,5},{8,10},{10,8},{12,... | collective-permute-start | bytes 1966088 | tf_op jit(solution)/shard_map/ppermute | solution.py:297
  209.1 31.8 %collective-permute-start.10 = (bf16[256,2560]{1,0:T(8,128)(2,1)S(1)}, bf16[256,2560]{1,0:T(8,128)(2,1)S(1)}, u32[]{:S(2)}, u32[]{:S(2)}) collective-permute-start(bf16[256,2560]{1,0:T(8,128)(2,1)S(1)} %pad_maximum_fusion.6), channel_id=1, source_target_pairs={{0,4},{2,6},{4,0},{6,2},{1,5},{3,7},{5,1},{7,3},{8,12},{10,14},{12... | collective-permute-start | bytes 3932168 | tf_op jit(solution)/shard_map/ppermute | solution.py:297
  209.8 31.8 %collective-permute-start.8 = (bf16[256,2560]{1,0:T(8,128)(2,1)S(1)}, bf16[256,2560]{1,0:T(8,128)(2,1)S(1)}, u32[]{:S(2)}, u32[]{:S(2)}) collective-permute-start(bf16[256,2560]{1,0:T(8,128)(2,1)S(1)} %pad_maximum_fusion.5), channel_id=1, source_target_pairs={{0,2},{2,0},{4,6},{6,4},{1,3},{3,1},{5,7},{7,5},{8,10},{10,8},{12,... | collective-permute-start | bytes 3932168 | tf_op jit(solution)/shard_map/ppermute | solution.py:297
  212.6 42.3 %collective-permute-start.17 = (bf16[128,2560]{1,0:T(8,128)(2,1)S(1)}, bf16[128,2560]{1,0:T(8,128)(2,1)S(1)}, u32[]{:S(2)}, u32[]{:S(2)}) collective-permute-start(bf16[128,2560]{1,0:T(8,128)(2,1)S(1)} %slice.486), channel_id=1, source_target_pairs={{0,4},{2,6},{4,0},{6,2},{1,5},{3,7},{5,1},{7,3},{8,12},{10,14},{12... | collective-permute-start | bytes 1966088 | tf_op jit(solution)/shard_map/ppermute | solution.py:297
  215.2 40.4 %collective-permute-start.18 = (bf16[128,2560]{1,0:T(8,128)(2,1)S(1)}, bf16[128,2560]{1,0:T(8,128)(2,1)S(1)}, u32[]{:S(2)}, u32[]{:S(2)}) collective-permute-start(bf16[128,2560]{1,0:T(8,128)(2,1)S(1)} %slice.487), channel_id=1, source_target_pairs={{0,2},{2,0},{4,6},{6,4},{1,3},{3,1},{5,7},{7,5},{8,10},{10,8},{12,... | collective-permute-start | bytes 1966088 | tf_op jit(solution)/shard_map/ppermute | solution.py:297
  247.7 33.4 %collective-permute-start.11 = (bf16[256,2560]{1,0:T(8,128)(2,1)S(1)}, bf16[256,2560]{1,0:T(8,128)(2,1)S(1)}, u32[]{:S(2)}, u32[]{:S(2)}) collective-permute-start(bf16[256,2560]{1,0:T(8,128)(2,1)S(1)} %get-tuple-element.90), channel_id=1, source_target_pairs={{0,2},{2,0},{4,6},{6,4},{1,3},{3,1},{5,7},{7,5},{8,10},{10,8},{12,... | collective-permute-start | bytes 3932168 | tf_op jit(solution)/shard_map/ppermute | solution.py:297
  249.2 33.5 %collective-permute-start.12 = (bf16[256,2560]{1,0:T(8,128)(2,1)S(1)}, bf16[256,2560]{1,0:T(8,128)(2,1)S(1)}, u32[]{:S(2)}, u32[]{:S(2)}) collective-permute-start(bf16[256,2560]{1,0:T(8,128)(2,1)S(1)} %get-tuple-element.90), channel_id=1, source_target_pairs={{0,4},{2,6},{4,0},{6,2},{1,5},{3,7},{5,1},{7,3},{8,12},{10,14},{12... | collective-permute-start | bytes 3932168 | tf_op jit(solution)/shard_map/ppermute | solution.py:297
  419.7 331.5 %reduce-scatter.6.cloned.1.call-start = ((), (), s32[]{:S(2)}) async-start(), calls=%async_computation.8 | async-start | bytes 20643840 | tf_op jit(solution)/shard_map/reduce_scatter | solution.py:405
  451.5 17.8 %collective-permute-start.19 = (bf16[128,2560]{1,0:T(8,128)(2,1)S(1)}, bf16[128,2560]{1,0:T(8,128)(2,1)S(1)}, u32[]{:S(2)}, u32[]{:S(2)}) collective-permute-start(bf16[128,2560]{1,0:T(8,128)(2,1)S(1)} %get-tuple-element.127), channel_id=1, source_target_pairs={{0,4},{2,6},{4,0},{6,2},{1,5},{3,7},{5,1},{7,3},{8,12},{10,14},{12... | collective-permute-start | bytes 1966088 | tf_op jit(solution)/shard_map/ppermute | solution.py:297
  453.0 16.7 %collective-permute-start.21 = (bf16[128,2560]{1,0:T(8,128)(2,1)S(1)}, bf16[128,2560]{1,0:T(8,128)(2,1)}, u32[]{:S(2)}, u32[]{:S(2)}) collective-permute-start(bf16[128,2560]{1,0:T(8,128)(2,1)S(1)} %get-tuple-element.128), channel_id=1, source_target_pairs={{0,2},{2,0},{4,6},{6,4},{1,3},{3,1},{5,7},{7,5},{8,10},{10,8},{12,... | collective-permute-start | bytes 1966088 | tf_op jit(solution)/shard_map/ppermute | solution.py:297
  471.2 30.1 %collective-permute-start.22 = (bf16[256,2560]{1,0:T(8,128)(2,1)S(1)}, bf16[256,2560]{1,0:T(8,128)(2,1)}, u32[]{:S(2)}, u32[]{:S(2)}) collective-permute-start(bf16[256,2560]{1,0:T(8,128)(2,1)S(1)} %pad_maximum_fusion.8), channel_id=1, source_target_pairs={{0,4},{2,6},{4,0},{6,2},{1,5},{3,7},{5,1},{7,3},{8,12},{10,14},{12... | collective-permute-start | bytes 3932168 | tf_op jit(solution)/shard_map/ppermute | solution.py:297
  471.9 29.8 %collective-permute-start.20 = (bf16[256,2560]{1,0:T(8,128)(2,1)S(1)}, bf16[256,2560]{1,0:T(8,128)(2,1)}, u32[]{:S(2)}, u32[]{:S(2)}) collective-permute-start(bf16[256,2560]{1,0:T(8,128)(2,1)S(1)} %pad_maximum_fusion.7), channel_id=1, source_target_pairs={{0,2},{2,0},{4,6},{6,4},{1,3},{3,1},{5,7},{7,5},{8,10},{10,8},{12,... | collective-permute-start | bytes 3932168 | tf_op jit(solution)/shard_map/ppermute | solution.py:297
  517.4 340.1 %reduce-scatter.8.cloned.1.call-start = ((), (), s32[]{:S(2)}) async-start(), calls=%async_computation.9 | async-start | bytes 9584640 | tf_op jit(solution)/shard_map/reduce_scatter | solution.py:405
  526.4 46.7 %collective-permute-start.27 = (bf16[256,2560]{1,0:T(8,128)(2,1)}, bf16[256,2560]{1,0:T(8,128)(2,1)}, u32[]{:S(2)}, u32[]{:S(2)}) collective-permute-start(bf16[256,2560]{1,0:T(8,128)(2,1)} %get-tuple-element.87), channel_id=1, source_target_pairs={{0,4},{2,6},{4,0},{6,2},{1,5},{3,7},{5,1},{7,3},{8,12},{10,14},{12... | collective-permute-start | bytes 3932168 | tf_op jit(solution)/shard_map/ppermute | solution.py:297
  527.9 48.7 %collective-permute-start.25 = (bf16[256,2560]{1,0:T(8,128)(2,1)}, bf16[256,2560]{1,0:T(8,128)(2,1)}, u32[]{:S(2)}, u32[]{:S(2)}) collective-permute-start(bf16[256,2560]{1,0:T(8,128)(2,1)} %get-tuple-element.87), channel_id=1, source_target_pairs={{0,2},{2,0},{4,6},{6,4},{1,3},{3,1},{5,7},{7,5},{8,10},{10,8},{12,... | collective-permute-start | bytes 3932168 | tf_op jit(solution)/shard_map/ppermute | solution.py:297
  552.7 17.8 %collective-permute-start.24 = (bf16[128,2560]{1,0:T(8,128)(2,1)S(1)}, bf16[128,2560]{1,0:T(8,128)(2,1)S(1)}, u32[]{:S(2)}, u32[]{:S(2)}) collective-permute-start(bf16[128,2560]{1,0:T(8,128)(2,1)S(1)} %get-tuple-element.125), channel_id=1, source_target_pairs={{0,2},{2,0},{4,6},{6,4},{1,3},{3,1},{5,7},{7,5},{8,10},{10,8},{12,... | collective-permute-start | bytes 1966088 | tf_op jit(solution)/shard_map/ppermute | solution.py:297
  553.3 17.3 %collective-permute-start.23 = (bf16[128,2560]{1,0:T(8,128)(2,1)S(1)}, bf16[128,2560]{1,0:T(8,128)(2,1)S(1)}, u32[]{:S(2)}, u32[]{:S(2)}) collective-permute-start(bf16[128,2560]{1,0:T(8,128)(2,1)S(1)} %get-tuple-element.126), channel_id=1, source_target_pairs={{0,4},{2,6},{4,0},{6,2},{1,5},{3,7},{5,1},{7,3},{8,12},{10,14},{12... | collective-permute-start | bytes 1966088 | tf_op jit(solution)/shard_map/ppermute | solution.py:297
  575.1 32.9 %collective-permute-start.28 = (bf16[128,2560]{1,0:T(8,128)(2,1)}, bf16[128,2560]{1,0:T(8,128)(2,1)S(1)}, u32[]{:S(2)}, u32[]{:S(2)}) collective-permute-start(bf16[128,2560]{1,0:T(8,128)(2,1)} %slice.505), channel_id=1, source_target_pairs={{0,2},{2,0},{4,6},{6,4},{1,3},{3,1},{5,7},{7,5},{8,10},{10,8},{12,... | collective-permute-start | bytes 1966088 | tf_op jit(solution)/shard_map/ppermute | solution.py:297
  578.6 29.5 %collective-permute-start.26 = (bf16[128,2560]{1,0:T(8,128)(2,1)}, bf16[128,2560]{1,0:T(8,128)(2,1)}, u32[]{:S(2)}, u32[]{:S(2)}) collective-permute-start(bf16[128,2560]{1,0:T(8,128)(2,1)} %slice.504), channel_id=1, source_target_pairs={{0,4},{2,6},{4,0},{6,2},{1,5},{3,7},{5,1},{7,3},{8,12},{10,14},{12... | collective-permute-start | bytes 1966088 | tf_op jit(solution)/shard_map/ppermute | solution.py:297
  609.3 62.2 %collective-permute-start.30 = (bf16[256,2560]{1,0:T(8,128)(2,1)}, bf16[256,2560]{1,0:T(8,128)(2,1)}, u32[]{:S(2)}, u32[]{:S(2)}) collective-permute-start(bf16[256,2560]{1,0:T(8,128)(2,1)} %pad_maximum_fusion.10), channel_id=1, source_target_pairs={{0,4},{2,6},{4,0},{6,2},{1,5},{3,7},{5,1},{7,3},{8,12},{10,14},{12... | collective-permute-start | bytes 3932168 | tf_op jit(solution)/shard_map/ppermute | solution.py:297
  628.5 36.2 %collective-permute-start.35 = (bf16[80,1792]{1,0:T(8,128)(2,1)}, bf16[80,1792]{1,0:T(8,128)(2,1)}, u32[]{:S(2)}, u32[]{:S(2)}) collective-permute-start(bf16[80,1792]{1,0:T(8,128)(2,1)} %get-tuple-element.136), channel_id=1, source_target_pairs={{0,3},{1,7},{2,2},{3,6},{4,1},{5,5},{6,0},{7,4},{8,11},{9,15},{10,... | collective-permute-start | bytes 860168 | tf_op jit(solution)/shard_map/ppermute | solution.py:430
  630.4 34.3 %collective-permute-start.34 = (bf16[80,1792]{1,0:T(8,128)(2,1)}, bf16[80,1792]{1,0:T(8,128)(2,1)}, u32[]{:S(2)}, u32[]{:S(2)}) collective-permute-start(bf16[80,1792]{1,0:T(8,128)(2,1)} %get-tuple-element.137), channel_id=1, source_target_pairs={{0,2},{1,6},{2,3},{3,7},{4,0},{5,4},{6,1},{7,5},{8,10},{9,14},{10,... | collective-permute-start | bytes 860168 | tf_op jit(solution)/shard_map/ppermute | solution.py:430
  632.4 34.8 %collective-permute-start.33 = (bf16[80,1792]{1,0:T(8,128)(2,1)}, bf16[80,1792]{1,0:T(8,128)(2,1)}, u32[]{:S(2)}, u32[]{:S(2)}) collective-permute-start(bf16[80,1792]{1,0:T(8,128)(2,1)} %get-tuple-element.138), channel_id=1, source_target_pairs={{0,1},{1,5},{2,0},{3,4},{4,3},{5,7},{6,2},{7,6},{8,9},{9,13},{10,8... | collective-permute-start | bytes 860168 | tf_op jit(solution)/shard_map/ppermute | solution.py:430
  633.5 35.0 %collective-permute-start.32 = (bf16[80,1792]{1,0:T(8,128)(2,1)}, bf16[80,1792]{1,0:T(8,128)(2,1)}, u32[]{:S(2)}, u32[]{:S(2)}) collective-permute-start(bf16[80,1792]{1,0:T(8,128)(2,1)} %get-tuple-element.135), channel_id=1, source_target_pairs={{0,0},{1,4},{2,1},{3,5},{4,2},{5,6},{6,3},{7,7},{8,8},{9,12},{10,9... | collective-permute-start | bytes 860168 | tf_op jit(solution)/shard_map/ppermute | solution.py:430
  664.7 30.6 %collective-permute-start.29 = (bf16[256,2560]{1,0:T(8,128)(2,1)S(1)}, bf16[256,2560]{1,0:T(8,128)(2,1)S(1)}, u32[]{:S(2)}, u32[]{:S(2)}) collective-permute-start(bf16[256,2560]{1,0:T(8,128)(2,1)S(1)} %copy-done.21), channel_id=1, source_target_pairs={{0,2},{2,0},{4,6},{6,4},{1,3},{3,1},{5,7},{7,5},{8,10},{10,8},{12,... | collective-permute-start | bytes 3932168 | tf_op jit(solution)/shard_map/ppermute | solution.py:297
  664.7 69.0 %collective-permute-start.31 = (bf16[320,1024]{1,0:T(8,128)(2,1)}, bf16[320,1024]{1,0:T(8,128)(2,1)}, u32[]{:S(2)}, u32[]{:S(2)}) collective-permute-start(bf16[320,1024]{1,0:T(8,128)(2,1)} %get-tuple-element.102), channel_id=1, source_target_pairs={{0,16},{8,24},{16,0},{24,8},{1,17},{9,25},{17,1},{25,9},{2,18},{10... | collective-permute-start | bytes 1966088 | tf_op jit(solution)/shard_map/ppermute | solution.py:448
  667.2 66.7 %collective-permute-start.37 = (bf16[320,1024]{1,0:T(8,128)(2,1)}, bf16[320,1024]{1,0:T(8,128)(2,1)}, u32[]{:S(2)}, u32[]{:S(2)}) collective-permute-start(bf16[320,1024]{1,0:T(8,128)(2,1)} %get-tuple-element.101), channel_id=1, source_target_pairs={{0,24},{8,16},{16,8},{24,0},{1,25},{9,17},{17,9},{25,1},{2,26},{10... | collective-permute-start | bytes 1966088 | tf_op jit(solution)/shard_map/ppermute | solution.py:448
  668.5 68.8 %collective-permute-start.36 = (bf16[320,1024]{1,0:T(8,128)(2,1)S(1)}, bf16[320,1024]{1,0:T(8,128)(2,1)}, u32[]{:S(2)}, u32[]{:S(2)}) collective-permute-start(bf16[320,1024]{1,0:T(8,128)(2,1)S(1)} %get-tuple-element.100), channel_id=1, source_target_pairs={{0,8},{8,0},{16,24},{24,16},{1,9},{9,1},{17,25},{25,17},{2,10},{10... | collective-permute-start | bytes 1966088 | tf_op jit(solution)/shard_map/ppermute | solution.py:448
  757.0 16.1 %collective-permute-start.38 = (bf16[128,2560]{1,0:T(8,128)(2,1)S(1)}, bf16[128,2560]{1,0:T(8,128)(2,1)S(1)}, u32[]{:S(2)}, u32[]{:S(2)}) collective-permute-start(bf16[128,2560]{1,0:T(8,128)(2,1)S(1)} %get-tuple-element.123), channel_id=1, source_target_pairs={{0,4},{2,6},{4,0},{6,2},{1,5},{3,7},{5,1},{7,3},{8,12},{10,14},{12... | collective-permute-start | bytes 1966088 | tf_op jit(solution)/shard_map/ppermute | solution.py:297
  775.0 29.1 %collective-permute-start.41 = (bf16[256,2560]{1,0:T(8,128)(2,1)S(1)}, bf16[256,2560]{1,0:T(8,128)(2,1)}, u32[]{:S(2)}, u32[]{:S(2)}) collective-permute-start(bf16[256,2560]{1,0:T(8,128)(2,1)S(1)} %pad_maximum_fusion.13), channel_id=1, source_target_pairs={{0,4},{2,6},{4,0},{6,2},{1,5},{3,7},{5,1},{7,3},{8,12},{10,14},{12... | collective-permute-start | bytes 3932168 | tf_op jit(solution)/shard_map/ppermute | solution.py:297
  776.5 29.1 %collective-permute-start.39 = (bf16[256,2560]{1,0:T(8,128)(2,1)}, bf16[256,2560]{1,0:T(8,128)(2,1)}, u32[]{:S(2)}, u32[]{:S(2)}) collective-permute-start(bf16[256,2560]{1,0:T(8,128)(2,1)} %pad_maximum_fusion.12), channel_id=1, source_target_pairs={{0,2},{2,0},{4,6},{6,4},{1,3},{3,1},{5,7},{7,5},{8,10},{10,8},{12,... | collective-permute-start | bytes 3932168 | tf_op jit(solution)/shard_map/ppermute | solution.py:297
  808.7 18.7 %collective-permute-start.49 = (bf16[80,3584]{1,0:T(8,128)(2,1)S(1)}, bf16[80,3584]{1,0:T(8,128)(2,1)S(1)}, u32[]{:S(2)}, u32[]{:S(2)}) collective-permute-start(bf16[80,3584]{1,0:T(8,128)(2,1)S(1)} %get-tuple-element.120), channel_id=1, source_target_pairs={{0,3},{1,7},{2,2},{3,6},{4,1},{5,5},{6,0},{7,4},{8,11},{9,15},{10,... | collective-permute-start | bytes 1720328 | tf_op jit(solution)/shard_map/ppermute | solution.py:430
  810.7 26.2 %collective-permute-start.48 = (bf16[80,3584]{1,0:T(8,128)(2,1)S(1)}, bf16[80,3584]{1,0:T(8,128)(2,1)S(1)}, u32[]{:S(2)}, u32[]{:S(2)}) collective-permute-start(bf16[80,3584]{1,0:T(8,128)(2,1)S(1)} %get-tuple-element.121), channel_id=1, source_target_pairs={{0,2},{1,6},{2,3},{3,7},{4,0},{5,4},{6,1},{7,5},{8,10},{9,14},{10,... | collective-permute-start | bytes 1720328 | tf_op jit(solution)/shard_map/ppermute | solution.py:430
  810.8 26.1 %collective-permute-start.47 = (bf16[80,3584]{1,0:T(8,128)(2,1)S(1)}, bf16[80,3584]{1,0:T(8,128)(2,1)S(1)}, u32[]{:S(2)}, u32[]{:S(2)}) collective-permute-start(bf16[80,3584]{1,0:T(8,128)(2,1)S(1)} %get-tuple-element.122), channel_id=1, source_target_pairs={{0,1},{1,5},{2,0},{3,4},{4,3},{5,7},{6,2},{7,6},{8,9},{9,13},{10,8... | collective-permute-start | bytes 1720328 | tf_op jit(solution)/shard_map/ppermute | solution.py:430
  813.8 23.1 %collective-permute-start.46 = (bf16[80,3584]{1,0:T(8,128)(2,1)S(1)}, bf16[80,3584]{1,0:T(8,128)(2,1)S(1)}, u32[]{:S(2)}, u32[]{:S(2)}) collective-permute-start(bf16[80,3584]{1,0:T(8,128)(2,1)S(1)} %get-tuple-element.119), channel_id=1, source_target_pairs={{0,0},{1,4},{2,1},{3,5},{4,2},{5,6},{6,3},{7,7},{8,8},{9,12},{10,9... | collective-permute-start | bytes 1720328 | tf_op jit(solution)/shard_map/ppermute | solution.py:430
  (59 other events, 1047.3 us)
Sparse Core Ops, SparseCore 0:
  14.0 85.8 all-gather.4
  112.5 53.2 all-gather.6
  168.0 162.7 all-gather.8
  332.9 86.7 all-gather.10
  421.8 95.4 reduce-scatter.3
  519.6 217.3 reduce-scatter.5
  751.3 106.0 reduce-scatter.7

commit v4 on v3

--- a/solution.py
+++ b/solution.py
@@ -17,7 +17,6 @@
 rope_base = 1000000.0
 
 CHIPS = 4
-SUM_AXES = ("group", "core", "dp")
 REPLICA = ("dp", "chip", "core")
 
 
@@ -401,8 +400,19 @@
     kv_all = lax.all_gather(kv_own_tokens, "group", axis=0, tiled=True)
     kv_all = kv_all.reshape(groups, 2 * kv_width, tokens)
 
-    def reduced(total):
-        return lax.psum_scatter(total, SUM_AXES, scatter_dimension=0, tiled=True)
+    def beside(value):
+        return lax.ppermute(value, "core", [(0, 1), (1, 0)])
+
+    def across(total):
+        halves = total.reshape(groups, 2, half_rows, total.shape[1])
+        own = lax.dynamic_index_in_dim(halves, core, axis=1, keepdims=False)
+        out = lax.dynamic_index_in_dim(halves, 1 - core, axis=1, keepdims=False)
+        back = beside(out)
+        own = (own.astype(jnp.float32) + back.astype(jnp.float32)).astype(jnp.bfloat16)
+        return own.reshape(groups * half_rows, total.shape[1])
+
+    def reduced(total, axes=("group", "core", "dp")):
+        return lax.psum_scatter(total, axes, scatter_dimension=0, tiled=True)
 
     def product_low(left, right):
         return inner_t(left, right).astype(jnp.bfloat16)
@@ -465,6 +475,12 @@
     gated, lifted = both_up[:, :wide], both_up[:, wide:]
     activated = jax.nn.silu(gated)
     hidden = (activated * lifted).astype(jnp.bfloat16)
+    normed_rows = normed_one.T.reshape(groups, 2, half_rows, tokens)
+    own_rows = lax.dynamic_index_in_dim(normed_rows, core, axis=1, keepdims=False)
+    other_rows = lax.dynamic_index_in_dim(normed_rows, 1 - core, axis=1, keepdims=False)
+    pair_rows = jnp.concatenate([own_rows, beside(other_rows)], axis=2)
+    pair_rows = pair_rows.reshape(groups * half_rows, 2 * tokens)
+    hidden, pair_rows = then((hidden, pair_rows))
     total_down, w_sink = then((product_low(grad_low, hidden), w_sink))
     sum_down = reduced(total_down)
 
@@ -510,15 +526,15 @@
     spare = -2 * kv_width % 128
     assert spare >= extra.size
     extra = jnp.pad(extra.reshape(1, -1), ((0, 0), (0, spare - extra.size)))
-    extra = jnp.broadcast_to(extra, (model_width, spare)).astype(jnp.bfloat16)
+    extra = jnp.broadcast_to(extra, (model_width // 2, spare)).astype(jnp.bfloat16)
     grad_kv_own = lax.dynamic_index_in_dim(grad_kv, group_at, axis=0, keepdims=False)
     grad_kv_others = from_group(grad_kv)
     attn_totals = with_layout_constraint(
         jnp.concatenate(
             [
-                product_low(normed_one, grad_query_low),
-                product_low(grad_middle_low, mixed_low),
-                jnp.zeros((model_width, 2 * kv_width + spare), jnp.bfloat16),
+                across(product_low(normed_one, grad_query_low)),
+                across(product_low(grad_middle_low, mixed_low)),
+                jnp.zeros((model_width // 2, 2 * kv_width + spare), jnp.bfloat16),
             ],
             axis=1,
         ),
@@ -532,11 +548,13 @@
     for part in grad_kv_others:
         grad_kv = grad_kv + part.astype(jnp.float32)
     grad_key = unrotate(grad_kv[:kv_width], cosine, sine)
-    grad_kv_low = jnp.concatenate([grad_key, grad_kv[kv_width:]], axis=0).astype(jnp.bfloat16).T
-    total_kv = jnp.concatenate([product_low(normed_one, grad_kv_low), extra], axis=1)
+    grad_kv_rows = jnp.concatenate([grad_key, grad_kv[kv_width:]], axis=0).astype(jnp.bfloat16)
+    grad_kv_low = grad_kv_rows.T
+    pair_kv = jnp.concatenate([grad_kv_rows, beside(grad_kv_rows)], axis=1)
+    total_kv = jnp.concatenate([times_t(pair_rows, pair_kv).astype(jnp.bfloat16), extra], axis=1)
     attn_totals = lax.dynamic_update_slice(attn_totals, total_kv, (0, 2 * query_width))
     attn_totals, grad_query_low, sum_lift = then((attn_totals, grad_query_low, sum_lift))
-    attn_sums = reduced(attn_totals)
+    attn_sums = reduced(attn_totals, ("group", "dp"))
     added = give_back(jnp.concatenate([grad_query_low, grad_kv_low], axis=1), w_qkv)
     input_grad = grad_middle + norm_back(added, source, inverse_one, gain_one)
     added, sum_lift = then((added, sum_lift))
@@ -552,18 +570,25 @@
         laid(attn_parts, 2 * query_width + at * kv_width, kv_width) for at in range(2)
     )
 
-    def gain_grad(gain, *pairs):
-        rows = pairs[0][1].shape[0]
+    def gain_grad(gain, parts, weights):
+        rows = parts[0].shape[0]
         total = 0.0
-        for weight, grad in pairs:
-            weight = lax.dynamic_slice(weight, (whose * rows, 0), (rows, weight.shape[1]))
-            total = total + jnp.sum(weight.astype(jnp.float32) * grad, axis=1)
+        for at, part in enumerate(parts):
+            columns = []
+            for weight in weights:
+                if isinstance(weight, int):
+                    columns.append(jnp.zeros((rows, weight), jnp.bfloat16))
+                else:
+                    width = weight.shape[1] // CHIPS
+                    start = (whose * rows, at * width)
+                    columns.append(lax.dynamic_slice(weight, start, (rows, width)))
+            columns = jnp.concatenate(columns, axis=1)
+            total = total + columns.astype(jnp.float32) * part.astype(jnp.float32)
+        total = jnp.sum(total, axis=1)
         return total / lax.dynamic_slice(gain, (whose * rows,), (rows,)).astype(jnp.float32)
 
-    grad_norm_mlp = gain_grad(gain_mlp, (w_gate, grad_gate), (w_up, grad_up))
-    grad_norm_attn = gain_grad(
-        gain_attn, (w_query, grad_query), (w_key, grad_key), (w_value, grad_value)
-    )
+    grad_norm_mlp = gain_grad(gain_mlp, lift_parts, (w_gate, w_up))
+    grad_norm_attn = gain_grad(gain_attn, attn_parts, (w_query, query_width, w_key, w_value))
 
     return (
         output_full.astype(jnp.bfloat16)[None],

time: 904 us -> 897 us (level)
  waiting for transfers between devices: 371 us -> 334 us
  local copies, waits for them, and re-layouts: 49.5 us -> 75.2 us
    all_gather x1, waiting for transfers between devices: 27.4 us -> 6.17 us  [shards(): kv_all = lax.all_gather(kv_own_tokens, 'group', axis=0, tiled=True)]
    ppermute x35, waiting for transfers between devices: 156 us -> 141 us  [swap(): return lax.ppermute(value, 'chip', pairs)]
    reduce_scatter x3, waiting for transfers between devices: 18.6 us -> 4.67 us  [reduced(): return lax.psum_scatter(total, axes, scatter_dimension=0, tiled=True)]
    transpose x1 -> x2, local copies, waits for them, and re-layouts: 0.35 us -> 9.73 us  [the longest x1 8.58 us: shards(): normed_rows = normed_one.T.reshape(groups, 2, half_rows, tokens)]
    dot_general x5 -> x4, matrix products: 63.5 us -> 55.3 us  [inner_t(): lax.dot_general(left, right, (((0,), (0,)), ((), ())), preferred_element_...]
    unnamed x106 -> x102, local copies, waits for them, and re-layouts: 14 us -> 21.4 us
    dot_general x12 -> x13, matrix products: 87.3 us -> 92.2 us  [times_t(): lax.dot_general(left, right, (((1,), (1,)), ((), ())), preferred_element_...]
  transfers between devices with their start and end apart: 57 -> 61, of which waited for: 33 -> 32; matrix products, arithmetic and copies ran while one was open for 35% -> 38% of each run, Pallas kernels for 8% -> 8%
where the time goes in v4:
time: 897 us; the launch traced here: 882 us
  waiting for transfers between devices  334 us (37%)
  matrix products  220 us (25%)
  other arithmetic  81.5 us (9%)
  local copies, waits for them, and re-layouts  75.2 us (8%)
  starting transfers between devices  71 us (8%)
  Pallas kernels  66.4 us (7%)
  between operations  20.9 us (2%)
  blocking collectives  13.4 us (1%)
    ppermute x35, waiting for transfers between devices, swap(): return lax.ppermute(value, 'chip', pairs)  141 us
    all_gather x3, waiting for transfers between devices, gathered(): return lax.all_gather(part, ('group', 'core'), axis=0, tiled=True)  109 us
    dot_general x13, matrix products, times_t(): lax.dot_general(left, right, (((1,), (1,)), ((), ())), preferred_element_...  92.2 us
    dot_general x5, matrix products, times(): return jnp.dot(left, right, preferred_element_type=jnp.float32)  62.6 us
    dot_general x4, matrix products, inner_t(): lax.dot_general(left, right, (((0,), (0,)), ((), ())), preferred_element_...  55.3 us
    pallas_call x3, Pallas kernels, attend_back(): pl.pallas_call(kernel, out_shape=(jax.ShapeDtypeStruct((tokens, query_wid...  45.6 us
    ppermute x35, starting transfers between devices, swap(): return lax.ppermute(value, 'chip', pairs)  45.4 us
    ppermute x3, waiting for transfers between devices, from_group(): lax.ppermute(lax.dynamic_index_in_dim(values, group_at ^ step, axis=0, ke...  43 us
  transfers between devices with their start and end apart: 61, of which 32 were waited for; matrix products, arithmetic and copies ran while one was open for 38% of the time, Pallas kernels for 8%

profile of v4, /device:TPU:0, one launch (start us, length us, event | category | flops | bytes accessed | tf_op | source)
XLA Modules:
  0.0 882.4 jit_solution(11530798376437451085)
XLA Ops:
  22.0 13.4 %all_gather.16 = bf16[2,2560]{1,0:T(2,128)(2,1)S(1)} all-gather(bf16[2,640]{1,0:T(2,128)(2,1)S(1)} %pad_maximum_fusion.23), channel_id=1, replica_groups=mesh['group'=4,'dp'=1,'chip'=4,'core'=2] {'group'}, dimensions={1}, use_global_device_ids=true | all-gather | bytes 12800 | tf_op jit(solution)/shard_map/all_gather | solution.py:374
  35.6 11.5 %collective-permute-done.6 = s32[258]{0:T(512)S(1)} collective-permute-done((s32[258]{0:T(512)S(1)}, s32[258]{0:T(512)S(1)}, u32[]{:S(2)}, u32[]{:S(2)}) %collective-permute-start.6) | collective-permute-done | bytes 1064 | tf_op jit(solution)/shard_map/ppermute | solution.py:296
  50.4 13.1 %collective-permute-done.2 = bf16[128,2560]{1,0:T(8,128)(2,1)S(1)} collective-permute-done((bf16[128,2560]{1,0:T(8,128)(2,1)S(1)}, bf16[128,2560]{1,0:T(8,128)(2,1)S(1)}, u32[]{:S(2)}, u32[]{:S(2)}) %collective-permute-start.2) | collective-permute-done | bytes 655392 | tf_op jit(solution)/shard_map/ppermute | solution.py:296
  67.1 32.8 %all-gather.5.cloned.1.call-done = bf16[2560,1600]{1,0:T(8,128)(2,1)} async-done(((bf16[320,1600]{1,0:T(8,128)(2,1)}), bf16[2560,1600]{1,0:T(8,128)(2,1)}) %all-gather.5.cloned.1.call-update) | async-done | bytes 8192016 | tf_op jit(solution)/shard_map/all_gather | solution.py:372
  99.9 9.5 %fusion.20 = f32[960,1024]{1,0:T(8,128)S(1)} fusion(bf16[2560,1600]{1,0:T(8,128)(2,1)} %all-gather.5.cloned.1.call-done, bf16[1024,2560]{1,0:T(8,128)(2,1)} %copy-done.2, f32[2560]{0:T(1024)S(1)} %get-tuple-element.79, f32[1024]{0:T(1024)S(1)} %add_rsqrt_fusion), kind=kOutput, calls=%fused_computation.46 | convolution fusion | flops 5043650560 | bytes 14432256 | tf_op jit(solution)/shard_map/dot_general | solution.py:392
  136.1 10.8 %collective-permute-done.16 = bf16[256,2560]{1,0:T(8,128)(2,1)} collective-permute-done((bf16[256,2560]{1,0:T(8,128)(2,1)S(1)}, bf16[256,2560]{1,0:T(8,128)(2,1)}, u32[]{:S(2)}, u32[]{:S(2)}) %collective-permute-start.16) | collective-permute-done | bytes 1310752 | tf_op jit(solution)/shard_map/ppermute | solution.py:296
  159.6 6.2 all-gather.7.cloned.1.call-done
  165.8 20.8 %attend.1 = (bf16[1024,640]{1,0:T(8,128)(2,1)}, f32[4,8,256]{2,1,0:T(8,128)}) custom-call(bf16[640,1024]{1,0:T(8,128)(2,1)} %bitcast.177, bf16[4,320,1024]{2,1,0:T(8,128)(2,1)} %bitcast.188, s32[4,1,256]{2,1,0:T(1,128)} %broadcast_in_dim.39.refs_2_), custom_call_target="tpu_custom_call" | custom-call | flops 2684354560 | bytes 5242880 | tf_op jit(solution)/shard_map/attend/pallas_call | solution.py:99
  193.4 4.6 convolution_convert_fusion.6
  198.1 8.8 collective-permute-done.7
  216.2 8.6 copy.38
  230.6 8.7 collective-permute-done.10
  240.7 4.8 multiply_reduce_fusion.3
  257.2 18.6 %collective-permute-done.11 = bf16[256,2560]{1,0:T(8,128)(2,1)S(1)} collective-permute-done((bf16[256,2560]{1,0:T(8,128)(2,1)S(1)}, bf16[256,2560]{1,0:T(8,128)(2,1)S(1)}, u32[]{:S(2)}, u32[]{:S(2)}) %collective-permute-start.11) | collective-permute-done | bytes 1310752 | tf_op jit(solution)/shard_map/ppermute | solution.py:296
  281.2 9.8 %collective-permute-done.13 = bf16[128,2560]{1,0:T(8,128)(2,1)S(1)} collective-permute-done((bf16[128,2560]{1,0:T(8,128)(2,1)S(1)}, bf16[128,2560]{1,0:T(8,128)(2,1)S(1)}, u32[]{:S(2)}, u32[]{:S(2)}) %collective-permute-start.13) | collective-permute-done | bytes 655392 | tf_op jit(solution)/shard_map/ppermute | solution.py:296
  292.8 38.0 %all-gather.9.cloned.1.call-done = bf16[2560,3584]{1,0:T(8,128)(2,1)} async-done(((bf16[320,3584]{1,0:T(8,128)(2,1)}), bf16[2560,3584]{1,0:T(8,128)(2,1)}) %all-gather.9.cloned.1.call-update) | async-done | bytes 18350096 | tf_op jit(solution)/shard_map/all_gather | solution.py:372
  330.8 27.5 %fusion.129 = f32[1024,3584]{1,0:T(8,128)} fusion(bf16[1024,2560]{1,0:T(8,128)(2,1)} %constant_dynamic-update-slice_fusion.5, bf16[2560,3584]{1,0:T(8,128)(2,1)} %all-gather.9.cloned.1.call-done), kind=kOutput, calls=%fused_computation.303 | convolution fusion | flops 18790481920 | bytes 38273024 | tf_op jit(solution)/shard_map/dot_general | solution.py:261
  358.3 6.3 multiply_convert_fusion.2
  366.5 14.0 %convolution_convert_fusion.1 = bf16[2560,1792]{1,0:T(8,128)(2,1)} fusion(bf16[1024,2560]{1,0:T(8,128)(2,1)} %constant_dynamic-update-slice_fusion.10, bf16[1024,1792]{1,0:T(8,128)(2,1)S(1)} %multiply_convert_fusion.2), kind=kOutput, calls=%fused_computation.3 | convolution fusion | flops 9399828480 | bytes 18087936 | tf_op jit(solution)/shard_map/dot_general | solution.py:271
  380.5 38.6 %all-gather.11.cloned.1.call-done = bf16[2560,1792]{1,0:T(8,128)(2,1)} async-done(((bf16[320,1792]{1,0:T(8,128)(2,1)}), bf16[2560,1792]{1,0:T(8,128)(2,1)}) %all-gather.11.cloned.1.call-update) | async-done | bytes 9175056 | tf_op jit(solution)/shard_map/all_gather | solution.py:372
  419.2 19.6 %multiply_convert_fusion = (bf16[1024,1792]{1,0:T(8,128)(2,1)S(1)}, bf16[1024,1792]{1,0:T(8,128)(2,1)S(1)}) fusion(f32[1024,3584]{1,0:T(8,128)} %fusion.129, bf16[1024,2560]{1,0:T(8,128)(2,1)} %constant_dynamic-update-slice_fusion.10, bf16[2560,1792]{1,0:T(8,128)(2,1)} %all-gather.11.cloned.1.call-done), kind=kOutput, calls=%fused_computation.12 | convolution fusion | flops 9417261056 | bytes 36438016 | tf_op jit(solution)/shard_map/dot_general | solution.py:261
  438.8 11.8 %convolution_convert_fusion.9 = bf16[256,2560]{1,0:T(8,128)(2,1)S(1)} fusion(bf16[2560,3584]{1,0:T(8,128)(2,1)} %all-gather.9.cloned.1.call-done, bf16[1024,1792]{1,0:T(8,128)(2,1)S(1)} %get-tuple-element.96, bf16[1024,1792]{1,0:T(8,128)(2,1)S(1)} %get-tuple-element.95), kind=kOutput, calls=%fused_computation.39 | convolution fusion | flops 4701945856 | bytes 27000832 | tf_op jit(solution)/shard_map/dot_general | solution.py:265
  453.6 14.6 %convolution_convert_fusion.3 = bf16[512,2560]{1,0:T(8,128)(2,1)S(1)} fusion(bf16[2560,3584]{1,0:T(8,128)(2,1)} %all-gather.9.cloned.1.call-done, bf16[1024,1792]{1,0:T(8,128)(2,1)} %copy-done.42, bf16[1024,1792]{1,0:T(8,128)(2,1)} %copy-done.41), kind=kOutput, calls=%fused_computation.32 | convolution fusion | flops 9403891712 | bytes 28311552 | tf_op jit(solution)/shard_map/dot_general | solution.py:265
  472.6 27.4 %convolution_convert_fusion = bf16[2560,3584]{1,0:T(8,128)(2,1)} fusion(bf16[1024,2560]{1,0:T(8,128)(2,1)} %constant_dynamic-update-slice_fusion.5, bf16[1024,1792]{1,0:T(8,128)(2,1)} %copy-done.41, bf16[1024,1792]{1,0:T(8,128)(2,1)} %copy-done.42), kind=kOutput, calls=%fused_computation | convolution fusion | flops 18814337024 | bytes 30932992 | tf_op jit(solution)/shard_map/dot_general | solution.py:271
  500.8 11.3 %convert_add_fusion.4 = f32[256,2560]{1,0:T(8,128)} fusion(bf16[256,2560]{1,0:T(8,128)(2,1)} %collective-permute-done.23, bf16[256,2560]{1,0:T(8,128)(2,1)} %collective-permute-done.21, bf16[2560,3584]{1,0:T(8,128)(2,1)} %all-gather.9.cloned.1.call-done, bf16[1024,1792]{1,0:T(8,128)(2,1)} %copy-done.41, bf16[1024,1792]{1,0:T(8,128)(2,1)} %copy-done.42), kind=kOutput, calls=%fused_computation.69 | convolution fusion | flops 4703911936 | bytes 30932992 | tf_op jit(solution)/shard_map/dot_general | solution.py:265
  512.1 4.7 reduce-scatter.4.cloned.1.call-done
  528.7 4.8 fusion.65.refs_5_
  533.5 11.8 %attend_back.3 = (bf16[1024,640]{1,0:T(8,128)(2,1)}, bf16[4,320,1024]{2,1,0:T(8,128)(2,1)}) custom-call(bf16[640,1024]{1,0:T(8,128)(2,1)} %bitcast.178, bf16[4,320,1024]{2,1,0:T(8,128)(2,1)} %bitcast.189, s32[4,1,256]{2,1,0:T(1,128)} %broadcast_in_dim.39.refs_2_, f32[4,8,256]{2,1,0:T(8,128)} %get-tuple-element.45.refs_3_, ...), custom_call_target="tpu_custom_call" | custom-call | flops 1677721600 | bytes 2621440 | tf_op jit(solution)/shard_map/attend_back/pallas_call | solution.py:224
  545.3 6.7 convolution_convert_fusion.8
  553.2 7.7 fusion.74
  560.9 8.9 %convolution_convert_fusion.5 = bf16[512,2560]{1,0:T(8,128)(2,1)S(1)} fusion(bf16[2560,1792]{1,0:T(8,128)(2,1)} %all-gather.11.cloned.1.call-done, bf16[1024,1792]{1,0:T(8,128)(2,1)S(1)} %copy-done.16), kind=kOutput, calls=%fused_computation.34 | convolution fusion | flops 4698931200 | bytes 13631488 | tf_op jit(solution)/shard_map/dot_general | solution.py:265
  579.5 6.3 fusion.44.refs_5_
  585.7 21.8 %attend_back.4 = (bf16[1024,640]{1,0:T(8,128)(2,1)}, bf16[4,320,1024]{2,1,0:T(8,128)(2,1)}) custom-call(bf16[640,1024]{1,0:T(8,128)(2,1)} %bitcast.179, bf16[4,320,1024]{2,1,0:T(8,128)(2,1)} %bitcast.190, s32[4,1,256]{2,1,0:T(1,128)} %broadcast_in_dim.39.refs_2_, ...), custom_call_target="tpu_custom_call", output_to_operand_aliasing={{0}: (8, {}), {1}: (9, {})} | custom-call | flops 3355443200 | bytes 5242880 | tf_op jit(solution)/shard_map/attend_back/pallas_call | solution.py:224
  613.7 12.0 %attend_back.5 = (bf16[1024,640]{1,0:T(8,128)(2,1)}, bf16[4,320,1024]{2,1,0:T(8,128)(2,1)}) custom-call(bf16[640,1024]{1,0:T(8,128)(2,1)} %bitcast.180, bf16[4,320,1024]{2,1,0:T(8,128)(2,1)} %bitcast.191, s32[4,1,256]{2,1,0:T(1,128)} %broadcast_in_dim.39.refs_2_, ...), custom_call_target="tpu_custom_call", output_to_operand_aliasing={{0}: (8, {}), {1}: (9, {})} | custom-call | flops 1677721600 | bytes 2621440 | tf_op jit(solution)/shard_map/attend_back/pallas_call | solution.py:224
  632.8 6.9 fusion.11
  642.0 7.1 convolution_convert_fusion.2
  663.6 22.8 %collective-permute-done.30 = bf16[256,2560]{1,0:T(8,128)(2,1)S(1)} collective-permute-done((bf16[256,2560]{1,0:T(8,128)(2,1)S(1)}, bf16[256,2560]{1,0:T(8,128)(2,1)S(1)}, u32[]{:S(2)}, u32[]{:S(2)}) %collective-permute-start.30) | collective-permute-done | bytes 1310752 | tf_op jit(solution)/shard_map/ppermute | solution.py:296
  701.8 25.8 %collective-permute-done.32 = bf16[320,1024]{1,0:T(8,128)(2,1)} collective-permute-done((bf16[320,1024]{1,0:T(8,128)(2,1)}, bf16[320,1024]{1,0:T(8,128)(2,1)}, u32[]{:S(2)}, u32[]{:S(2)}) %collective-permute-start.32) | collective-permute-done | bytes 655392 | tf_op jit(solution)/shard_map/ppermute | solution.py:458
  727.7 17.1 %collective-permute-done.39 = bf16[320,1024]{1,0:T(8,128)(2,1)} collective-permute-done((bf16[320,1024]{1,0:T(8,128)(2,1)}, bf16[320,1024]{1,0:T(8,128)(2,1)}, u32[]{:S(2)}, u32[]{:S(2)}) %collective-permute-start.39) | collective-permute-done | bytes 655392 | tf_op jit(solution)/shard_map/ppermute | solution.py:458
  749.7 4.5 convolution_convert_fusion.11
  763.8 5.4 convolution_convert_fusion.4
  769.3 9.4 %collective-permute-done.42 = bf16[128,2560]{1,0:T(8,128)(2,1)} collective-permute-done((bf16[128,2560]{1,0:T(8,128)(2,1)}, bf16[128,2560]{1,0:T(8,128)(2,1)}, u32[]{:S(2)}, u32[]{:S(2)}) %collective-permute-start.42) | collective-permute-done | bytes 655392 | tf_op jit(solution)/shard_map/ppermute | solution.py:296
  794.1 18.2 %collective-permute-done.45 = bf16[256,2560]{1,0:T(8,128)(2,1)} collective-permute-done((bf16[256,2560]{1,0:T(8,128)(2,1)}, bf16[256,2560]{1,0:T(8,128)(2,1)}, u32[]{:S(2)}, u32[]{:S(2)}) %collective-permute-start.45) | collective-permute-done | bytes 1310752 | tf_op jit(solution)/shard_map/ppermute | solution.py:296
  825.3 10.3 %collective-permute-done.53 = bf16[80,3584]{1,0:T(8,128)(2,1)S(1)} collective-permute-done((bf16[80,3584]{1,0:T(8,128)(2,1)S(1)}, bf16[80,3584]{1,0:T(8,128)(2,1)S(1)}, u32[]{:S(2)}, u32[]{:S(2)}) %collective-permute-start.53) | collective-permute-done | bytes 573472 | tf_op jit(solution)/shard_map/ppermute | solution.py:440
  835.6 9.1 %collective-permute-done.52 = bf16[80,3584]{1,0:T(8,128)(2,1)S(1)} collective-permute-done((bf16[80,3584]{1,0:T(8,128)(2,1)S(1)}, bf16[80,3584]{1,0:T(8,128)(2,1)S(1)}, u32[]{:S(2)}, u32[]{:S(2)}) %collective-permute-start.52) | collective-permute-done | bytes 573472 | tf_op jit(solution)/shard_map/ppermute | solution.py:440
  851.7 6.1 collective-permute-start.49
  859.9 4.7 collective-permute-done.49
  864.6 4.9 collective-permute-done.48
  (365 shorter events, 233.6 us)
Async XLA Ops:
  7.2 92.7 %all-gather.5.cloned.1.call-start = ((), (), s32[]{:S(2)}) async-start(), calls=%async_computation.3 | async-start | bytes 9584640 | tf_op jit(solution)/shard_map/all_gather | solution.py:372
  13.8 151.9 %all-gather.7.cloned.1.call-start = ((), (), s32[]{:S(2)}) async-start(), calls=%async_computation.4 | async-start | bytes 3276800 | tf_op jit(solution)/shard_map/all_gather | solution.py:400
  13.9 34.0 %collective-permute-start = (bf16[256,2560]{1,0:T(8,128)(2,1)S(1)}, bf16[256,2560]{1,0:T(8,128)(2,1)S(1)}, u32[]{:S(2)}, u32[]{:S(2)}) collective-permute-start(bf16[256,2560]{1,0:T(8,128)(2,1)S(1)} %bitcast.169), channel_id=1, source_target_pairs={{0,2},{2,0},{4,6},{6,4},{1,3},{3,1},{5,7},{7,5},{8,10},{10,8},{12,... | collective-permute-start | bytes 3932168 | tf_op jit(solution)/shard_map/ppermute | solution.py:296
  16.9 32.6 %collective-permute-start.1 = (bf16[256,2560]{1,0:T(8,128)(2,1)S(1)}, bf16[256,2560]{1,0:T(8,128)(2,1)S(1)}, u32[]{:S(2)}, u32[]{:S(2)}) collective-permute-start(bf16[256,2560]{1,0:T(8,128)(2,1)S(1)} %bitcast.170), channel_id=1, source_target_pairs={{0,4},{2,6},{4,0},{6,2},{1,5},{3,7},{5,1},{7,3},{8,12},{10,14},{12... | collective-permute-start | bytes 3932168 | tf_op jit(solution)/shard_map/ppermute | solution.py:296
  18.4 28.7 %collective-permute-start.6 = (s32[258]{0:T(512)S(1)}, s32[258]{0:T(512)S(1)}, u32[]{:S(2)}, u32[]{:S(2)}) collective-permute-start(s32[258]{0:T(512)S(1)} %pad_add_fusion.4), channel_id=1, source_target_pairs={{0,6},{2,4},{4,2},{6,0},{1,7},{3,5},{5,3},{7,1},{8,14},{10,12},{12... | collective-permute-start | bytes 3104 | tf_op jit(solution)/shard_map/ppermute | solution.py:296
  18.5 28.7 %collective-permute-start.5 = (s32[258]{0:T(512)S(1)}, s32[258]{0:T(512)S(1)}, u32[]{:S(2)}, u32[]{:S(2)}) collective-permute-start(s32[258]{0:T(512)S(1)} %pad_add_fusion.4), channel_id=1, source_target_pairs={{0,4},{2,6},{4,0},{6,2},{1,5},{3,7},{5,1},{7,3},{8,12},{10,14},{12... | collective-permute-start | bytes 3104 | tf_op jit(solution)/shard_map/ppermute | solution.py:296
  20.5 26.7 %collective-permute-start.4 = (s32[258]{0:T(512)S(1)}, s32[258]{0:T(512)S(1)}, u32[]{:S(2)}, u32[]{:S(2)}) collective-permute-start(s32[258]{0:T(512)S(1)} %pad_add_fusion.4), channel_id=1, source_target_pairs={{0,2},{2,0},{4,6},{6,4},{1,3},{3,1},{5,7},{7,5},{8,10},{10,8},{12,... | collective-permute-start | bytes 3104 | tf_op jit(solution)/shard_map/ppermute | solution.py:296
  112.4 218.5 %all-gather.9.cloned.1.call-start = ((), (), s32[]{:S(2)}) async-start(), calls=%async_computation.5 | async-start | bytes 20643840 | tf_op jit(solution)/shard_map/all_gather | solution.py:372
  115.6 303.5 %all-gather.11.cloned.1.call-start = ((), (), s32[]{:S(2)}) async-start(), calls=%async_computation.6 | async-start | bytes 10321920 | tf_op jit(solution)/shard_map/all_gather | solution.py:372
  115.9 31.0 %collective-permute-start.16 = (bf16[256,2560]{1,0:T(8,128)(2,1)S(1)}, bf16[256,2560]{1,0:T(8,128)(2,1)}, u32[]{:S(2)}, u32[]{:S(2)}) collective-permute-start(bf16[256,2560]{1,0:T(8,128)(2,1)S(1)} %bitcast.175), channel_id=1, source_target_pairs={{0,2},{2,0},{4,6},{6,4},{1,3},{3,1},{5,7},{7,5},{8,10},{10,8},{12,... | collective-permute-start | bytes 3932168 | tf_op jit(solution)/shard_map/ppermute | solution.py:296
  117.3 33.0 %collective-permute-start.17 = (bf16[256,2560]{1,0:T(8,128)(2,1)S(1)}, bf16[256,2560]{1,0:T(8,128)(2,1)}, u32[]{:S(2)}, u32[]{:S(2)}) collective-permute-start(bf16[256,2560]{1,0:T(8,128)(2,1)S(1)} %bitcast.176), channel_id=1, source_target_pairs={{0,4},{2,6},{4,0},{6,2},{1,5},{3,7},{5,1},{7,3},{8,12},{10,14},{12... | collective-permute-start | bytes 3932168 | tf_op jit(solution)/shard_map/ppermute | solution.py:296
  121.2 395.6 %reduce-scatter.4.cloned.1.call-start = ((), (), s32[]{:S(2)}) async-start(), calls=%async_computation.7 | async-start | bytes 10321920 | tf_op jit(solution)/shard_map/reduce_scatter | solution.py:415
  148.9 101.6 %collective-permute-start.18 = (bf16[128,2560]{1,0:T(8,128)(2,1)}, bf16[128,2560]{1,0:T(8,128)(2,1)}, u32[]{:S(2)}, u32[]{:S(2)}) collective-permute-start(bf16[128,2560]{1,0:T(8,128)(2,1)} %slice.486), channel_id=1, source_target_pairs={{0,4},{2,6},{4,0},{6,2},{1,5},{3,7},{5,1},{7,3},{8,12},{10,14},{12... | collective-permute-start | bytes 1966088 | tf_op jit(solution)/shard_map/ppermute | solution.py:296
  152.3 100.1 %collective-permute-start.19 = (bf16[128,2560]{1,0:T(8,128)(2,1)}, bf16[128,2560]{1,0:T(8,128)(2,1)}, u32[]{:S(2)}, u32[]{:S(2)}) collective-permute-start(bf16[128,2560]{1,0:T(8,128)(2,1)} %slice.487), channel_id=1, source_target_pairs={{0,2},{2,0},{4,6},{6,4},{1,3},{3,1},{5,7},{7,5},{8,10},{10,8},{12,... | collective-permute-start | bytes 1966088 | tf_op jit(solution)/shard_map/ppermute | solution.py:296
  209.6 29.7 %collective-permute-start.10 = (bf16[256,2560]{1,0:T(8,128)(2,1)}, bf16[256,2560]{1,0:T(8,128)(2,1)}, u32[]{:S(2)}, u32[]{:S(2)}) collective-permute-start(bf16[256,2560]{1,0:T(8,128)(2,1)} %pad_maximum_fusion.7), channel_id=1, source_target_pairs={{0,4},{2,6},{4,0},{6,2},{1,5},{3,7},{5,1},{7,3},{8,12},{10,14},{12... | collective-permute-start | bytes 3932168 | tf_op jit(solution)/shard_map/ppermute | solution.py:296
  211.3 29.5 %collective-permute-start.8 = (bf16[256,2560]{1,0:T(8,128)(2,1)}, bf16[256,2560]{1,0:T(8,128)(2,1)}, u32[]{:S(2)}, u32[]{:S(2)}) collective-permute-start(bf16[256,2560]{1,0:T(8,128)(2,1)} %pad_maximum_fusion.6), channel_id=1, source_target_pairs={{0,2},{2,0},{4,6},{6,4},{1,3},{3,1},{5,7},{7,5},{8,10},{10,8},{12,... | collective-permute-start | bytes 3932168 | tf_op jit(solution)/shard_map/ppermute | solution.py:296
  228.0 26.4 %collective-permute-start.15 = (bf16[4,320,1024]{2,1,0:T(8,128)(2,1)S(1)}, bf16[4,320,1024]{2,1,0:T(8,128)(2,1)S(1)}, u32[]{:S(2)}, u32[]{:S(2)}) collective-permute-start(bf16[4,320,1024]{2,1,0:T(8,128)(2,1)S(1)} %get-tuple-element.107), channel_id=1, source_target_pairs={{0,1},{1,0},{2,3},{3,2},{4,5},{5,4},{6,7},{7,6},{8,9},{9,8},{10,11... | collective-permute-start | bytes 7864328 | tf_op jit(solution)/shard_map/ppermute | solution.py:404
  247.6 28.2 %collective-permute-start.11 = (bf16[256,2560]{1,0:T(8,128)(2,1)S(1)}, bf16[256,2560]{1,0:T(8,128)(2,1)S(1)}, u32[]{:S(2)}, u32[]{:S(2)}) collective-permute-start(bf16[256,2560]{1,0:T(8,128)(2,1)S(1)} %get-tuple-element.94), channel_id=1, source_target_pairs={{0,2},{2,0},{4,6},{6,4},{1,3},{3,1},{5,7},{7,5},{8,10},{10,8},{12,... | collective-permute-start | bytes 3932168 | tf_op jit(solution)/shard_map/ppermute | solution.py:296
  249.0 29.6 %collective-permute-start.12 = (bf16[256,2560]{1,0:T(8,128)(2,1)S(1)}, bf16[256,2560]{1,0:T(8,128)(2,1)S(1)}, u32[]{:S(2)}, u32[]{:S(2)}) collective-permute-start(bf16[256,2560]{1,0:T(8,128)(2,1)S(1)} %get-tuple-element.94), channel_id=1, source_target_pairs={{0,4},{2,6},{4,0},{6,2},{1,5},{3,7},{5,1},{7,3},{8,12},{10,14},{12... | collective-permute-start | bytes 3932168 | tf_op jit(solution)/shard_map/ppermute | solution.py:296
  419.1 337.4 %reduce-scatter.6.cloned.1.call-start = ((), (), s32[]{:S(2)}) async-start(), calls=%async_computation.8 | async-start | bytes 20643840 | tf_op jit(solution)/shard_map/reduce_scatter | solution.py:415
  450.7 17.6 %collective-permute-start.20 = (bf16[128,2560]{1,0:T(8,128)(2,1)S(1)}, bf16[128,2560]{1,0:T(8,128)(2,1)S(1)}, u32[]{:S(2)}, u32[]{:S(2)}) collective-permute-start(bf16[128,2560]{1,0:T(8,128)(2,1)S(1)} %get-tuple-element.141), channel_id=1, source_target_pairs={{0,4},{2,6},{4,0},{6,2},{1,5},{3,7},{5,1},{7,3},{8,12},{10,14},{12... | collective-permute-start | bytes 1966088 | tf_op jit(solution)/shard_map/ppermute | solution.py:296
  470.3 30.1 %collective-permute-start.23 = (bf16[256,2560]{1,0:T(8,128)(2,1)S(1)}, bf16[256,2560]{1,0:T(8,128)(2,1)}, u32[]{:S(2)}, u32[]{:S(2)}) collective-permute-start(bf16[256,2560]{1,0:T(8,128)(2,1)S(1)} %pad_maximum_fusion.9), channel_id=1, source_target_pairs={{0,4},{2,6},{4,0},{6,2},{1,5},{3,7},{5,1},{7,3},{8,12},{10,14},{12... | collective-permute-start | bytes 3932168 | tf_op jit(solution)/shard_map/ppermute | solution.py:296
  471.1 29.7 %collective-permute-start.21 = (bf16[256,2560]{1,0:T(8,128)(2,1)S(1)}, bf16[256,2560]{1,0:T(8,128)(2,1)}, u32[]{:S(2)}, u32[]{:S(2)}) collective-permute-start(bf16[256,2560]{1,0:T(8,128)(2,1)S(1)} %pad_maximum_fusion.8), channel_id=1, source_target_pairs={{0,2},{2,0},{4,6},{6,4},{1,3},{3,1},{5,7},{7,5},{8,10},{10,8},{12,... | collective-permute-start | bytes 3932168 | tf_op jit(solution)/shard_map/ppermute | solution.py:296
  516.8 333.6 %reduce-scatter.8.cloned.1.call-start = ((), (), s32[]{:S(2)}) async-start(), calls=%async_computation.9 | async-start | bytes 5324800 | tf_op jit(solution)/shard_map/reduce_scatter | solution.py:415
  525.8 46.8 %collective-permute-start.28 = (bf16[256,2560]{1,0:T(8,128)(2,1)}, bf16[256,2560]{1,0:T(8,128)(2,1)}, u32[]{:S(2)}, u32[]{:S(2)}) collective-permute-start(bf16[256,2560]{1,0:T(8,128)(2,1)} %get-tuple-element.91), channel_id=1, source_target_pairs={{0,4},{2,6},{4,0},{6,2},{1,5},{3,7},{5,1},{7,3},{8,12},{10,14},{12... | collective-permute-start | bytes 3932168 | tf_op jit(solution)/shard_map/ppermute | solution.py:296
  527.3 48.7 %collective-permute-start.26 = (bf16[256,2560]{1,0:T(8,128)(2,1)}, bf16[256,2560]{1,0:T(8,128)(2,1)}, u32[]{:S(2)}, u32[]{:S(2)}) collective-permute-start(bf16[256,2560]{1,0:T(8,128)(2,1)} %get-tuple-element.91), channel_id=1, source_target_pairs={{0,2},{2,0},{4,6},{6,4},{1,3},{3,1},{5,7},{7,5},{8,10},{10,8},{12,... | collective-permute-start | bytes 3932168 | tf_op jit(solution)/shard_map/ppermute | solution.py:296
  552.1 17.8 %collective-permute-start.25 = (bf16[128,2560]{1,0:T(8,128)(2,1)S(1)}, bf16[128,2560]{1,0:T(8,128)(2,1)S(1)}, u32[]{:S(2)}, u32[]{:S(2)}) collective-permute-start(bf16[128,2560]{1,0:T(8,128)(2,1)S(1)} %get-tuple-element.139), channel_id=1, source_target_pairs={{0,2},{2,0},{4,6},{6,4},{1,3},{3,1},{5,7},{7,5},{8,10},{10,8},{12,... | collective-permute-start | bytes 1966088 | tf_op jit(solution)/shard_map/ppermute | solution.py:296
  552.6 17.3 %collective-permute-start.24 = (bf16[128,2560]{1,0:T(8,128)(2,1)S(1)}, bf16[128,2560]{1,0:T(8,128)(2,1)S(1)}, u32[]{:S(2)}, u32[]{:S(2)}) collective-permute-start(bf16[128,2560]{1,0:T(8,128)(2,1)S(1)} %get-tuple-element.140), channel_id=1, source_target_pairs={{0,4},{2,6},{4,0},{6,2},{1,5},{3,7},{5,1},{7,3},{8,12},{10,14},{12... | collective-permute-start | bytes 1966088 | tf_op jit(solution)/shard_map/ppermute | solution.py:296
  574.5 33.1 %collective-permute-start.29 = (bf16[128,2560]{1,0:T(8,128)(2,1)}, bf16[128,2560]{1,0:T(8,128)(2,1)S(1)}, u32[]{:S(2)}, u32[]{:S(2)}) collective-permute-start(bf16[128,2560]{1,0:T(8,128)(2,1)} %slice.505), channel_id=1, source_target_pairs={{0,2},{2,0},{4,6},{6,4},{1,3},{3,1},{5,7},{7,5},{8,10},{10,8},{12,... | collective-permute-start | bytes 1966088 | tf_op jit(solution)/shard_map/ppermute | solution.py:296
  578.0 29.6 %collective-permute-start.27 = (bf16[128,2560]{1,0:T(8,128)(2,1)}, bf16[128,2560]{1,0:T(8,128)(2,1)}, u32[]{:S(2)}, u32[]{:S(2)}) collective-permute-start(bf16[128,2560]{1,0:T(8,128)(2,1)} %slice.504), channel_id=1, source_target_pairs={{0,4},{2,6},{4,0},{6,2},{1,5},{3,7},{5,1},{7,3},{8,12},{10,14},{12... | collective-permute-start | bytes 1966088 | tf_op jit(solution)/shard_map/ppermute | solution.py:296
  608.9 53.5 %collective-permute-start.31 = (bf16[256,2560]{1,0:T(8,128)(2,1)}, bf16[256,2560]{1,0:T(8,128)(2,1)}, u32[]{:S(2)}, u32[]{:S(2)}) collective-permute-start(bf16[256,2560]{1,0:T(8,128)(2,1)} %pad_maximum_fusion.11), channel_id=1, source_target_pairs={{0,4},{2,6},{4,0},{6,2},{1,5},{3,7},{5,1},{7,3},{8,12},{10,14},{12... | collective-permute-start | bytes 3932168 | tf_op jit(solution)/shard_map/ppermute | solution.py:296
  627.1 26.9 %collective-permute-start.38 = (bf16[80,1792]{1,0:T(8,128)(2,1)S(1)}, bf16[80,1792]{1,0:T(8,128)(2,1)S(1)}, u32[]{:S(2)}, u32[]{:S(2)}) collective-permute-start(bf16[80,1792]{1,0:T(8,128)(2,1)S(1)} %get-tuple-element.150), channel_id=1, source_target_pairs={{0,3},{1,7},{2,2},{3,6},{4,1},{5,5},{6,0},{7,4},{8,11},{9,15},{10,... | collective-permute-start | bytes 860168 | tf_op jit(solution)/shard_map/ppermute | solution.py:440
  629.0 28.7 %collective-permute-start.37 = (bf16[80,1792]{1,0:T(8,128)(2,1)S(1)}, bf16[80,1792]{1,0:T(8,128)(2,1)S(1)}, u32[]{:S(2)}, u32[]{:S(2)}) collective-permute-start(bf16[80,1792]{1,0:T(8,128)(2,1)S(1)} %get-tuple-element.151), channel_id=1, source_target_pairs={{0,2},{1,6},{2,3},{3,7},{4,0},{5,4},{6,1},{7,5},{8,10},{9,14},{10,... | collective-permute-start | bytes 860168 | tf_op jit(solution)/shard_map/ppermute | solution.py:440
  629.1 30.9 %collective-permute-start.36 = (bf16[80,1792]{1,0:T(8,128)(2,1)S(1)}, bf16[80,1792]{1,0:T(8,128)(2,1)S(1)}, u32[]{:S(2)}, u32[]{:S(2)}) collective-permute-start(bf16[80,1792]{1,0:T(8,128)(2,1)S(1)} %get-tuple-element.152), channel_id=1, source_target_pairs={{0,1},{1,5},{2,0},{3,4},{4,3},{5,7},{6,2},{7,6},{8,9},{9,13},{10,8... | collective-permute-start | bytes 860168 | tf_op jit(solution)/shard_map/ppermute | solution.py:440
  632.1 27.9 %collective-permute-start.35 = (bf16[80,1792]{1,0:T(8,128)(2,1)S(1)}, bf16[80,1792]{1,0:T(8,128)(2,1)S(1)}, u32[]{:S(2)}, u32[]{:S(2)}) collective-permute-start(bf16[80,1792]{1,0:T(8,128)(2,1)S(1)} %get-tuple-element.149), channel_id=1, source_target_pairs={{0,0},{1,4},{2,1},{3,5},{4,2},{5,6},{6,3},{7,7},{8,8},{9,12},{10,9... | collective-permute-start | bytes 860168 | tf_op jit(solution)/shard_map/ppermute | solution.py:440
  654.7 31.7 %collective-permute-start.30 = (bf16[256,2560]{1,0:T(8,128)(2,1)S(1)}, bf16[256,2560]{1,0:T(8,128)(2,1)S(1)}, u32[]{:S(2)}, u32[]{:S(2)}) collective-permute-start(bf16[256,2560]{1,0:T(8,128)(2,1)S(1)} %copy-done.25), channel_id=1, source_target_pairs={{0,2},{2,0},{4,6},{6,4},{1,3},{3,1},{5,7},{7,5},{8,10},{10,8},{12,... | collective-permute-start | bytes 3932168 | tf_op jit(solution)/shard_map/ppermute | solution.py:296
  657.7 69.9 %collective-permute-start.32 = (bf16[320,1024]{1,0:T(8,128)(2,1)}, bf16[320,1024]{1,0:T(8,128)(2,1)}, u32[]{:S(2)}, u32[]{:S(2)}) collective-permute-start(bf16[320,1024]{1,0:T(8,128)(2,1)} %get-tuple-element.120), channel_id=1, source_target_pairs={{0,16},{8,24},{16,0},{24,8},{1,17},{9,25},{17,1},{25,9},{2,18},{10... | collective-permute-start | bytes 1966088 | tf_op jit(solution)/shard_map/ppermute | solution.py:458
  660.0 34.8 %collective-permute-start.34 = (bf16[4,320,640]{2,1,0:T(8,128)(2,1)}, bf16[4,320,640]{2,1,0:T(8,128)(2,1)}, u32[]{:S(2)}, u32[]{:S(2)}) collective-permute-start(bf16[4,320,640]{2,1,0:T(8,128)(2,1)} %dynamic-slice_bitcast_fusion.1), channel_id=1, source_target_pairs={{0,1},{1,0},{2,3},{3,2},{4,5},{5,4},{6,7},{7,6},{8,9},{9,8},{10,11... | collective-permute-start | bytes 4915208 | tf_op jit(solution)/shard_map/ppermute | solution.py:404
  660.0 37.1 %collective-permute-start.33 = (bf16[4,320,640]{2,1,0:T(8,128)(2,1)}, bf16[4,320,640]{2,1,0:T(8,128)(2,1)}, u32[]{:S(2)}, u32[]{:S(2)}) collective-permute-start(bf16[4,320,640]{2,1,0:T(8,128)(2,1)} %dynamic-slice_bitcast_fusion.2), channel_id=1, source_target_pairs={{0,1},{1,0},{2,3},{3,2},{4,5},{5,4},{6,7},{7,6},{8,9},{9,8},{10,11... | collective-permute-start | bytes 4915208 | tf_op jit(solution)/shard_map/ppermute | solution.py:404
  662.4 65.3 %collective-permute-start.40 = (bf16[320,1024]{1,0:T(8,128)(2,1)}, bf16[320,1024]{1,0:T(8,128)(2,1)}, u32[]{:S(2)}, u32[]{:S(2)}) collective-permute-start(bf16[320,1024]{1,0:T(8,128)(2,1)} %get-tuple-element.119), channel_id=1, source_target_pairs={{0,24},{8,16},{16,8},{24,0},{1,25},{9,17},{17,9},{25,1},{2,26},{10... | collective-permute-start | bytes 1966088 | tf_op jit(solution)/shard_map/ppermute | solution.py:458
  686.4 58.4 %collective-permute-start.39 = (bf16[320,1024]{1,0:T(8,128)(2,1)}, bf16[320,1024]{1,0:T(8,128)(2,1)}, u32[]{:S(2)}, u32[]{:S(2)}) collective-permute-start(bf16[320,1024]{1,0:T(8,128)(2,1)} %get-tuple-element.118), channel_id=1, source_target_pairs={{0,8},{8,0},{16,24},{24,16},{1,9},{9,1},{17,25},{25,17},{2,10},{10... | collective-permute-start | bytes 1966088 | tf_op jit(solution)/shard_map/ppermute | solution.py:458
  761.6 17.1 %collective-permute-start.42 = (bf16[128,2560]{1,0:T(8,128)(2,1)}, bf16[128,2560]{1,0:T(8,128)(2,1)}, u32[]{:S(2)}, u32[]{:S(2)}) collective-permute-start(bf16[128,2560]{1,0:T(8,128)(2,1)} %get-tuple-element.137), channel_id=1, source_target_pairs={{0,4},{2,6},{4,0},{6,2},{1,5},{3,7},{5,1},{7,3},{8,12},{10,14},{12... | collective-permute-start | bytes 1966088 | tf_op jit(solution)/shard_map/ppermute | solution.py:296
  782.3 30.0 %collective-permute-start.45 = (bf16[256,2560]{1,0:T(8,128)(2,1)}, bf16[256,2560]{1,0:T(8,128)(2,1)}, u32[]{:S(2)}, u32[]{:S(2)}) collective-permute-start(bf16[256,2560]{1,0:T(8,128)(2,1)} %pad_maximum_fusion.14), channel_id=1, source_target_pairs={{0,4},{2,6},{4,0},{6,2},{1,5},{3,7},{5,1},{7,3},{8,12},{10,14},{12... | collective-permute-start | bytes 3932168 | tf_op jit(solution)/shard_map/ppermute | solution.py:296
  784.1 29.9 %collective-permute-start.43 = (bf16[256,2560]{1,0:T(8,128)(2,1)}, bf16[256,2560]{1,0:T(8,128)(2,1)}, u32[]{:S(2)}, u32[]{:S(2)}) collective-permute-start(bf16[256,2560]{1,0:T(8,128)(2,1)} %pad_maximum_fusion.13), channel_id=1, source_target_pairs={{0,2},{2,0},{4,6},{6,4},{1,3},{3,1},{5,7},{7,5},{8,10},{10,8},{12,... | collective-permute-start | bytes 3932168 | tf_op jit(solution)/shard_map/ppermute | solution.py:296
  816.9 18.7 %collective-permute-start.53 = (bf16[80,3584]{1,0:T(8,128)(2,1)S(1)}, bf16[80,3584]{1,0:T(8,128)(2,1)S(1)}, u32[]{:S(2)}, u32[]{:S(2)}) collective-permute-start(bf16[80,3584]{1,0:T(8,128)(2,1)S(1)} %get-tuple-element.134), channel_id=1, source_target_pairs={{0,3},{1,7},{2,2},{3,6},{4,1},{5,5},{6,0},{7,4},{8,11},{9,15},{10,... | collective-permute-start | bytes 1720328 | tf_op jit(solution)/shard_map/ppermute | solution.py:440
  818.9 25.8 %collective-permute-start.52 = (bf16[80,3584]{1,0:T(8,128)(2,1)S(1)}, bf16[80,3584]{1,0:T(8,128)(2,1)S(1)}, u32[]{:S(2)}, u32[]{:S(2)}) collective-permute-start(bf16[80,3584]{1,0:T(8,128)(2,1)S(1)} %get-tuple-element.135), channel_id=1, source_target_pairs={{0,2},{1,6},{2,3},{3,7},{4,0},{5,4},{6,1},{7,5},{8,10},{9,14},{10,... | collective-permute-start | bytes 1720328 | tf_op jit(solution)/shard_map/ppermute | solution.py:440
  819.1 25.6 %collective-permute-start.51 = (bf16[80,3584]{1,0:T(8,128)(2,1)S(1)}, bf16[80,3584]{1,0:T(8,128)(2,1)S(1)}, u32[]{:S(2)}, u32[]{:S(2)}) collective-permute-start(bf16[80,3584]{1,0:T(8,128)(2,1)S(1)} %get-tuple-element.136), channel_id=1, source_target_pairs={{0,1},{1,5},{2,0},{3,4},{4,3},{5,7},{6,2},{7,6},{8,9},{9,13},{10,8... | collective-permute-start | bytes 1720328 | tf_op jit(solution)/shard_map/ppermute | solution.py:440
  822.0 22.7 %collective-permute-start.50 = (bf16[80,3584]{1,0:T(8,128)(2,1)S(1)}, bf16[80,3584]{1,0:T(8,128)(2,1)S(1)}, u32[]{:S(2)}, u32[]{:S(2)}) collective-permute-start(bf16[80,3584]{1,0:T(8,128)(2,1)S(1)} %get-tuple-element.133), channel_id=1, source_target_pairs={{0,0},{1,4},{2,1},{3,5},{4,2},{5,6},{6,3},{7,7},{8,8},{9,12},{10,9... | collective-permute-start | bytes 1720328 | tf_op jit(solution)/shard_map/ppermute | solution.py:440
  (61 other events, 1240.7 us)
Sparse Core Ops, SparseCore 0:
  14.0 85.8 all-gather.4
  112.5 53.2 all-gather.6
  168.0 162.7 all-gather.8
  332.3 86.7 all-gather.10
  421.3 95.4 reduce-scatter.3
  519.0 218.5 reduce-scatter.5
  763.9 80.7 reduce-scatter.7

commit v5 on v4

--- a/solution.py
+++ b/solution.py
@@ -327,11 +327,12 @@
     return for_first, for_second
 
 
-def given(left, right, for_first, for_second):
+def given(left, right, for_first, for_second, after=()):
     block = left.shape[0] // CHIPS
-    from_first = swap(for_first, 1).astype(jnp.float32)
-    from_second = swap(for_second, 2).astype(jnp.float32)
-    return times_t(left[:block], right) + from_first + from_second
+    from_first, from_second = swap(for_first, 1), swap(for_second, 2)
+    from_first, from_second, _ = lax.optimization_barrier((from_first, from_second, after))
+    own = times_t(left[:block], right)
+    return own + from_first.astype(jnp.float32) + from_second.astype(jnp.float32)
 
 
 def shards(
@@ -403,6 +404,13 @@
     def beside(value):
         return lax.ppermute(value, "core", [(0, 1), (1, 0)])
 
+    def pair_of(normed):
+        rows = normed.T.reshape(groups, 2, half_rows, tokens)
+        own = lax.dynamic_index_in_dim(rows, core, axis=1, keepdims=False)
+        out = lax.dynamic_index_in_dim(rows, 1 - core, axis=1, keepdims=False)
+        pair = jnp.concatenate([own, beside(out)], axis=2)
+        return pair.reshape(groups * half_rows, 2 * tokens)
+
     def across(total):
         halves = total.reshape(groups, 2, half_rows, total.shape[1])
         own = lax.dynamic_index_in_dim(halves, core, axis=1, keepdims=False)
@@ -475,12 +483,8 @@
     gated, lifted = both_up[:, :wide], both_up[:, wide:]
     activated = jax.nn.silu(gated)
     hidden = (activated * lifted).astype(jnp.bfloat16)
-    normed_rows = normed_one.T.reshape(groups, 2, half_rows, tokens)
-    own_rows = lax.dynamic_index_in_dim(normed_rows, core, axis=1, keepdims=False)
-    other_rows = lax.dynamic_index_in_dim(normed_rows, 1 - core, axis=1, keepdims=False)
-    pair_rows = jnp.concatenate([own_rows, beside(other_rows)], axis=2)
-    pair_rows = pair_rows.reshape(groups * half_rows, 2 * tokens)
-    hidden, pair_rows = then((hidden, pair_rows))
+    pair_rows, pair_rows_two = pair_of(normed_one), pair_of(normed_two)
+    hidden, pair_rows, pair_rows_two = then((hidden, pair_rows, pair_rows_two))
     total_down, w_sink = then((product_low(grad_low, hidden), w_sink))
     sum_down = reduced(total_down)
 
@@ -491,10 +495,12 @@
     ).astype(jnp.bfloat16)
     grad_lift_low = (grad_hidden * activated).astype(jnp.bfloat16)
     grad_both = jnp.concatenate([grad_gate_low, grad_lift_low], axis=1)
-    grad_normed_two = give_back(grad_both, w_lift)
-    total_lift = product_low(normed_two, grad_both)
-    grad_normed_two, sum_down, total_lift = then((grad_normed_two, sum_down, total_lift))
-    sum_lift = reduced(total_lift)
+    pair_both = jnp.concatenate([grad_both, beside(grad_both)], axis=0)
+    total_lift = times(pair_rows_two, pair_both).astype(jnp.bfloat16)
+    grad_normed_two = given(
+        grad_both, w_lift, *to_give(grad_both, w_lift), (sum_down, total_lift)
+    )
+    sum_lift = reduced(total_lift, ("group", "dp"))
     grad_middle = out_grad[0].astype(jnp.float32) + norm_back(
         grad_normed_two, middle, inverse_two, gain_two
     )

time: 897 us -> 879 us (0.980)
  waiting for transfers between devices: 334 us -> 298 us
  other arithmetic: 81.5 us -> 102 us
  local copies, waits for them, and re-layouts: 75.2 us -> 87.3 us
    all_gather x3, waiting for transfers between devices: 109 us -> 40.7 us  [gathered(): return lax.all_gather(part, ('group', 'core'), axis=0, tiled=True)]
    dot_general x4 -> x3, matrix products: 55.3 us -> 26 us  [inner_t(): lax.dot_general(left, right, (((0,), (0,)), ((), ())), preferred_element_...]
    dot_general x5 -> x6, matrix products: 62.6 us -> 90.7 us  [times(): return jnp.dot(left, right, preferred_element_type=jnp.float32)]
    all_gather x1, waiting for transfers between devices: 6.17 us -> 33 us  [shards(): kv_all = lax.all_gather(kv_own_tokens, 'group', axis=0, tiled=True)]
    ppermute x35, waiting for transfers between devices: 141 us -> 167 us  [swap(): return lax.ppermute(value, 'chip', pairs)]
    ppermute x3, waiting for transfers between devices: 43 us -> 23 us  [from_group(): lax.ppermute(lax.dynamic_index_in_dim(values, group_at ^ step, axis=0, ke...]
    concatenate x1 -> x4, other arithmetic: 2.75 us -> 16.6 us  [the longest x2 9.47 us: pair_of(): pair = jnp.concatenate([own, beside(out)], axis=2)]
    unnamed x102 -> x100, local copies, waits for them, and re-layouts: 21.4 us -> 20.3 us
  transfers between devices with their start and end apart: 61 -> 63, of which waited for: 32 -> 29; matrix products, arithmetic and copies ran while one was open for 38% -> 42% of each run, Pallas kernels for 8% -> 8%
where the time goes in v5:
time: 879 us; the launch traced here: 869 us
  waiting for transfers between devices  298 us (34%)
  matrix products  215 us (24%)
  other arithmetic  102 us (12%)
  local copies, waits for them, and re-layouts  87.3 us (10%)
  Pallas kernels  66.3 us (8%)
  starting transfers between devices  65 us (7%)
  between operations  21 us (2%)
  blocking collectives  13.4 us (2%)
    ppermute x35, waiting for transfers between devices, swap(): return lax.ppermute(value, 'chip', pairs)  167 us
    dot_general x6, matrix products, times(): return jnp.dot(left, right, preferred_element_type=jnp.float32)  90.7 us
    dot_general x13, matrix products, times_t(): lax.dot_general(left, right, (((1,), (1,)), ((), ())), preferred_element_...  89.2 us
    pallas_call x3, Pallas kernels, attend_back(): pl.pallas_call(kernel, out_shape=(jax.ShapeDtypeStruct((tokens, query_wid...  45.4 us
    ppermute x35, starting transfers between devices, swap(): return lax.ppermute(value, 'chip', pairs)  42.6 us
    all_gather x3, waiting for transfers between devices, gathered(): return lax.all_gather(part, ('group', 'core'), axis=0, tiled=True)  40.7 us
    all_gather x1, waiting for transfers between devices, shards(): kv_all = lax.all_gather(kv_own_tokens, 'group', axis=0, tiled=True)  33 us
    ppermute x12, waiting for transfers between devices, owned(): pieces.append(lax.ppermute(block, REPLICA, pairs))  30.2 us
  transfers between devices with their start and end apart: 63, of which 29 were waited for; matrix products, arithmetic and copies ran while one was open for 42% of the time, Pallas kernels for 8%

profile of v5, /device:TPU:0, one launch (start us, length us, event | category | flops | bytes accessed | tf_op | source)
XLA Modules:
  0.0 869.2 jit_solution(9113976309266391032)
XLA Ops:
  22.0 13.4 %all_gather.16 = bf16[2,2560]{1,0:T(2,128)(2,1)S(1)} all-gather(bf16[2,640]{1,0:T(2,128)(2,1)S(1)} %pad_maximum_fusion.23), channel_id=1, replica_groups=mesh['group'=4,'dp'=1,'chip'=4,'core'=2] {'group'}, dimensions={1}, use_global_device_ids=true | all-gather | bytes 12800 | tf_op jit(solution)/shard_map/all_gather | solution.py:375
  35.6 11.5 %collective-permute-done.6 = s32[258]{0:T(512)S(1)} collective-permute-done((s32[258]{0:T(512)S(1)}, s32[258]{0:T(512)S(1)}, u32[]{:S(2)}, u32[]{:S(2)}) %collective-permute-start.6) | collective-permute-done | bytes 1064 | tf_op jit(solution)/shard_map/ppermute | solution.py:296
  50.4 13.1 %collective-permute-done.2 = bf16[128,2560]{1,0:T(8,128)(2,1)S(1)} collective-permute-done((bf16[128,2560]{1,0:T(8,128)(2,1)S(1)}, bf16[128,2560]{1,0:T(8,128)(2,1)S(1)}, u32[]{:S(2)}, u32[]{:S(2)}) %collective-permute-start.2) | collective-permute-done | bytes 655392 | tf_op jit(solution)/shard_map/ppermute | solution.py:296
  67.1 32.8 %all-gather.5.cloned.1.call-done = bf16[2560,1600]{1,0:T(8,128)(2,1)} async-done(((bf16[320,1600]{1,0:T(8,128)(2,1)}), bf16[2560,1600]{1,0:T(8,128)(2,1)}) %all-gather.5.cloned.1.call-update) | async-done | bytes 8192016 | tf_op jit(solution)/shard_map/all_gather | solution.py:373
  99.9 9.5 %fusion.25 = f32[960,1024]{1,0:T(8,128)S(1)} fusion(bf16[2560,1600]{1,0:T(8,128)(2,1)} %all-gather.5.cloned.1.call-done, bf16[1024,2560]{1,0:T(8,128)(2,1)} %copy-done.2, f32[2560]{0:T(1024)S(1)} %get-tuple-element.91, f32[1024]{0:T(1024)S(1)} %add_rsqrt_fusion), kind=kOutput, calls=%fused_computation.54 | convolution fusion | flops 5043650560 | bytes 14432256 | tf_op jit(solution)/shard_map/dot_general | solution.py:393
  132.8 33.0 %all-gather.7.cloned.1.call-done = bf16[1280,1024]{1,0:T(8,128)(2,1)} async-done(((bf16[320,1024]{1,0:T(8,128)(2,1)}), bf16[1280,1024]{1,0:T(8,128)(2,1)}) %all-gather.7.cloned.1.call-update) | async-done | bytes 2621456 | tf_op jit(solution)/shard_map/all_gather | solution.py:401
  165.8 20.8 %attend.1 = (bf16[1024,640]{1,0:T(8,128)(2,1)}, f32[4,8,256]{2,1,0:T(8,128)}) custom-call(bf16[640,1024]{1,0:T(8,128)(2,1)} %bitcast.182, bf16[4,320,1024]{2,1,0:T(8,128)(2,1)} %bitcast.193, s32[4,1,256]{2,1,0:T(1,128)} %broadcast_in_dim.39.refs_2_), custom_call_target="tpu_custom_call" | custom-call | flops 2684354560 | bytes 5242880 | tf_op jit(solution)/shard_map/attend/pallas_call | solution.py:99
  198.1 8.8 %collective-permute-done.9 = bf16[128,2560]{1,0:T(8,128)(2,1)S(1)} collective-permute-done((bf16[128,2560]{1,0:T(8,128)(2,1)S(1)}, bf16[128,2560]{1,0:T(8,128)(2,1)S(1)}, u32[]{:S(2)}, u32[]{:S(2)}) %collective-permute-start.9) | collective-permute-done | bytes 655392 | tf_op jit(solution)/shard_map/ppermute | solution.py:296
  218.8 20.6 %collective-permute-done.8 = bf16[256,2560]{1,0:T(8,128)(2,1)} collective-permute-done((bf16[256,2560]{1,0:T(8,128)(2,1)}, bf16[256,2560]{1,0:T(8,128)(2,1)}, u32[]{:S(2)}, u32[]{:S(2)}) %collective-permute-start.8) | collective-permute-done | bytes 1310752 | tf_op jit(solution)/shard_map/ppermute | solution.py:296
  250.9 6.1 fusion.102
  257.0 8.3 copy.39
  265.4 4.9 constant_dynamic-slice_fusion.7
  270.2 8.7 collective-permute-done.11
  289.3 29.3 %collective-permute-done.13 = bf16[128,2560]{1,0:T(8,128)(2,1)S(1)} collective-permute-done((bf16[128,2560]{1,0:T(8,128)(2,1)S(1)}, bf16[128,2560]{1,0:T(8,128)(2,1)S(1)}, u32[]{:S(2)}, u32[]{:S(2)}) %collective-permute-start.13) | collective-permute-done | bytes 655392 | tf_op jit(solution)/shard_map/ppermute | solution.py:296
  320.3 8.0 copy.40
  340.5 10.9 %collective-permute-done.19 = bf16[128,2560]{1,0:T(8,128)(2,1)S(1)} collective-permute-done((bf16[128,2560]{1,0:T(8,128)(2,1)S(1)}, bf16[128,2560]{1,0:T(8,128)(2,1)S(1)}, u32[]{:S(2)}, u32[]{:S(2)}) %collective-permute-start.19) | collective-permute-done | bytes 655392 | tf_op jit(solution)/shard_map/ppermute | solution.py:296
  353.8 6.7 pad_maximum_fusion.1
  363.3 27.5 %fusion.129 = f32[1024,3584]{1,0:T(8,128)} fusion(bf16[1024,2560]{1,0:T(8,128)(2,1)} %constant_dynamic-update-slice_fusion.5, bf16[2560,3584]{1,0:T(8,128)(2,1)} %all-gather.9.cloned.1.call-done), kind=kOutput, calls=%fused_computation.311 | convolution fusion | flops 18790481920 | bytes 38273024 | tf_op jit(solution)/shard_map/dot_general | solution.py:261
  390.7 6.6 multiply_convert_fusion.2
  399.2 12.0 %convolution_convert_fusion.1 = bf16[2560,1792]{1,0:T(8,128)(2,1)} fusion(bf16[1024,2560]{1,0:T(8,128)(2,1)S(1)} %copy-done.28, bf16[1024,1792]{1,0:T(8,128)(2,1)S(1)} %multiply_convert_fusion.2), kind=kOutput, calls=%fused_computation.8 | convolution fusion | flops 9399828480 | bytes 18087936 | tf_op jit(solution)/shard_map/dot_general | solution.py:271
  411.1 8.0 all-gather.11.cloned.1.call-done
  420.5 20.9 %multiply_convert_fusion = (bf16[1024,1792]{1,0:T(8,128)(2,1)S(1)}, bf16[1024,1792]{1,0:T(8,128)(2,1)}) fusion(f32[1024,3584]{1,0:T(8,128)} %fusion.129, bf16[1024,2560]{1,0:T(8,128)(2,1)} %copy-done.27, bf16[2560,1792]{1,0:T(8,128)(2,1)} %all-gather.11.cloned.1.call-done), kind=kOutput, calls=%fused_computation.19 | convolution fusion | flops 9417261056 | bytes 36438016 | tf_op jit(solution)/shard_map/dot_general | solution.py:261
  441.3 6.9 pad_maximum_fusion
  448.5 9.2 %convolution_convert_fusion.9 = bf16[256,2560]{1,0:T(8,128)(2,1)S(1)} fusion(bf16[2560,3584]{1,0:T(8,128)(2,1)} %all-gather.9.cloned.1.call-done, bf16[1024,1792]{1,0:T(8,128)(2,1)} %get-tuple-element.110, bf16[1024,1792]{1,0:T(8,128)(2,1)S(1)} %get-tuple-element.109), kind=kOutput, calls=%fused_computation.47 | convolution fusion | flops 4701945856 | bytes 27000832 | tf_op jit(solution)/shard_map/dot_general | solution.py:265
  460.9 15.2 %convolution_convert_fusion.3 = bf16[512,2560]{1,0:T(8,128)(2,1)} fusion(bf16[2560,3584]{1,0:T(8,128)(2,1)} %all-gather.9.cloned.1.call-done, bf16[1024,1792]{1,0:T(8,128)(2,1)} %get-tuple-element.110, bf16[1024,1792]{1,0:T(8,128)(2,1)S(1)} %get-tuple-element.109), kind=kOutput, calls=%fused_computation.40 | convolution fusion | flops 9403891712 | bytes 28311552 | tf_op jit(solution)/shard_map/dot_general | solution.py:265
  483.3 26.6 %convolution_convert_fusion = bf16[1280,3584]{1,0:T(8,128)(2,1)} fusion(bf16[1280,2048]{1,0:T(8,128)(2,1)} %pad_maximum_fusion.2, bf16[1024,3584]{1,0:T(8,128)(2,1)} %collective-permute-done.25, bf16[1024,1792]{1,0:T(8,128)(2,1)} %copy-done.12, bf16[1024,1792]{1,0:T(8,128)(2,1)} %get-tuple-element.110), kind=kOutput, calls=%fused_computation | convolution fusion | flops 18839109632 | bytes 29097984 | tf_op jit(solution)/shard_map/dot_general | solution.py:261
  516.8 11.5 %multiply_reduce_fusion.1 = (f32[256]{0:T(256)S(1)}, f32[256,2560]{1,0:T(8,128)S(1)}) fusion(f32[256,2560]{1,0:T(8,128)S(1)} %copy-done.1, f32[2560]{0:T(1024)S(1)} %copy-done.32, bf16[256,2560]{1,0:T(8,128)(2,1)} %collective-permute-done.24, bf16[256,2560]{1,0:T(8,128)(2,1)} %collective-permute-done.22, ...), kind=kOutput, calls=%fused_computation.76 | convolution fusion | flops 4705878016 | bytes 33565696 | tf_op jit(solution)/shard_map/dot_general | solution.py:265
  528.3 5.3 fusion.104
  536.3 4.8 fusion.65.refs_5_
  541.1 11.7 %attend_back.3 = (bf16[1024,640]{1,0:T(8,128)(2,1)}, bf16[4,320,1024]{2,1,0:T(8,128)(2,1)}) custom-call(bf16[640,1024]{1,0:T(8,128)(2,1)} %bitcast.183, bf16[4,320,1024]{2,1,0:T(8,128)(2,1)} %bitcast.194, s32[4,1,256]{2,1,0:T(1,128)} %broadcast_in_dim.39.refs_2_, f32[4,8,256]{2,1,0:T(8,128)} %get-tuple-element.53.refs_3_, ...), custom_call_target="tpu_custom_call" | custom-call | flops 1677721600 | bytes 2621440 | tf_op jit(solution)/shard_map/attend_back/pallas_call | solution.py:224
  552.8 6.9 convolution_convert_fusion.8
  561.1 7.7 fusion.74
  568.8 8.8 %convolution_convert_fusion.5 = bf16[512,2560]{1,0:T(8,128)(2,1)S(1)} fusion(bf16[2560,1792]{1,0:T(8,128)(2,1)} %all-gather.11.cloned.1.call-done, bf16[1024,1792]{1,0:T(8,128)(2,1)S(1)} %copy-done.14), kind=kOutput, calls=%fused_computation.42 | convolution fusion | flops 4698931200 | bytes 13631488 | tf_op jit(solution)/shard_map/dot_general | solution.py:265
  587.1 6.4 fusion.46.refs_5_
  593.4 22.0 %attend_back.4 = (bf16[1024,640]{1,0:T(8,128)(2,1)}, bf16[4,320,1024]{2,1,0:T(8,128)(2,1)}) custom-call(bf16[640,1024]{1,0:T(8,128)(2,1)} %bitcast.184, bf16[4,320,1024]{2,1,0:T(8,128)(2,1)} %bitcast.195, s32[4,1,256]{2,1,0:T(1,128)} %broadcast_in_dim.39.refs_2_, ...), custom_call_target="tpu_custom_call", output_to_operand_aliasing={{0}: (8, {}), {1}: (9, {})} | custom-call | flops 3355443200 | bytes 5242880 | tf_op jit(solution)/shard_map/attend_back/pallas_call | solution.py:224
  621.5 11.8 %attend_back.5 = (bf16[1024,640]{1,0:T(8,128)(2,1)}, bf16[4,320,1024]{2,1,0:T(8,128)(2,1)}) custom-call(bf16[640,1024]{1,0:T(8,128)(2,1)} %bitcast.185, bf16[4,320,1024]{2,1,0:T(8,128)(2,1)} %bitcast.196, s32[4,1,256]{2,1,0:T(1,128)} %broadcast_in_dim.39.refs_2_, ...), custom_call_target="tpu_custom_call", output_to_operand_aliasing={{0}: (8, {}), {1}: (9, {})} | custom-call | flops 1677721600 | bytes 2621440 | tf_op jit(solution)/shard_map/attend_back/pallas_call | solution.py:224
  640.2 6.9 fusion.16
  649.5 7.1 convolution_convert_fusion.2
  668.7 24.8 %collective-permute-done.33 = bf16[256,2560]{1,0:T(8,128)(2,1)S(1)} collective-permute-done((bf16[256,2560]{1,0:T(8,128)(2,1)S(1)}, bf16[256,2560]{1,0:T(8,128)(2,1)S(1)}, u32[]{:S(2)}, u32[]{:S(2)}) %collective-permute-start.33) | collective-permute-done | bytes 1310752 | tf_op jit(solution)/shard_map/ppermute | solution.py:296
  707.1 23.0 %collective-permute-done.34 = bf16[320,1024]{1,0:T(8,128)(2,1)} collective-permute-done((bf16[320,1024]{1,0:T(8,128)(2,1)}, bf16[320,1024]{1,0:T(8,128)(2,1)}, u32[]{:S(2)}, u32[]{:S(2)}) %collective-permute-start.34) | collective-permute-done | bytes 655392 | tf_op jit(solution)/shard_map/ppermute | solution.py:466
  749.8 5.4 convolution_convert_fusion.4
  755.3 8.6 collective-permute-done.46
  779.4 18.2 %collective-permute-done.45 = bf16[256,2560]{1,0:T(8,128)(2,1)} collective-permute-done((bf16[256,2560]{1,0:T(8,128)(2,1)}, bf16[256,2560]{1,0:T(8,128)(2,1)}, u32[]{:S(2)}, u32[]{:S(2)}) %collective-permute-start.45) | collective-permute-done | bytes 1310752 | tf_op jit(solution)/shard_map/ppermute | solution.py:296
  810.8 10.2 %collective-permute-done.55 = bf16[80,3584]{1,0:T(8,128)(2,1)S(1)} collective-permute-done((bf16[80,3584]{1,0:T(8,128)(2,1)S(1)}, bf16[80,3584]{1,0:T(8,128)(2,1)S(1)}, u32[]{:S(2)}, u32[]{:S(2)}) %collective-permute-start.55) | collective-permute-done | bytes 573472 | tf_op jit(solution)/shard_map/ppermute | solution.py:448
  821.0 9.6 %collective-permute-done.54 = bf16[80,3584]{1,0:T(8,128)(2,1)S(1)} collective-permute-done((bf16[80,3584]{1,0:T(8,128)(2,1)S(1)}, bf16[80,3584]{1,0:T(8,128)(2,1)S(1)}, u32[]{:S(2)}, u32[]{:S(2)}) %collective-permute-start.54) | collective-permute-done | bytes 573472 | tf_op jit(solution)/shard_map/ppermute | solution.py:448
  837.6 6.1 collective-permute-start.51
  845.8 4.7 collective-permute-done.51
  850.5 5.7 collective-permute-done.50
  (369 shorter events, 242.1 us)
Async XLA Ops:
  7.2 92.7 %all-gather.5.cloned.1.call-start = ((), (), s32[]{:S(2)}) async-start(), calls=%async_computation.3 | async-start | bytes 9584640 | tf_op jit(solution)/shard_map/all_gather | solution.py:373
  13.8 152.0 %all-gather.7.cloned.1.call-start = ((), (), s32[]{:S(2)}) async-start(), calls=%async_computation.4 | async-start | bytes 3276800 | tf_op jit(solution)/shard_map/all_gather | solution.py:401
  13.9 34.0 %collective-permute-start = (bf16[256,2560]{1,0:T(8,128)(2,1)S(1)}, bf16[256,2560]{1,0:T(8,128)(2,1)S(1)}, u32[]{:S(2)}, u32[]{:S(2)}) collective-permute-start(bf16[256,2560]{1,0:T(8,128)(2,1)S(1)} %bitcast.175), channel_id=1, source_target_pairs={{0,2},{2,0},{4,6},{6,4},{1,3},{3,1},{5,7},{7,5},{8,10},{10,8},{12,... | collective-permute-start | bytes 3932168 | tf_op jit(solution)/shard_map/ppermute | solution.py:296
  16.9 32.6 %collective-permute-start.1 = (bf16[256,2560]{1,0:T(8,128)(2,1)S(1)}, bf16[256,2560]{1,0:T(8,128)(2,1)S(1)}, u32[]{:S(2)}, u32[]{:S(2)}) collective-permute-start(bf16[256,2560]{1,0:T(8,128)(2,1)S(1)} %bitcast.176), channel_id=1, source_target_pairs={{0,4},{2,6},{4,0},{6,2},{1,5},{3,7},{5,1},{7,3},{8,12},{10,14},{12... | collective-permute-start | bytes 3932168 | tf_op jit(solution)/shard_map/ppermute | solution.py:296
  18.4 28.7 %collective-permute-start.6 = (s32[258]{0:T(512)S(1)}, s32[258]{0:T(512)S(1)}, u32[]{:S(2)}, u32[]{:S(2)}) collective-permute-start(s32[258]{0:T(512)S(1)} %pad_add_fusion.4), channel_id=1, source_target_pairs={{0,6},{2,4},{4,2},{6,0},{1,7},{3,5},{5,3},{7,1},{8,14},{10,12},{12... | collective-permute-start | bytes 3104 | tf_op jit(solution)/shard_map/ppermute | solution.py:296
  18.5 28.7 %collective-permute-start.5 = (s32[258]{0:T(512)S(1)}, s32[258]{0:T(512)S(1)}, u32[]{:S(2)}, u32[]{:S(2)}) collective-permute-start(s32[258]{0:T(512)S(1)} %pad_add_fusion.4), channel_id=1, source_target_pairs={{0,4},{2,6},{4,0},{6,2},{1,5},{3,7},{5,1},{7,3},{8,12},{10,14},{12... | collective-permute-start | bytes 3104 | tf_op jit(solution)/shard_map/ppermute | solution.py:296
  20.5 26.7 %collective-permute-start.4 = (s32[258]{0:T(512)S(1)}, s32[258]{0:T(512)S(1)}, u32[]{:S(2)}, u32[]{:S(2)}) collective-permute-start(s32[258]{0:T(512)S(1)} %pad_add_fusion.4), channel_id=1, source_target_pairs={{0,2},{2,0},{4,6},{6,4},{1,3},{3,1},{5,7},{7,5},{8,10},{10,8},{12,... | collective-permute-start | bytes 3104 | tf_op jit(solution)/shard_map/ppermute | solution.py:296
  112.4 250.9 %all-gather.9.cloned.1.call-start = ((), (), s32[]{:S(2)}) async-start(), calls=%async_computation.5 | async-start | bytes 20643840 | tf_op jit(solution)/shard_map/all_gather | solution.py:373
  115.6 303.5 %all-gather.11.cloned.1.call-start = ((), (), s32[]{:S(2)}) async-start(), calls=%async_computation.6 | async-start | bytes 10321920 | tf_op jit(solution)/shard_map/all_gather | solution.py:373
  209.6 29.7 %collective-permute-start.8 = (bf16[256,2560]{1,0:T(8,128)(2,1)}, bf16[256,2560]{1,0:T(8,128)(2,1)}, u32[]{:S(2)}, u32[]{:S(2)}) collective-permute-start(bf16[256,2560]{1,0:T(8,128)(2,1)} %pad_maximum_fusion.6), channel_id=1, source_target_pairs={{0,2},{2,0},{4,6},{6,4},{1,3},{3,1},{5,7},{7,5},{8,10},{10,8},{12,... | collective-permute-start | bytes 3932168 | tf_op jit(solution)/shard_map/ppermute | solution.py:296
  211.3 29.5 %collective-permute-start.10 = (bf16[256,2560]{1,0:T(8,128)(2,1)}, bf16[256,2560]{1,0:T(8,128)(2,1)}, u32[]{:S(2)}, u32[]{:S(2)}) collective-permute-start(bf16[256,2560]{1,0:T(8,128)(2,1)} %pad_maximum_fusion.7), channel_id=1, source_target_pairs={{0,4},{2,6},{4,0},{6,2},{1,5},{3,7},{5,1},{7,3},{8,12},{10,14},{12... | collective-permute-start | bytes 3932168 | tf_op jit(solution)/shard_map/ppermute | solution.py:296
  215.2 301.6 %reduce-scatter.4.cloned.1.call-start = ((), (), s32[]{:S(2)}) async-start(), calls=%async_computation.7 | async-start | bytes 10321920 | tf_op jit(solution)/shard_map/reduce_scatter | solution.py:423
  246.9 32.0 %collective-permute-start.11 = (bf16[256,2560]{1,0:T(8,128)(2,1)}, bf16[256,2560]{1,0:T(8,128)(2,1)}, u32[]{:S(2)}, u32[]{:S(2)}) collective-permute-start(bf16[256,2560]{1,0:T(8,128)(2,1)} %get-tuple-element.106), channel_id=1, source_target_pairs={{0,2},{2,0},{4,6},{6,4},{1,3},{3,1},{5,7},{7,5},{8,10},{10,8},{12,... | collective-permute-start | bytes 3932168 | tf_op jit(solution)/shard_map/ppermute | solution.py:296
  248.3 33.3 %collective-permute-start.12 = (bf16[256,2560]{1,0:T(8,128)(2,1)}, bf16[256,2560]{1,0:T(8,128)(2,1)}, u32[]{:S(2)}, u32[]{:S(2)}) collective-permute-start(bf16[256,2560]{1,0:T(8,128)(2,1)} %get-tuple-element.106), channel_id=1, source_target_pairs={{0,4},{2,6},{4,0},{6,2},{1,5},{3,7},{5,1},{7,3},{8,12},{10,14},{12... | collective-permute-start | bytes 3932168 | tf_op jit(solution)/shard_map/ppermute | solution.py:296
  249.8 83.2 %collective-permute-start.17 = (bf16[256,2560]{1,0:T(8,128)(2,1)}, bf16[256,2560]{1,0:T(8,128)(2,1)}, u32[]{:S(2)}, u32[]{:S(2)}) collective-permute-start(bf16[256,2560]{1,0:T(8,128)(2,1)} %bitcast.26), channel_id=1, source_target_pairs={{0,2},{2,0},{4,6},{6,4},{1,3},{3,1},{5,7},{7,5},{8,10},{10,8},{12,... | collective-permute-start | bytes 3932168 | tf_op jit(solution)/shard_map/ppermute | solution.py:296
  250.4 85.3 %collective-permute-start.18 = (bf16[256,2560]{1,0:T(8,128)(2,1)}, bf16[256,2560]{1,0:T(8,128)(2,1)}, u32[]{:S(2)}, u32[]{:S(2)}) collective-permute-start(bf16[256,2560]{1,0:T(8,128)(2,1)} %bitcast.26), channel_id=1, source_target_pairs={{0,4},{2,6},{4,0},{6,2},{1,5},{3,7},{5,1},{7,3},{8,12},{10,14},{12... | collective-permute-start | bytes 3932168 | tf_op jit(solution)/shard_map/ppermute | solution.py:296
  270.2 83.6 %collective-permute-start.15 = (bf16[4,320,1024]{2,1,0:T(8,128)(2,1)}, bf16[4,320,1024]{2,1,0:T(8,128)(2,1)}, u32[]{:S(2)}, u32[]{:S(2)}) collective-permute-start(bf16[4,320,1024]{2,1,0:T(8,128)(2,1)} %get-tuple-element.123), channel_id=1, source_target_pairs={{0,1},{1,0},{2,3},{3,2},{4,5},{5,4},{6,7},{7,6},{8,9},{9,8},{10,11... | collective-permute-start | bytes 7864328 | tf_op jit(solution)/shard_map/ppermute | solution.py:405
  280.0 38.5 %collective-permute-start.13 = (bf16[128,2560]{1,0:T(8,128)(2,1)S(1)}, bf16[128,2560]{1,0:T(8,128)(2,1)S(1)}, u32[]{:S(2)}, u32[]{:S(2)}) collective-permute-start(bf16[128,2560]{1,0:T(8,128)(2,1)S(1)} %slice.482), channel_id=1, source_target_pairs={{0,4},{2,6},{4,0},{6,2},{1,5},{3,7},{5,1},{7,3},{8,12},{10,14},{12... | collective-permute-start | bytes 1966088 | tf_op jit(solution)/shard_map/ppermute | solution.py:296
  282.7 36.7 %collective-permute-start.14 = (bf16[128,2560]{1,0:T(8,128)(2,1)S(1)}, bf16[128,2560]{1,0:T(8,128)(2,1)S(1)}, u32[]{:S(2)}, u32[]{:S(2)}) collective-permute-start(bf16[128,2560]{1,0:T(8,128)(2,1)S(1)} %slice.483), channel_id=1, source_target_pairs={{0,2},{2,0},{4,6},{6,4},{1,3},{3,1},{5,7},{7,5},{8,10},{10,8},{12,... | collective-permute-start | bytes 1966088 | tf_op jit(solution)/shard_map/ppermute | solution.py:296
  331.5 29.0 %collective-permute-start.16 = (bf16[4,320,1024]{2,1,0:T(8,128)(2,1)S(1)}, bf16[4,320,1024]{2,1,0:T(8,128)(2,1)S(1)}, u32[]{:S(2)}, u32[]{:S(2)}) collective-permute-start(bf16[4,320,1024]{2,1,0:T(8,128)(2,1)S(1)} %get-tuple-element.121), channel_id=1, source_target_pairs={{0,1},{1,0},{2,3},{3,2},{4,5},{5,4},{6,7},{7,6},{8,9},{9,8},{10,11... | collective-permute-start | bytes 7864328 | tf_op jit(solution)/shard_map/ppermute | solution.py:405
  419.2 322.6 %reduce-scatter.6.cloned.1.call-start = ((), (), s32[]{:S(2)}) async-start(), calls=%async_computation.8 | async-start | bytes 11468800 | tf_op jit(solution)/shard_map/reduce_scatter | solution.py:423
  448.3 35.0 %collective-permute-start.25 = (bf16[1024,3584]{1,0:T(8,128)(2,1)}, bf16[1024,3584]{1,0:T(8,128)(2,1)}, u32[]{:S(2)}, u32[]{:S(2)}) collective-permute-start(bf16[1024,3584]{1,0:T(8,128)(2,1)} %pad_maximum_fusion), channel_id=1, source_target_pairs={{0,1},{1,0},{2,3},{3,2},{4,5},{5,4},{6,7},{7,6},{8,9},{9,8},{10,11... | collective-permute-start | bytes 22020104 | tf_op jit(solution)/shard_map/ppermute | solution.py:405
  457.9 19.8 %collective-permute-start.23 = (bf16[128,2560]{1,0:T(8,128)(2,1)S(1)}, bf16[128,2560]{1,0:T(8,128)(2,1)}, u32[]{:S(2)}, u32[]{:S(2)}) collective-permute-start(bf16[128,2560]{1,0:T(8,128)(2,1)S(1)} %get-tuple-element.158), channel_id=1, source_target_pairs={{0,2},{2,0},{4,6},{6,4},{1,3},{3,1},{5,7},{7,5},{8,10},{10,8},{12,... | collective-permute-start | bytes 1966088 | tf_op jit(solution)/shard_map/ppermute | solution.py:296
  459.4 18.3 %collective-permute-start.21 = (bf16[128,2560]{1,0:T(8,128)(2,1)S(1)}, bf16[128,2560]{1,0:T(8,128)(2,1)}, u32[]{:S(2)}, u32[]{:S(2)}) collective-permute-start(bf16[128,2560]{1,0:T(8,128)(2,1)S(1)} %get-tuple-element.159), channel_id=1, source_target_pairs={{0,4},{2,6},{4,0},{6,2},{1,5},{3,7},{5,1},{7,3},{8,12},{10,14},{12... | collective-permute-start | bytes 1966088 | tf_op jit(solution)/shard_map/ppermute | solution.py:296
  481.1 30.7 %collective-permute-start.22 = (bf16[256,2560]{1,0:T(8,128)(2,1)}, bf16[256,2560]{1,0:T(8,128)(2,1)}, u32[]{:S(2)}, u32[]{:S(2)}) collective-permute-start(bf16[256,2560]{1,0:T(8,128)(2,1)} %pad_maximum_fusion.8), channel_id=1, source_target_pairs={{0,2},{2,0},{4,6},{6,4},{1,3},{3,1},{5,7},{7,5},{8,10},{10,8},{12,... | collective-permute-start | bytes 3932168 | tf_op jit(solution)/shard_map/ppermute | solution.py:296
  482.7 30.5 %collective-permute-start.24 = (bf16[256,2560]{1,0:T(8,128)(2,1)}, bf16[256,2560]{1,0:T(8,128)(2,1)}, u32[]{:S(2)}, u32[]{:S(2)}) collective-permute-start(bf16[256,2560]{1,0:T(8,128)(2,1)} %pad_maximum_fusion.9), channel_id=1, source_target_pairs={{0,4},{2,6},{4,0},{6,2},{1,5},{3,7},{5,1},{7,3},{8,12},{10,14},{12... | collective-permute-start | bytes 3932168 | tf_op jit(solution)/shard_map/ppermute | solution.py:296
  510.0 326.3 %reduce-scatter.8.cloned.1.call-start = ((), (), s32[]{:S(2)}) async-start(), calls=%async_computation.9 | async-start | bytes 5324800 | tf_op jit(solution)/shard_map/reduce_scatter | solution.py:423
  533.6 46.7 %collective-permute-start.30 = (bf16[256,2560]{1,0:T(8,128)(2,1)}, bf16[256,2560]{1,0:T(8,128)(2,1)}, u32[]{:S(2)}, u32[]{:S(2)}) collective-permute-start(bf16[256,2560]{1,0:T(8,128)(2,1)} %get-tuple-element.103), channel_id=1, source_target_pairs={{0,4},{2,6},{4,0},{6,2},{1,5},{3,7},{5,1},{7,3},{8,12},{10,14},{12... | collective-permute-start | bytes 3932168 | tf_op jit(solution)/shard_map/ppermute | solution.py:296
  534.8 48.7 %collective-permute-start.28 = (bf16[256,2560]{1,0:T(8,128)(2,1)}, bf16[256,2560]{1,0:T(8,128)(2,1)}, u32[]{:S(2)}, u32[]{:S(2)}) collective-permute-start(bf16[256,2560]{1,0:T(8,128)(2,1)} %get-tuple-element.103), channel_id=1, source_target_pairs={{0,2},{2,0},{4,6},{6,4},{1,3},{3,1},{5,7},{7,5},{8,10},{10,8},{12,... | collective-permute-start | bytes 3932168 | tf_op jit(solution)/shard_map/ppermute | solution.py:296
  582.2 33.2 %collective-permute-start.31 = (bf16[128,2560]{1,0:T(8,128)(2,1)}, bf16[128,2560]{1,0:T(8,128)(2,1)S(1)}, u32[]{:S(2)}, u32[]{:S(2)}) collective-permute-start(bf16[128,2560]{1,0:T(8,128)(2,1)} %slice.507), channel_id=1, source_target_pairs={{0,2},{2,0},{4,6},{6,4},{1,3},{3,1},{5,7},{7,5},{8,10},{10,8},{12,... | collective-permute-start | bytes 1966088 | tf_op jit(solution)/shard_map/ppermute | solution.py:296
  585.5 29.9 %collective-permute-start.29 = (bf16[128,2560]{1,0:T(8,128)(2,1)}, bf16[128,2560]{1,0:T(8,128)(2,1)}, u32[]{:S(2)}, u32[]{:S(2)}) collective-permute-start(bf16[128,2560]{1,0:T(8,128)(2,1)} %slice.506), channel_id=1, source_target_pairs={{0,4},{2,6},{4,0},{6,2},{1,5},{3,7},{5,1},{7,3},{8,12},{10,14},{12... | collective-permute-start | bytes 1966088 | tf_op jit(solution)/shard_map/ppermute | solution.py:296
  616.6 51.4 %collective-permute-start.32 = (bf16[256,2560]{1,0:T(8,128)(2,1)}, bf16[256,2560]{1,0:T(8,128)(2,1)}, u32[]{:S(2)}, u32[]{:S(2)}) collective-permute-start(bf16[256,2560]{1,0:T(8,128)(2,1)} %pad_maximum_fusion.10), channel_id=1, source_target_pairs={{0,2},{2,0},{4,6},{6,4},{1,3},{3,1},{5,7},{7,5},{8,10},{10,8},{12,... | collective-permute-start | bytes 3932168 | tf_op jit(solution)/shard_map/ppermute | solution.py:296
  634.5 27.0 %collective-permute-start.40 = (bf16[80,1792]{1,0:T(8,128)(2,1)S(1)}, bf16[80,1792]{1,0:T(8,128)(2,1)S(1)}, u32[]{:S(2)}, u32[]{:S(2)}) collective-permute-start(bf16[80,1792]{1,0:T(8,128)(2,1)S(1)} %get-tuple-element.167), channel_id=1, source_target_pairs={{0,3},{1,7},{2,2},{3,6},{4,1},{5,5},{6,0},{7,4},{8,11},{9,15},{10,... | collective-permute-start | bytes 860168 | tf_op jit(solution)/shard_map/ppermute | solution.py:448
  636.5 27.8 %collective-permute-start.39 = (bf16[80,1792]{1,0:T(8,128)(2,1)S(1)}, bf16[80,1792]{1,0:T(8,128)(2,1)S(1)}, u32[]{:S(2)}, u32[]{:S(2)}) collective-permute-start(bf16[80,1792]{1,0:T(8,128)(2,1)S(1)} %get-tuple-element.168), channel_id=1, source_target_pairs={{0,2},{1,6},{2,3},{3,7},{4,0},{5,4},{6,1},{7,5},{8,10},{9,14},{10,... | collective-permute-start | bytes 860168 | tf_op jit(solution)/shard_map/ppermute | solution.py:448
  636.9 28.8 %collective-permute-start.38 = (bf16[80,1792]{1,0:T(8,128)(2,1)S(1)}, bf16[80,1792]{1,0:T(8,128)(2,1)S(1)}, u32[]{:S(2)}, u32[]{:S(2)}) collective-permute-start(bf16[80,1792]{1,0:T(8,128)(2,1)S(1)} %get-tuple-element.169), channel_id=1, source_target_pairs={{0,1},{1,5},{2,0},{3,4},{4,3},{5,7},{6,2},{7,6},{8,9},{9,13},{10,8... | collective-permute-start | bytes 860168 | tf_op jit(solution)/shard_map/ppermute | solution.py:448
  639.5 26.3 %collective-permute-start.37 = (bf16[80,1792]{1,0:T(8,128)(2,1)S(1)}, bf16[80,1792]{1,0:T(8,128)(2,1)S(1)}, u32[]{:S(2)}, u32[]{:S(2)}) collective-permute-start(bf16[80,1792]{1,0:T(8,128)(2,1)S(1)} %get-tuple-element.166), channel_id=1, source_target_pairs={{0,0},{1,4},{2,1},{3,5},{4,2},{5,6},{6,3},{7,7},{8,8},{9,12},{10,9... | collective-permute-start | bytes 860168 | tf_op jit(solution)/shard_map/ppermute | solution.py:448
  662.1 31.4 %collective-permute-start.33 = (bf16[256,2560]{1,0:T(8,128)(2,1)S(1)}, bf16[256,2560]{1,0:T(8,128)(2,1)S(1)}, u32[]{:S(2)}, u32[]{:S(2)}) collective-permute-start(bf16[256,2560]{1,0:T(8,128)(2,1)S(1)} %copy-done.24), channel_id=1, source_target_pairs={{0,4},{2,6},{4,0},{6,2},{1,5},{3,7},{5,1},{7,3},{8,12},{10,14},{12... | collective-permute-start | bytes 3932168 | tf_op jit(solution)/shard_map/ppermute | solution.py:296
  664.2 65.9 %collective-permute-start.42 = (bf16[320,1024]{1,0:T(8,128)(2,1)}, bf16[320,1024]{1,0:T(8,128)(2,1)}, u32[]{:S(2)}, u32[]{:S(2)}) collective-permute-start(bf16[320,1024]{1,0:T(8,128)(2,1)} %get-tuple-element.135), channel_id=1, source_target_pairs={{0,24},{8,16},{16,8},{24,0},{1,25},{9,17},{17,9},{25,1},{2,26},{10... | collective-permute-start | bytes 1966088 | tf_op jit(solution)/shard_map/ppermute | solution.py:466
  665.7 34.4 %collective-permute-start.36 = (bf16[4,320,640]{2,1,0:T(8,128)(2,1)}, bf16[4,320,640]{2,1,0:T(8,128)(2,1)}, u32[]{:S(2)}, u32[]{:S(2)}) collective-permute-start(bf16[4,320,640]{2,1,0:T(8,128)(2,1)} %dynamic-slice_bitcast_fusion.2), channel_id=1, source_target_pairs={{0,1},{1,0},{2,3},{3,2},{4,5},{5,4},{6,7},{7,6},{8,9},{9,8},{10,11... | collective-permute-start | bytes 4915208 | tf_op jit(solution)/shard_map/ppermute | solution.py:405
  665.8 36.7 %collective-permute-start.35 = (bf16[4,320,640]{2,1,0:T(8,128)(2,1)}, bf16[4,320,640]{2,1,0:T(8,128)(2,1)}, u32[]{:S(2)}, u32[]{:S(2)}) collective-permute-start(bf16[4,320,640]{2,1,0:T(8,128)(2,1)} %dynamic-slice_bitcast_fusion.3), channel_id=1, source_target_pairs={{0,1},{1,0},{2,3},{3,2},{4,5},{5,4},{6,7},{7,6},{8,9},{9,8},{10,11... | collective-permute-start | bytes 4915208 | tf_op jit(solution)/shard_map/ppermute | solution.py:405
  668.1 62.0 %collective-permute-start.34 = (bf16[320,1024]{1,0:T(8,128)(2,1)}, bf16[320,1024]{1,0:T(8,128)(2,1)}, u32[]{:S(2)}, u32[]{:S(2)}) collective-permute-start(bf16[320,1024]{1,0:T(8,128)(2,1)} %get-tuple-element.136), channel_id=1, source_target_pairs={{0,16},{8,24},{16,0},{24,8},{1,17},{9,25},{17,1},{25,9},{2,18},{10... | collective-permute-start | bytes 1966088 | tf_op jit(solution)/shard_map/ppermute | solution.py:466
  693.5 36.6 %collective-permute-start.41 = (bf16[320,1024]{1,0:T(8,128)(2,1)}, bf16[320,1024]{1,0:T(8,128)(2,1)}, u32[]{:S(2)}, u32[]{:S(2)}) collective-permute-start(bf16[320,1024]{1,0:T(8,128)(2,1)} %get-tuple-element.134), channel_id=1, source_target_pairs={{0,8},{8,0},{16,24},{24,16},{1,9},{9,1},{17,25},{25,17},{2,10},{10... | collective-permute-start | bytes 1966088 | tf_op jit(solution)/shard_map/ppermute | solution.py:466
  767.6 30.0 %collective-permute-start.45 = (bf16[256,2560]{1,0:T(8,128)(2,1)}, bf16[256,2560]{1,0:T(8,128)(2,1)}, u32[]{:S(2)}, u32[]{:S(2)}) collective-permute-start(bf16[256,2560]{1,0:T(8,128)(2,1)} %pad_maximum_fusion.13), channel_id=1, source_target_pairs={{0,2},{2,0},{4,6},{6,4},{1,3},{3,1},{5,7},{7,5},{8,10},{10,8},{12,... | collective-permute-start | bytes 3932168 | tf_op jit(solution)/shard_map/ppermute | solution.py:296
  769.3 29.9 %collective-permute-start.47 = (bf16[256,2560]{1,0:T(8,128)(2,1)}, bf16[256,2560]{1,0:T(8,128)(2,1)}, u32[]{:S(2)}, u32[]{:S(2)}) collective-permute-start(bf16[256,2560]{1,0:T(8,128)(2,1)} %pad_maximum_fusion.14), channel_id=1, source_target_pairs={{0,4},{2,6},{4,0},{6,2},{1,5},{3,7},{5,1},{7,3},{8,12},{10,14},{12... | collective-permute-start | bytes 3932168 | tf_op jit(solution)/shard_map/ppermute | solution.py:296
  802.3 18.7 %collective-permute-start.55 = (bf16[80,3584]{1,0:T(8,128)(2,1)S(1)}, bf16[80,3584]{1,0:T(8,128)(2,1)S(1)}, u32[]{:S(2)}, u32[]{:S(2)}) collective-permute-start(bf16[80,3584]{1,0:T(8,128)(2,1)S(1)} %get-tuple-element.150), channel_id=1, source_target_pairs={{0,3},{1,7},{2,2},{3,6},{4,1},{5,5},{6,0},{7,4},{8,11},{9,15},{10,... | collective-permute-start | bytes 1720328 | tf_op jit(solution)/shard_map/ppermute | solution.py:448
  804.3 26.2 %collective-permute-start.54 = (bf16[80,3584]{1,0:T(8,128)(2,1)S(1)}, bf16[80,3584]{1,0:T(8,128)(2,1)S(1)}, u32[]{:S(2)}, u32[]{:S(2)}) collective-permute-start(bf16[80,3584]{1,0:T(8,128)(2,1)S(1)} %get-tuple-element.151), channel_id=1, source_target_pairs={{0,2},{1,6},{2,3},{3,7},{4,0},{5,4},{6,1},{7,5},{8,10},{9,14},{10,... | collective-permute-start | bytes 1720328 | tf_op jit(solution)/shard_map/ppermute | solution.py:448
  804.4 26.2 %collective-permute-start.53 = (bf16[80,3584]{1,0:T(8,128)(2,1)S(1)}, bf16[80,3584]{1,0:T(8,128)(2,1)S(1)}, u32[]{:S(2)}, u32[]{:S(2)}) collective-permute-start(bf16[80,3584]{1,0:T(8,128)(2,1)S(1)} %get-tuple-element.152), channel_id=1, source_target_pairs={{0,1},{1,5},{2,0},{3,4},{4,3},{5,7},{6,2},{7,6},{8,9},{9,13},{10,8... | collective-permute-start | bytes 1720328 | tf_op jit(solution)/shard_map/ppermute | solution.py:448
  807.4 23.2 %collective-permute-start.52 = (bf16[80,3584]{1,0:T(8,128)(2,1)S(1)}, bf16[80,3584]{1,0:T(8,128)(2,1)S(1)}, u32[]{:S(2)}, u32[]{:S(2)}) collective-permute-start(bf16[80,3584]{1,0:T(8,128)(2,1)S(1)} %get-tuple-element.149), channel_id=1, source_target_pairs={{0,0},{1,4},{2,1},{3,5},{4,2},{5,6},{6,3},{7,7},{8,8},{9,12},{10,9... | collective-permute-start | bytes 1720328 | tf_op jit(solution)/shard_map/ppermute | solution.py:448
  (62 other events, 1292.5 us)
Sparse Core Ops, SparseCore 0:
  14.0 85.8 all-gather.4
  112.5 53.2 all-gather.6
  168.0 162.7 all-gather.8
  332.3 86.7 all-gather.10
  421.3 95.4 reduce-scatter.3
  519.1 159.1 reduce-scatter.5
  749.9 75.0 reduce-scatter.7

commit v6 on v5

--- a/solution.py
+++ b/solution.py
@@ -522,8 +522,12 @@
         )
     grad_query_low, grad_kv = grads
     grad_middle_low = jnp.concatenate(grad_blocks, axis=0)
+    grad_kv_own = lax.dynamic_index_in_dim(grad_kv, group_at, axis=0, keepdims=False)
+    grad_kv_others = from_group(grad_kv)
+    grad_kv_others[0], grad_query_low, grad_middle_low, sum_down, sink_out = then(
+        (grad_kv_others[0], grad_query_low, grad_middle_low, sum_down, sink_out)
+    )
     output_full = middle + given(hidden, w_sink, *sink_out)
-    grad_kv, sum_down = then((grad_kv, sum_down))
     squares = jnp.stack(
         [jnp.sum(source * source), jnp.sum(middle * middle), jnp.sum(output_full * output_full)]
     )
@@ -533,8 +537,6 @@
     assert spare >= extra.size
     extra = jnp.pad(extra.reshape(1, -1), ((0, 0), (0, spare - extra.size)))
     extra = jnp.broadcast_to(extra, (model_width // 2, spare)).astype(jnp.bfloat16)
-    grad_kv_own = lax.dynamic_index_in_dim(grad_kv, group_at, axis=0, keepdims=False)
-    grad_kv_others = from_group(grad_kv)
     attn_totals = with_layout_constraint(
         jnp.concatenate(
             [

time: 879 us -> 919 us (1.046)
  waiting for transfers between devices: 298 us -> 342 us
    ppermute x3, waiting for transfers between devices: 23 us -> 58.2 us  [from_group(): lax.ppermute(lax.dynamic_index_in_dim(values, group_at ^ step, axis=0, ke...]
    ppermute x35, waiting for transfers between devices: 167 us -> 178 us  [swap(): return lax.ppermute(value, 'chip', pairs)]
    unnamed x100 -> x112, local copies, waits for them, and re-layouts: 20.3 us -> 17.4 us
  transfers between devices with their start and end apart: 63 -> 63, of which waited for: 29 -> 32; matrix products, arithmetic and copies ran while one was open for 42% -> 40% of each run, Pallas kernels for 8% -> 7%
where the time goes in v6:
time: 919 us; the launch traced here: 908 us
  waiting for transfers between devices  342 us (37%)
  matrix products  210 us (23%)
  other arithmetic  104 us (11%)
  local copies, waits for them, and re-layouts  84.3 us (9%)
  starting transfers between devices  67 us (7%)
  Pallas kernels  66 us (7%)
  between operations  21 us (2%)
  blocking collectives  13.4 us (1%)
    ppermute x35, waiting for transfers between devices, swap(): return lax.ppermute(value, 'chip', pairs)  178 us
    dot_general x6, matrix products, times(): return jnp.dot(left, right, preferred_element_type=jnp.float32)  90.8 us
    dot_general x13, matrix products, times_t(): lax.dot_general(left, right, (((1,), (1,)), ((), ())), preferred_element_...  88.3 us
    ppermute x3, waiting for transfers between devices, from_group(): lax.ppermute(lax.dynamic_index_in_dim(values, group_at ^ step, axis=0, ke...  58.2 us
    pallas_call x3, Pallas kernels, attend_back(): pl.pallas_call(kernel, out_shape=(jax.ShapeDtypeStruct((tokens, query_wid...  45.1 us
    all_gather x3, waiting for transfers between devices, gathered(): return lax.all_gather(part, ('group', 'core'), axis=0, tiled=True)  40.7 us
    ppermute x35, starting transfers between devices, swap(): return lax.ppermute(value, 'chip', pairs)  40.5 us
    all_gather x1, waiting for transfers between devices, shards(): kv_all = lax.all_gather(kv_own_tokens, 'group', axis=0, tiled=True)  33.3 us
  transfers between devices with their start and end apart: 63, of which 32 were waited for; matrix products, arithmetic and copies ran while one was open for 40% of the time, Pallas kernels for 7%

profile of v6, /device:TPU:0, one launch (start us, length us, event | category | flops | bytes accessed | tf_op | source)
XLA Modules:
  0.0 907.9 jit_solution(7319016147476961172)
XLA Ops:
  22.0 13.4 %all_gather.16 = bf16[2,2560]{1,0:T(2,128)(2,1)S(1)} all-gather(bf16[2,640]{1,0:T(2,128)(2,1)S(1)} %pad_maximum_fusion.24), channel_id=1, replica_groups=mesh['group'=4,'dp'=1,'chip'=4,'core'=2] {'group'}, dimensions={1}, use_global_device_ids=true | all-gather | bytes 12800 | tf_op jit(solution)/shard_map/all_gather | solution.py:375
  35.6 11.5 %collective-permute-done.6 = s32[258]{0:T(512)S(1)} collective-permute-done((s32[258]{0:T(512)S(1)}, s32[258]{0:T(512)S(1)}, u32[]{:S(2)}, u32[]{:S(2)}) %collective-permute-start.6) | collective-permute-done | bytes 1064 | tf_op jit(solution)/shard_map/ppermute | solution.py:296
  50.4 13.1 %collective-permute-done.2 = bf16[128,2560]{1,0:T(8,128)(2,1)S(1)} collective-permute-done((bf16[128,2560]{1,0:T(8,128)(2,1)S(1)}, bf16[128,2560]{1,0:T(8,128)(2,1)S(1)}, u32[]{:S(2)}, u32[]{:S(2)}) %collective-permute-start.2) | collective-permute-done | bytes 655392 | tf_op jit(solution)/shard_map/ppermute | solution.py:296
  67.1 32.8 %all-gather.5.cloned.1.call-done = bf16[2560,1600]{1,0:T(8,128)(2,1)} async-done(((bf16[320,1600]{1,0:T(8,128)(2,1)}), bf16[2560,1600]{1,0:T(8,128)(2,1)}) %all-gather.5.cloned.1.call-update) | async-done | bytes 8192016 | tf_op jit(solution)/shard_map/all_gather | solution.py:373
  99.9 9.5 %fusion.14 = f32[960,1024]{1,0:T(8,128)S(1)} fusion(bf16[2560,1600]{1,0:T(8,128)(2,1)} %all-gather.5.cloned.1.call-done, bf16[1024,2560]{1,0:T(8,128)(2,1)} %copy-done.2, f32[2560]{0:T(1024)S(1)} %get-tuple-element.99, f32[1024]{0:T(1024)S(1)} %add_rsqrt_fusion), kind=kOutput, calls=%fused_computation.47 | convolution fusion | flops 5043650560 | bytes 14432256 | tf_op jit(solution)/shard_map/dot_general | solution.py:393
  132.5 33.3 %all-gather.7.cloned.1.call-done = bf16[1280,1024]{1,0:T(8,128)(2,1)} async-done(((bf16[320,1024]{1,0:T(8,128)(2,1)}), bf16[1280,1024]{1,0:T(8,128)(2,1)}) %all-gather.7.cloned.1.call-update) | async-done | bytes 2621456 | tf_op jit(solution)/shard_map/all_gather | solution.py:401
  165.8 20.8 %attend.1 = (bf16[1024,640]{1,0:T(8,128)(2,1)}, f32[4,8,256]{2,1,0:T(8,128)}) custom-call(bf16[640,1024]{1,0:T(8,128)(2,1)} %bitcast.185, bf16[4,320,1024]{2,1,0:T(8,128)(2,1)} %bitcast.196, s32[4,1,256]{2,1,0:T(1,128)} %broadcast_in_dim.39.refs_2_), custom_call_target="tpu_custom_call" | custom-call | flops 2684354560 | bytes 5242880 | tf_op jit(solution)/shard_map/attend/pallas_call | solution.py:99
  198.1 8.8 collective-permute-done.9
  218.7 20.6 %collective-permute-done.8 = bf16[256,2560]{1,0:T(8,128)(2,1)} collective-permute-done((bf16[256,2560]{1,0:T(8,128)(2,1)}, bf16[256,2560]{1,0:T(8,128)(2,1)}, u32[]{:S(2)}, u32[]{:S(2)}) %collective-permute-start.8) | collective-permute-done | bytes 1310752 | tf_op jit(solution)/shard_map/ppermute | solution.py:296
  250.9 6.1 fusion.90
  257.0 8.3 copy.39
  265.4 4.9 constant_dynamic-slice_fusion.7
  270.2 8.7 collective-permute-done.11
  289.2 29.4 %collective-permute-done.13 = bf16[128,2560]{1,0:T(8,128)(2,1)S(1)} collective-permute-done((bf16[128,2560]{1,0:T(8,128)(2,1)S(1)}, bf16[128,2560]{1,0:T(8,128)(2,1)S(1)}, u32[]{:S(2)}, u32[]{:S(2)}) %collective-permute-start.13) | collective-permute-done | bytes 655392 | tf_op jit(solution)/shard_map/ppermute | solution.py:296
  320.4 7.9 copy.40
  340.5 10.9 %collective-permute-done.19 = bf16[128,2560]{1,0:T(8,128)(2,1)S(1)} collective-permute-done((bf16[128,2560]{1,0:T(8,128)(2,1)S(1)}, bf16[128,2560]{1,0:T(8,128)(2,1)S(1)}, u32[]{:S(2)}, u32[]{:S(2)}) %collective-permute-start.19) | collective-permute-done | bytes 655392 | tf_op jit(solution)/shard_map/ppermute | solution.py:296
  353.8 6.7 pad_maximum_fusion.1
  363.3 27.5 %fusion.117 = f32[1024,3584]{1,0:T(8,128)} fusion(bf16[1024,2560]{1,0:T(8,128)(2,1)} %constant_dynamic-update-slice_fusion.5, bf16[2560,3584]{1,0:T(8,128)(2,1)} %all-gather.9.cloned.1.call-done), kind=kOutput, calls=%fused_computation.303 | convolution fusion | flops 18790481920 | bytes 38273024 | tf_op jit(solution)/shard_map/dot_general | solution.py:261
  390.8 6.6 multiply_convert_fusion.2
  399.2 12.0 %convolution_convert_fusion.1 = bf16[2560,1792]{1,0:T(8,128)(2,1)} fusion(bf16[1024,2560]{1,0:T(8,128)(2,1)S(1)} %copy-done.32, bf16[1024,1792]{1,0:T(8,128)(2,1)S(1)} %multiply_convert_fusion.2), kind=kOutput, calls=%fused_computation.8 | convolution fusion | flops 9399828480 | bytes 18087936 | tf_op jit(solution)/shard_map/dot_general | solution.py:271
  411.2 7.9 all-gather.11.cloned.1.call-done
  420.5 20.9 %multiply_convert_fusion = (bf16[1024,1792]{1,0:T(8,128)(2,1)S(1)}, bf16[1024,1792]{1,0:T(8,128)(2,1)}) fusion(f32[1024,3584]{1,0:T(8,128)} %fusion.117, bf16[1024,2560]{1,0:T(8,128)(2,1)} %copy-done.31, bf16[2560,1792]{1,0:T(8,128)(2,1)} %all-gather.11.cloned.1.call-done), kind=kOutput, calls=%fused_computation.19 | convolution fusion | flops 9417261056 | bytes 36438016 | tf_op jit(solution)/shard_map/dot_general | solution.py:261
  441.4 7.0 pad_maximum_fusion
  448.6 9.2 %convolution_convert_fusion.10 = bf16[256,2560]{1,0:T(8,128)(2,1)S(1)} fusion(bf16[2560,3584]{1,0:T(8,128)(2,1)} %all-gather.9.cloned.1.call-done, bf16[1024,1792]{1,0:T(8,128)(2,1)} %get-tuple-element.118, bf16[1024,1792]{1,0:T(8,128)(2,1)S(1)} %get-tuple-element.117), kind=kOutput, calls=%fused_computation.40 | convolution fusion | flops 4701945856 | bytes 27000832 | tf_op jit(solution)/shard_map/dot_general | solution.py:265
  461.0 15.3 %convolution_convert_fusion.4 = bf16[512,2560]{1,0:T(8,128)(2,1)} fusion(bf16[2560,3584]{1,0:T(8,128)(2,1)} %all-gather.9.cloned.1.call-done, bf16[1024,1792]{1,0:T(8,128)(2,1)} %get-tuple-element.118, bf16[1024,1792]{1,0:T(8,128)(2,1)S(1)} %get-tuple-element.117), kind=kOutput, calls=%fused_computation.33 | convolution fusion | flops 9403891712 | bytes 28311552 | tf_op jit(solution)/shard_map/dot_general | solution.py:265
  483.4 26.7 %convolution_convert_fusion = bf16[1280,3584]{1,0:T(8,128)(2,1)} fusion(bf16[1280,2048]{1,0:T(8,128)(2,1)} %pad_maximum_fusion.2, bf16[1024,3584]{1,0:T(8,128)(2,1)} %collective-permute-done.25, bf16[1024,1792]{1,0:T(8,128)(2,1)} %copy-done.13, bf16[1024,1792]{1,0:T(8,128)(2,1)} %get-tuple-element.118), kind=kOutput, calls=%fused_computation | convolution fusion | flops 18839109632 | bytes 29097984 | tf_op jit(solution)/shard_map/dot_general | solution.py:261
  516.8 11.5 %multiply_reduce_fusion.1 = (f32[256]{0:T(256)S(1)}, f32[256,2560]{1,0:T(8,128)S(1)}) fusion(f32[256,2560]{1,0:T(8,128)S(1)} %copy-done.1, f32[2560]{0:T(1024)S(1)} %copy-done.36, bf16[256,2560]{1,0:T(8,128)(2,1)} %collective-permute-done.24, bf16[256,2560]{1,0:T(8,128)(2,1)} %collective-permute-done.22, ...), kind=kOutput, calls=%fused_computation.69 | convolution fusion | flops 4705878016 | bytes 33565696 | tf_op jit(solution)/shard_map/dot_general | solution.py:265
  528.4 5.3 fusion.92
  536.4 4.8 fusion.54.refs_5_
  541.1 11.8 %attend_back.3 = (bf16[1024,640]{1,0:T(8,128)(2,1)}, bf16[4,320,1024]{2,1,0:T(8,128)(2,1)}) custom-call(bf16[640,1024]{1,0:T(8,128)(2,1)} %bitcast.186, bf16[4,320,1024]{2,1,0:T(8,128)(2,1)} %bitcast.197, s32[4,1,256]{2,1,0:T(1,128)} %broadcast_in_dim.39.refs_2_, f32[4,8,256]{2,1,0:T(8,128)} %get-tuple-element.57.refs_3_, ...), custom_call_target="tpu_custom_call" | custom-call | flops 1677721600 | bytes 2621440 | tf_op jit(solution)/shard_map/attend_back/pallas_call | solution.py:224
  552.9 6.9 convolution_convert_fusion.9
  561.2 8.8 convolution_convert_fusion.6
  570.1 6.6 collective-permute-done.27
  585.3 6.1 fusion.35.refs_5_
  591.4 21.5 %attend_back.4 = (bf16[1024,640]{1,0:T(8,128)(2,1)}, bf16[4,320,1024]{2,1,0:T(8,128)(2,1)}) custom-call(bf16[640,1024]{1,0:T(8,128)(2,1)} %bitcast.187, bf16[4,320,1024]{2,1,0:T(8,128)(2,1)} %bitcast.198, s32[4,1,256]{2,1,0:T(1,128)} %broadcast_in_dim.39.refs_2_, ...), custom_call_target="tpu_custom_call", output_to_operand_aliasing={{0}: (8, {}), {1}: (9, {})} | custom-call | flops 3355443200 | bytes 5242880 | tf_op jit(solution)/shard_map/attend_back/pallas_call | solution.py:224
  614.2 4.9 fusion.57.refs_5_
  619.0 11.8 %attend_back.5 = (bf16[1024,640]{1,0:T(8,128)(2,1)}, bf16[4,320,1024]{2,1,0:T(8,128)(2,1)}) custom-call(bf16[640,1024]{1,0:T(8,128)(2,1)} %bitcast.188, bf16[4,320,1024]{2,1,0:T(8,128)(2,1)} %bitcast.199, s32[4,1,256]{2,1,0:T(1,128)} %broadcast_in_dim.39.refs_2_, ...), custom_call_target="tpu_custom_call", output_to_operand_aliasing={{0}: (8, {}), {1}: (9, {})} | custom-call | flops 1677721600 | bytes 2621440 | tf_op jit(solution)/shard_map/attend_back/pallas_call | solution.py:224
  635.6 6.6 fusion.63
  648.3 39.9 %collective-permute-done.32 = bf16[320,1024]{1,0:T(8,128)(2,1)S(1)} collective-permute-done((bf16[320,1024]{1,0:T(8,128)(2,1)S(1)}, bf16[320,1024]{1,0:T(8,128)(2,1)S(1)}, u32[]{:S(2)}, u32[]{:S(2)}) %collective-permute-start.32) | collective-permute-done | bytes 655392 | tf_op jit(solution)/shard_map/ppermute | solution.py:466
  698.8 5.1 convolution_convert_fusion.3
  713.0 25.8 %collective-permute-done.33 = bf16[256,2560]{1,0:T(8,128)(2,1)S(1)} collective-permute-done((bf16[256,2560]{1,0:T(8,128)(2,1)S(1)}, bf16[256,2560]{1,0:T(8,128)(2,1)S(1)}, u32[]{:S(2)}, u32[]{:S(2)}) %collective-permute-start.33) | collective-permute-done | bytes 1310752 | tf_op jit(solution)/shard_map/ppermute | solution.py:296
  753.2 18.3 %collective-permute-done.35 = bf16[320,1024]{1,0:T(8,128)(2,1)} collective-permute-done((bf16[320,1024]{1,0:T(8,128)(2,1)}, bf16[320,1024]{1,0:T(8,128)(2,1)}, u32[]{:S(2)}, u32[]{:S(2)}) %collective-permute-start.35) | collective-permute-done | bytes 655392 | tf_op jit(solution)/shard_map/ppermute | solution.py:466
  789.3 5.4 convolution_convert_fusion.5
  794.8 10.5 %collective-permute-done.46 = bf16[128,2560]{1,0:T(8,128)(2,1)} collective-permute-done((bf16[128,2560]{1,0:T(8,128)(2,1)}, bf16[128,2560]{1,0:T(8,128)(2,1)}, u32[]{:S(2)}, u32[]{:S(2)}) %collective-permute-start.46) | collective-permute-done | bytes 655392 | tf_op jit(solution)/shard_map/ppermute | solution.py:296
  819.6 18.7 %collective-permute-done.45 = bf16[256,2560]{1,0:T(8,128)(2,1)} collective-permute-done((bf16[256,2560]{1,0:T(8,128)(2,1)}, bf16[256,2560]{1,0:T(8,128)(2,1)}, u32[]{:S(2)}, u32[]{:S(2)}) %collective-permute-start.45) | collective-permute-done | bytes 1310752 | tf_op jit(solution)/shard_map/ppermute | solution.py:296
  851.8 10.3 %collective-permute-done.55 = bf16[80,3584]{1,0:T(8,128)(2,1)S(1)} collective-permute-done((bf16[80,3584]{1,0:T(8,128)(2,1)S(1)}, bf16[80,3584]{1,0:T(8,128)(2,1)S(1)}, u32[]{:S(2)}, u32[]{:S(2)}) %collective-permute-start.55) | collective-permute-done | bytes 573472 | tf_op jit(solution)/shard_map/ppermute | solution.py:448
  862.1 7.6 collective-permute-done.54
  876.7 6.8 collective-permute-start.51
  (383 shorter events, 252.4 us)
Async XLA Ops:
  7.2 92.7 %all-gather.5.cloned.1.call-start = ((), (), s32[]{:S(2)}) async-start(), calls=%async_computation.3 | async-start | bytes 9584640 | tf_op jit(solution)/shard_map/all_gather | solution.py:373
  13.8 152.0 %all-gather.7.cloned.1.call-start = ((), (), s32[]{:S(2)}) async-start(), calls=%async_computation.4 | async-start | bytes 3276800 | tf_op jit(solution)/shard_map/all_gather | solution.py:401
  13.9 34.0 %collective-permute-start = (bf16[256,2560]{1,0:T(8,128)(2,1)S(1)}, bf16[256,2560]{1,0:T(8,128)(2,1)S(1)}, u32[]{:S(2)}, u32[]{:S(2)}) collective-permute-start(bf16[256,2560]{1,0:T(8,128)(2,1)S(1)} %bitcast.178), channel_id=1, source_target_pairs={{0,2},{2,0},{4,6},{6,4},{1,3},{3,1},{5,7},{7,5},{8,10},{10,8},{12,... | collective-permute-start | bytes 3932168 | tf_op jit(solution)/shard_map/ppermute | solution.py:296
  16.9 32.6 %collective-permute-start.1 = (bf16[256,2560]{1,0:T(8,128)(2,1)S(1)}, bf16[256,2560]{1,0:T(8,128)(2,1)S(1)}, u32[]{:S(2)}, u32[]{:S(2)}) collective-permute-start(bf16[256,2560]{1,0:T(8,128)(2,1)S(1)} %bitcast.179), channel_id=1, source_target_pairs={{0,4},{2,6},{4,0},{6,2},{1,5},{3,7},{5,1},{7,3},{8,12},{10,14},{12... | collective-permute-start | bytes 3932168 | tf_op jit(solution)/shard_map/ppermute | solution.py:296
  18.4 28.7 %collective-permute-start.6 = (s32[258]{0:T(512)S(1)}, s32[258]{0:T(512)S(1)}, u32[]{:S(2)}, u32[]{:S(2)}) collective-permute-start(s32[258]{0:T(512)S(1)} %pad_add_fusion.4), channel_id=1, source_target_pairs={{0,6},{2,4},{4,2},{6,0},{1,7},{3,5},{5,3},{7,1},{8,14},{10,12},{12... | collective-permute-start | bytes 3104 | tf_op jit(solution)/shard_map/ppermute | solution.py:296
  18.5 28.7 %collective-permute-start.5 = (s32[258]{0:T(512)S(1)}, s32[258]{0:T(512)S(1)}, u32[]{:S(2)}, u32[]{:S(2)}) collective-permute-start(s32[258]{0:T(512)S(1)} %pad_add_fusion.4), channel_id=1, source_target_pairs={{0,4},{2,6},{4,0},{6,2},{1,5},{3,7},{5,1},{7,3},{8,12},{10,14},{12... | collective-permute-start | bytes 3104 | tf_op jit(solution)/shard_map/ppermute | solution.py:296
  20.5 26.7 %collective-permute-start.4 = (s32[258]{0:T(512)S(1)}, s32[258]{0:T(512)S(1)}, u32[]{:S(2)}, u32[]{:S(2)}) collective-permute-start(s32[258]{0:T(512)S(1)} %pad_add_fusion.4), channel_id=1, source_target_pairs={{0,2},{2,0},{4,6},{6,4},{1,3},{3,1},{5,7},{7,5},{8,10},{10,8},{12,... | collective-permute-start | bytes 3104 | tf_op jit(solution)/shard_map/ppermute | solution.py:296
  112.4 250.9 %all-gather.9.cloned.1.call-start = ((), (), s32[]{:S(2)}) async-start(), calls=%async_computation.5 | async-start | bytes 20643840 | tf_op jit(solution)/shard_map/all_gather | solution.py:373
  115.6 303.5 %all-gather.11.cloned.1.call-start = ((), (), s32[]{:S(2)}) async-start(), calls=%async_computation.6 | async-start | bytes 10321920 | tf_op jit(solution)/shard_map/all_gather | solution.py:373
  209.6 29.7 %collective-permute-start.8 = (bf16[256,2560]{1,0:T(8,128)(2,1)}, bf16[256,2560]{1,0:T(8,128)(2,1)}, u32[]{:S(2)}, u32[]{:S(2)}) collective-permute-start(bf16[256,2560]{1,0:T(8,128)(2,1)} %pad_maximum_fusion.7), channel_id=1, source_target_pairs={{0,2},{2,0},{4,6},{6,4},{1,3},{3,1},{5,7},{7,5},{8,10},{10,8},{12,... | collective-permute-start | bytes 3932168 | tf_op jit(solution)/shard_map/ppermute | solution.py:296
  211.3 29.5 %collective-permute-start.10 = (bf16[256,2560]{1,0:T(8,128)(2,1)}, bf16[256,2560]{1,0:T(8,128)(2,1)}, u32[]{:S(2)}, u32[]{:S(2)}) collective-permute-start(bf16[256,2560]{1,0:T(8,128)(2,1)} %pad_maximum_fusion.8), channel_id=1, source_target_pairs={{0,4},{2,6},{4,0},{6,2},{1,5},{3,7},{5,1},{7,3},{8,12},{10,14},{12... | collective-permute-start | bytes 3932168 | tf_op jit(solution)/shard_map/ppermute | solution.py:296
  215.2 301.7 %reduce-scatter.4.cloned.1.call-start = ((), (), s32[]{:S(2)}) async-start(), calls=%async_computation.7 | async-start | bytes 10321920 | tf_op jit(solution)/shard_map/reduce_scatter | solution.py:423
  246.9 32.0 %collective-permute-start.11 = (bf16[256,2560]{1,0:T(8,128)(2,1)}, bf16[256,2560]{1,0:T(8,128)(2,1)}, u32[]{:S(2)}, u32[]{:S(2)}) collective-permute-start(bf16[256,2560]{1,0:T(8,128)(2,1)} %get-tuple-element.114), channel_id=1, source_target_pairs={{0,2},{2,0},{4,6},{6,4},{1,3},{3,1},{5,7},{7,5},{8,10},{10,8},{12,... | collective-permute-start | bytes 3932168 | tf_op jit(solution)/shard_map/ppermute | solution.py:296
  248.3 33.3 %collective-permute-start.12 = (bf16[256,2560]{1,0:T(8,128)(2,1)}, bf16[256,2560]{1,0:T(8,128)(2,1)}, u32[]{:S(2)}, u32[]{:S(2)}) collective-permute-start(bf16[256,2560]{1,0:T(8,128)(2,1)} %get-tuple-element.114), channel_id=1, source_target_pairs={{0,4},{2,6},{4,0},{6,2},{1,5},{3,7},{5,1},{7,3},{8,12},{10,14},{12... | collective-permute-start | bytes 3932168 | tf_op jit(solution)/shard_map/ppermute | solution.py:296
  249.8 83.2 %collective-permute-start.17 = (bf16[256,2560]{1,0:T(8,128)(2,1)}, bf16[256,2560]{1,0:T(8,128)(2,1)}, u32[]{:S(2)}, u32[]{:S(2)}) collective-permute-start(bf16[256,2560]{1,0:T(8,128)(2,1)} %bitcast.26), channel_id=1, source_target_pairs={{0,2},{2,0},{4,6},{6,4},{1,3},{3,1},{5,7},{7,5},{8,10},{10,8},{12,... | collective-permute-start | bytes 3932168 | tf_op jit(solution)/shard_map/ppermute | solution.py:296
  250.4 85.3 %collective-permute-start.18 = (bf16[256,2560]{1,0:T(8,128)(2,1)}, bf16[256,2560]{1,0:T(8,128)(2,1)}, u32[]{:S(2)}, u32[]{:S(2)}) collective-permute-start(bf16[256,2560]{1,0:T(8,128)(2,1)} %bitcast.26), channel_id=1, source_target_pairs={{0,4},{2,6},{4,0},{6,2},{1,5},{3,7},{5,1},{7,3},{8,12},{10,14},{12... | collective-permute-start | bytes 3932168 | tf_op jit(solution)/shard_map/ppermute | solution.py:296
  270.2 83.5 %collective-permute-start.15 = (bf16[4,320,1024]{2,1,0:T(8,128)(2,1)}, bf16[4,320,1024]{2,1,0:T(8,128)(2,1)}, u32[]{:S(2)}, u32[]{:S(2)}) collective-permute-start(bf16[4,320,1024]{2,1,0:T(8,128)(2,1)} %get-tuple-element.131), channel_id=1, source_target_pairs={{0,1},{1,0},{2,3},{3,2},{4,5},{5,4},{6,7},{7,6},{8,9},{9,8},{10,11... | collective-permute-start | bytes 7864328 | tf_op jit(solution)/shard_map/ppermute | solution.py:405
  280.1 38.5 %collective-permute-start.13 = (bf16[128,2560]{1,0:T(8,128)(2,1)S(1)}, bf16[128,2560]{1,0:T(8,128)(2,1)S(1)}, u32[]{:S(2)}, u32[]{:S(2)}) collective-permute-start(bf16[128,2560]{1,0:T(8,128)(2,1)S(1)} %slice.482), channel_id=1, source_target_pairs={{0,4},{2,6},{4,0},{6,2},{1,5},{3,7},{5,1},{7,3},{8,12},{10,14},{12... | collective-permute-start | bytes 1966088 | tf_op jit(solution)/shard_map/ppermute | solution.py:296
  282.7 36.8 %collective-permute-start.14 = (bf16[128,2560]{1,0:T(8,128)(2,1)S(1)}, bf16[128,2560]{1,0:T(8,128)(2,1)S(1)}, u32[]{:S(2)}, u32[]{:S(2)}) collective-permute-start(bf16[128,2560]{1,0:T(8,128)(2,1)S(1)} %slice.483), channel_id=1, source_target_pairs={{0,2},{2,0},{4,6},{6,4},{1,3},{3,1},{5,7},{7,5},{8,10},{10,8},{12,... | collective-permute-start | bytes 1966088 | tf_op jit(solution)/shard_map/ppermute | solution.py:296
  331.5 29.0 %collective-permute-start.16 = (bf16[4,320,1024]{2,1,0:T(8,128)(2,1)S(1)}, bf16[4,320,1024]{2,1,0:T(8,128)(2,1)S(1)}, u32[]{:S(2)}, u32[]{:S(2)}) collective-permute-start(bf16[4,320,1024]{2,1,0:T(8,128)(2,1)S(1)} %get-tuple-element.129), channel_id=1, source_target_pairs={{0,1},{1,0},{2,3},{3,2},{4,5},{5,4},{6,7},{7,6},{8,9},{9,8},{10,11... | collective-permute-start | bytes 7864328 | tf_op jit(solution)/shard_map/ppermute | solution.py:405
  419.2 363.9 %reduce-scatter.6.cloned.1.call-start = ((), (), s32[]{:S(2)}) async-start(), calls=%async_computation.8 | async-start | bytes 11468800 | tf_op jit(solution)/shard_map/reduce_scatter | solution.py:423
  448.3 35.0 %collective-permute-start.25 = (bf16[1024,3584]{1,0:T(8,128)(2,1)}, bf16[1024,3584]{1,0:T(8,128)(2,1)}, u32[]{:S(2)}, u32[]{:S(2)}) collective-permute-start(bf16[1024,3584]{1,0:T(8,128)(2,1)} %pad_maximum_fusion), channel_id=1, source_target_pairs={{0,1},{1,0},{2,3},{3,2},{4,5},{5,4},{6,7},{7,6},{8,9},{9,8},{10,11... | collective-permute-start | bytes 22020104 | tf_op jit(solution)/shard_map/ppermute | solution.py:405
  457.9 19.9 %collective-permute-start.23 = (bf16[128,2560]{1,0:T(8,128)(2,1)S(1)}, bf16[128,2560]{1,0:T(8,128)(2,1)}, u32[]{:S(2)}, u32[]{:S(2)}) collective-permute-start(bf16[128,2560]{1,0:T(8,128)(2,1)S(1)} %get-tuple-element.166), channel_id=1, source_target_pairs={{0,2},{2,0},{4,6},{6,4},{1,3},{3,1},{5,7},{7,5},{8,10},{10,8},{12,... | collective-permute-start | bytes 1966088 | tf_op jit(solution)/shard_map/ppermute | solution.py:296
  459.5 18.3 %collective-permute-start.21 = (bf16[128,2560]{1,0:T(8,128)(2,1)S(1)}, bf16[128,2560]{1,0:T(8,128)(2,1)}, u32[]{:S(2)}, u32[]{:S(2)}) collective-permute-start(bf16[128,2560]{1,0:T(8,128)(2,1)S(1)} %get-tuple-element.167), channel_id=1, source_target_pairs={{0,4},{2,6},{4,0},{6,2},{1,5},{3,7},{5,1},{7,3},{8,12},{10,14},{12... | collective-permute-start | bytes 1966088 | tf_op jit(solution)/shard_map/ppermute | solution.py:296
  481.2 30.7 %collective-permute-start.22 = (bf16[256,2560]{1,0:T(8,128)(2,1)}, bf16[256,2560]{1,0:T(8,128)(2,1)}, u32[]{:S(2)}, u32[]{:S(2)}) collective-permute-start(bf16[256,2560]{1,0:T(8,128)(2,1)} %pad_maximum_fusion.9), channel_id=1, source_target_pairs={{0,2},{2,0},{4,6},{6,4},{1,3},{3,1},{5,7},{7,5},{8,10},{10,8},{12,... | collective-permute-start | bytes 3932168 | tf_op jit(solution)/shard_map/ppermute | solution.py:296
  482.9 30.5 %collective-permute-start.24 = (bf16[256,2560]{1,0:T(8,128)(2,1)}, bf16[256,2560]{1,0:T(8,128)(2,1)}, u32[]{:S(2)}, u32[]{:S(2)}) collective-permute-start(bf16[256,2560]{1,0:T(8,128)(2,1)} %pad_maximum_fusion.10), channel_id=1, source_target_pairs={{0,4},{2,6},{4,0},{6,2},{1,5},{3,7},{5,1},{7,3},{8,12},{10,14},{12... | collective-permute-start | bytes 3932168 | tf_op jit(solution)/shard_map/ppermute | solution.py:296
  510.1 365.3 %reduce-scatter.8.cloned.1.call-start = ((), (), s32[]{:S(2)}) async-start(), calls=%async_computation.9 | async-start | bytes 5324800 | tf_op jit(solution)/shard_map/reduce_scatter | solution.py:423
  533.7 45.6 %collective-permute-start.30 = (bf16[256,2560]{1,0:T(8,128)(2,1)}, bf16[256,2560]{1,0:T(8,128)(2,1)}, u32[]{:S(2)}, u32[]{:S(2)}) collective-permute-start(bf16[256,2560]{1,0:T(8,128)(2,1)} %get-tuple-element.111), channel_id=1, source_target_pairs={{0,4},{2,6},{4,0},{6,2},{1,5},{3,7},{5,1},{7,3},{8,12},{10,14},{12... | collective-permute-start | bytes 3932168 | tf_op jit(solution)/shard_map/ppermute | solution.py:296
  534.9 47.8 %collective-permute-start.28 = (bf16[256,2560]{1,0:T(8,128)(2,1)}, bf16[256,2560]{1,0:T(8,128)(2,1)}, u32[]{:S(2)}, u32[]{:S(2)}) collective-permute-start(bf16[256,2560]{1,0:T(8,128)(2,1)} %get-tuple-element.111), channel_id=1, source_target_pairs={{0,2},{2,0},{4,6},{6,4},{1,3},{3,1},{5,7},{7,5},{8,10},{10,8},{12,... | collective-permute-start | bytes 3932168 | tf_op jit(solution)/shard_map/ppermute | solution.py:296
  581.3 31.7 %collective-permute-start.31 = (bf16[128,2560]{1,0:T(8,128)(2,1)}, bf16[128,2560]{1,0:T(8,128)(2,1)S(1)}, u32[]{:S(2)}, u32[]{:S(2)}) collective-permute-start(bf16[128,2560]{1,0:T(8,128)(2,1)} %slice.507), channel_id=1, source_target_pairs={{0,2},{2,0},{4,6},{6,4},{1,3},{3,1},{5,7},{7,5},{8,10},{10,8},{12,... | collective-permute-start | bytes 1966088 | tf_op jit(solution)/shard_map/ppermute | solution.py:296
  584.7 28.3 %collective-permute-start.29 = (bf16[128,2560]{1,0:T(8,128)(2,1)}, bf16[128,2560]{1,0:T(8,128)(2,1)}, u32[]{:S(2)}, u32[]{:S(2)}) collective-permute-start(bf16[128,2560]{1,0:T(8,128)(2,1)} %slice.506), channel_id=1, source_target_pairs={{0,4},{2,6},{4,0},{6,2},{1,5},{3,7},{5,1},{7,3},{8,12},{10,14},{12... | collective-permute-start | bytes 1966088 | tf_op jit(solution)/shard_map/ppermute | solution.py:296
  633.5 54.6 %collective-permute-start.32 = (bf16[320,1024]{1,0:T(8,128)(2,1)S(1)}, bf16[320,1024]{1,0:T(8,128)(2,1)S(1)}, u32[]{:S(2)}, u32[]{:S(2)}) collective-permute-start(bf16[320,1024]{1,0:T(8,128)(2,1)S(1)} %get-tuple-element.144), channel_id=1, source_target_pairs={{0,8},{8,0},{16,24},{24,16},{1,9},{9,1},{17,25},{25,17},{2,10},{10... | collective-permute-start | bytes 1966088 | tf_op jit(solution)/shard_map/ppermute | solution.py:466
  642.3 129.3 %collective-permute-start.42 = (bf16[320,1024]{1,0:T(8,128)(2,1)}, bf16[320,1024]{1,0:T(8,128)(2,1)}, u32[]{:S(2)}, u32[]{:S(2)}) collective-permute-start(bf16[320,1024]{1,0:T(8,128)(2,1)} %get-tuple-element.143), channel_id=1, source_target_pairs={{0,24},{8,16},{16,8},{24,0},{1,25},{9,17},{17,9},{25,1},{2,26},{10... | collective-permute-start | bytes 1966088 | tf_op jit(solution)/shard_map/ppermute | solution.py:466
  688.3 18.8 %collective-permute-start.41 = (bf16[80,1792]{1,0:T(8,128)(2,1)S(1)}, bf16[80,1792]{1,0:T(8,128)(2,1)S(1)}, u32[]{:S(2)}, u32[]{:S(2)}) collective-permute-start(bf16[80,1792]{1,0:T(8,128)(2,1)S(1)} %get-tuple-element.175), channel_id=1, source_target_pairs={{0,3},{1,7},{2,2},{3,6},{4,1},{5,5},{6,0},{7,4},{8,11},{9,15},{10,... | collective-permute-start | bytes 860168 | tf_op jit(solution)/shard_map/ppermute | solution.py:448
  690.2 19.9 %collective-permute-start.40 = (bf16[80,1792]{1,0:T(8,128)(2,1)S(1)}, bf16[80,1792]{1,0:T(8,128)(2,1)S(1)}, u32[]{:S(2)}, u32[]{:S(2)}) collective-permute-start(bf16[80,1792]{1,0:T(8,128)(2,1)S(1)} %get-tuple-element.176), channel_id=1, source_target_pairs={{0,2},{1,6},{2,3},{3,7},{4,0},{5,4},{6,1},{7,5},{8,10},{9,14},{10,... | collective-permute-start | bytes 860168 | tf_op jit(solution)/shard_map/ppermute | solution.py:448
  690.3 20.4 %collective-permute-start.39 = (bf16[80,1792]{1,0:T(8,128)(2,1)S(1)}, bf16[80,1792]{1,0:T(8,128)(2,1)S(1)}, u32[]{:S(2)}, u32[]{:S(2)}) collective-permute-start(bf16[80,1792]{1,0:T(8,128)(2,1)S(1)} %get-tuple-element.177), channel_id=1, source_target_pairs={{0,1},{1,5},{2,0},{3,4},{4,3},{5,7},{6,2},{7,6},{8,9},{9,13},{10,8... | collective-permute-start | bytes 860168 | tf_op jit(solution)/shard_map/ppermute | solution.py:448
  693.3 17.3 %collective-permute-start.38 = (bf16[80,1792]{1,0:T(8,128)(2,1)S(1)}, bf16[80,1792]{1,0:T(8,128)(2,1)S(1)}, u32[]{:S(2)}, u32[]{:S(2)}) collective-permute-start(bf16[80,1792]{1,0:T(8,128)(2,1)S(1)} %get-tuple-element.174), channel_id=1, source_target_pairs={{0,0},{1,4},{2,1},{3,5},{4,2},{5,6},{6,3},{7,7},{8,8},{9,12},{10,9... | collective-permute-start | bytes 860168 | tf_op jit(solution)/shard_map/ppermute | solution.py:448
  707.0 31.7 %collective-permute-start.33 = (bf16[256,2560]{1,0:T(8,128)(2,1)S(1)}, bf16[256,2560]{1,0:T(8,128)(2,1)S(1)}, u32[]{:S(2)}, u32[]{:S(2)}) collective-permute-start(bf16[256,2560]{1,0:T(8,128)(2,1)S(1)} %copy-done.26), channel_id=1, source_target_pairs={{0,2},{2,0},{4,6},{6,4},{1,3},{3,1},{5,7},{7,5},{8,10},{10,8},{12,... | collective-permute-start | bytes 3932168 | tf_op jit(solution)/shard_map/ppermute | solution.py:296
  710.1 31.1 %collective-permute-start.34 = (bf16[256,2560]{1,0:T(8,128)(2,1)S(1)}, bf16[256,2560]{1,0:T(8,128)(2,1)S(1)}, u32[]{:S(2)}, u32[]{:S(2)}) collective-permute-start(bf16[256,2560]{1,0:T(8,128)(2,1)S(1)} %copy-done.25), channel_id=1, source_target_pairs={{0,4},{2,6},{4,0},{6,2},{1,5},{3,7},{5,1},{7,3},{8,12},{10,14},{12... | collective-permute-start | bytes 3932168 | tf_op jit(solution)/shard_map/ppermute | solution.py:296
  710.6 35.7 %collective-permute-start.37 = (bf16[4,320,640]{2,1,0:T(8,128)(2,1)}, bf16[4,320,640]{2,1,0:T(8,128)(2,1)}, u32[]{:S(2)}, u32[]{:S(2)}) collective-permute-start(bf16[4,320,640]{2,1,0:T(8,128)(2,1)} %dynamic-slice_bitcast_fusion.2), channel_id=1, source_target_pairs={{0,1},{1,0},{2,3},{3,2},{4,5},{5,4},{6,7},{7,6},{8,9},{9,8},{10,11... | collective-permute-start | bytes 4915208 | tf_op jit(solution)/shard_map/ppermute | solution.py:405
  710.6 38.0 %collective-permute-start.36 = (bf16[4,320,640]{2,1,0:T(8,128)(2,1)}, bf16[4,320,640]{2,1,0:T(8,128)(2,1)}, u32[]{:S(2)}, u32[]{:S(2)}) collective-permute-start(bf16[4,320,640]{2,1,0:T(8,128)(2,1)} %dynamic-slice_bitcast_fusion.3), channel_id=1, source_target_pairs={{0,1},{1,0},{2,3},{3,2},{4,5},{5,4},{6,7},{7,6},{8,9},{9,8},{10,11... | collective-permute-start | bytes 4915208 | tf_op jit(solution)/shard_map/ppermute | solution.py:405
  738.8 32.8 %collective-permute-start.35 = (bf16[320,1024]{1,0:T(8,128)(2,1)}, bf16[320,1024]{1,0:T(8,128)(2,1)}, u32[]{:S(2)}, u32[]{:S(2)}) collective-permute-start(bf16[320,1024]{1,0:T(8,128)(2,1)} %get-tuple-element.142), channel_id=1, source_target_pairs={{0,16},{8,24},{16,0},{24,8},{1,17},{9,25},{17,1},{25,9},{2,18},{10... | collective-permute-start | bytes 1966088 | tf_op jit(solution)/shard_map/ppermute | solution.py:466
  808.1 30.2 %collective-permute-start.45 = (bf16[256,2560]{1,0:T(8,128)(2,1)}, bf16[256,2560]{1,0:T(8,128)(2,1)}, u32[]{:S(2)}, u32[]{:S(2)}) collective-permute-start(bf16[256,2560]{1,0:T(8,128)(2,1)} %pad_maximum_fusion.14), channel_id=1, source_target_pairs={{0,2},{2,0},{4,6},{6,4},{1,3},{3,1},{5,7},{7,5},{8,10},{10,8},{12,... | collective-permute-start | bytes 3932168 | tf_op jit(solution)/shard_map/ppermute | solution.py:296
  810.6 29.7 %collective-permute-start.47 = (bf16[256,2560]{1,0:T(8,128)(2,1)}, bf16[256,2560]{1,0:T(8,128)(2,1)}, u32[]{:S(2)}, u32[]{:S(2)}) collective-permute-start(bf16[256,2560]{1,0:T(8,128)(2,1)} %pad_maximum_fusion.15), channel_id=1, source_target_pairs={{0,4},{2,6},{4,0},{6,2},{1,5},{3,7},{5,1},{7,3},{8,12},{10,14},{12... | collective-permute-start | bytes 3932168 | tf_op jit(solution)/shard_map/ppermute | solution.py:296
  843.3 18.8 %collective-permute-start.55 = (bf16[80,3584]{1,0:T(8,128)(2,1)S(1)}, bf16[80,3584]{1,0:T(8,128)(2,1)S(1)}, u32[]{:S(2)}, u32[]{:S(2)}) collective-permute-start(bf16[80,3584]{1,0:T(8,128)(2,1)S(1)} %get-tuple-element.158), channel_id=1, source_target_pairs={{0,3},{1,7},{2,2},{3,6},{4,1},{5,5},{6,0},{7,4},{8,11},{9,15},{10,... | collective-permute-start | bytes 1720328 | tf_op jit(solution)/shard_map/ppermute | solution.py:448
  845.3 24.3 %collective-permute-start.54 = (bf16[80,3584]{1,0:T(8,128)(2,1)S(1)}, bf16[80,3584]{1,0:T(8,128)(2,1)S(1)}, u32[]{:S(2)}, u32[]{:S(2)}) collective-permute-start(bf16[80,3584]{1,0:T(8,128)(2,1)S(1)} %get-tuple-element.159), channel_id=1, source_target_pairs={{0,2},{1,6},{2,3},{3,7},{4,0},{5,4},{6,1},{7,5},{8,10},{9,14},{10,... | collective-permute-start | bytes 1720328 | tf_op jit(solution)/shard_map/ppermute | solution.py:448
  845.4 24.3 %collective-permute-start.53 = (bf16[80,3584]{1,0:T(8,128)(2,1)S(1)}, bf16[80,3584]{1,0:T(8,128)(2,1)S(1)}, u32[]{:S(2)}, u32[]{:S(2)}) collective-permute-start(bf16[80,3584]{1,0:T(8,128)(2,1)S(1)} %get-tuple-element.160), channel_id=1, source_target_pairs={{0,1},{1,5},{2,0},{3,4},{4,3},{5,7},{6,2},{7,6},{8,9},{9,13},{10,8... | collective-permute-start | bytes 1720328 | tf_op jit(solution)/shard_map/ppermute | solution.py:448
  848.4 21.3 %collective-permute-start.52 = (bf16[80,3584]{1,0:T(8,128)(2,1)S(1)}, bf16[80,3584]{1,0:T(8,128)(2,1)S(1)}, u32[]{:S(2)}, u32[]{:S(2)}) collective-permute-start(bf16[80,3584]{1,0:T(8,128)(2,1)S(1)} %get-tuple-element.157), channel_id=1, source_target_pairs={{0,0},{1,4},{2,1},{3,5},{4,2},{5,6},{6,3},{7,7},{8,8},{9,12},{10,9... | collective-permute-start | bytes 1720328 | tf_op jit(solution)/shard_map/ppermute | solution.py:448
  (68 other events, 1413.2 us)
Sparse Core Ops, SparseCore 0:
  14.0 85.8 all-gather.4
  112.5 53.2 all-gather.6
  168.0 162.7 all-gather.8
  332.4 86.7 all-gather.10
  421.3 95.4 reduce-scatter.3
  519.1 183.3 reduce-scatter.5
  788.9 77.9 reduce-scatter.7
